TPU v7x, 512 devices: a whole 4x4x16 slice. The times are simulated.
512 devices in a mesh: row: 32 (over z, core), col: 16 (over y, x).
Axes of the slice: x: 4, y: 4, z: 16, core: 2. Of those that a mesh axis runs over, the one named last changes fastest.
Arguments:
- train_points: float32 [64, 32768], P(None, ('row', 'col')), may hold values from -6 to 6
- cand_points: float32 [64, 32768], P(None, ('row', 'col')), may hold values from -6 to 6
- inv_length: float32 [64], replicated, may hold values from 0.04 to 0.7
- noise: float32 [32768], P(('row', 'col')), may hold values from 0.5 to 4
- targets: float32 [16, 32768], P(None, ('row', 'col')), may hold values from -15 to 15
Outputs:
- solution: float32 [16, 32768], P(None, ('row', 'col'))
- post_mean: float32 [16, 32768], P(None, ('row', 'col'))
All inputs are finite; a program needn't handle non-finite values.
Results may differ from a plain program's by a relative error of at most 0.0047.
Values may be sent and summed in bfloat16 or wider, within the bound.
No kernel may reach another device: no remote copies, remote signals or barrier semaphores. Data moves between devices by JAX's collectives and lax.ppermute only.
A program may use at most 64 MiB of HBM per device.

v0:
```python
import math

import jax
import jax.numpy as jnp
from jax import lax
from jax.sharding import PartitionSpec as P

ITERS = 2


root_five = math.sqrt(5.0)


def matern(left, left_norm, right, right_norm):
    inner = lax.dot_general(
        left, right, (((0,), (0,)), ((), ())), preferred_element_type=jnp.float32
    )
    dist_sq = jnp.maximum(left_norm[:, None] + right_norm[None, :] - 2.0 * inner, 0.0)
    radius = jnp.sqrt(dist_sq)
    return (1.0 + root_five * radius + 5.0 / 3.0 * dist_sq) * jnp.exp(-root_five * radius)


def tile_rows(amount):
    best = 1
    for candidate in range(1, 513):
        if amount % candidate == 0:
            best = candidate
    return best


def accumulate(carried, vector_piece, piece_points, piece_norms, other, other_norms):
    amount = vector_piece.shape[1]
    block = tile_rows(amount)

    def advance(block_index, running):
        offset = block_index * block
        sub_points = lax.dynamic_slice_in_dim(piece_points, offset, block, 1)
        sub_norms = lax.dynamic_slice_in_dim(piece_norms, offset, block, 0)
        sub_vector = lax.dynamic_slice_in_dim(vector_piece, offset, block, 1)
        kernel_tile = matern(sub_points, sub_norms, other, other_norms)
        return running + jnp.dot(
            sub_vector,
            kernel_tile,
            precision=lax.Precision.HIGHEST,
            preferred_element_type=jnp.float32,
        )

    return lax.fori_loop(0, amount // block, advance, carried)


def per_device(train_points, cand_points, inv_length, noise, targets):
    scaled_train = (train_points * inv_length[:, None]).astype(jnp.bfloat16)
    scaled_cand = (cand_points * inv_length[:, None]).astype(jnp.bfloat16)
    row_train, row_cand = (
        lax.all_gather(scaled_train, "col", axis=1, tiled=True),
        lax.all_gather(scaled_cand, "col", axis=1, tiled=True),
    )
    col_train = lax.all_gather(scaled_train, "row", axis=1, tiled=True)
    row_norms = jnp.sum(jnp.square(row_train.astype(jnp.float32)), axis=0)
    cand_norms = jnp.sum(jnp.square(row_cand.astype(jnp.float32)), axis=0)
    col_norms = jnp.sum(jnp.square(col_train.astype(jnp.float32)), axis=0)
    outputs = targets.shape[0]

    def from_columns(other, other_norms, carried, vector_piece):
        return accumulate(carried, vector_piece, col_train, col_norms, other, other_norms)

    def squares(residual):
        return lax.psum(jnp.sum(residual * residual, axis=1), ("row", "col"))

    solution = jnp.zeros_like(targets)
    residual = targets
    direction = targets
    norm_now = squares(residual)
    for iteration in range(ITERS):
        start_total = jnp.zeros((outputs, row_train.shape[1]), jnp.float32)
        partial_image = from_columns(
            row_train, row_norms, start_total, lax.all_gather(direction, "row", axis=1, tiled=True)
        )
        own_image = lax.psum_scatter(partial_image, "col", scatter_dimension=1, tiled=True)
        image = own_image + noise[None, :] * direction
        alpha = norm_now / lax.psum(jnp.sum(direction * image, axis=1), ("row", "col"))
        solution = solution + alpha[:, None] * direction
        residual = residual - alpha[:, None] * image
        norm_next = squares(residual)
        direction = residual + (norm_next / norm_now)[:, None] * direction
        norm_now = norm_next
    mean_start = jnp.zeros((outputs, row_cand.shape[1]), jnp.float32)
    partial_mean = from_columns(
        row_cand, cand_norms, mean_start, lax.all_gather(solution, "row", axis=1, tiled=True)
    )
    post_mean = lax.psum_scatter(partial_mean, "col", scatter_dimension=1, tiled=True)
    return (solution, post_mean)


def solution(mesh):
    placed = (
        P(None, ("row", "col")),
        P(None, ("row", "col")),
        P(),
        P(("row", "col")),
        P(None, ("row", "col")),
    )
    return jax.shard_map(
        per_device,
        mesh=mesh,
        in_specs=placed,
        out_specs=(P(None, ("row", "col")), P(None, ("row", "col"))),
        check_vma=False,
    )
```

profile of v0, /device:TPU:1, one launch (start us, length us, event | category | flops | bytes accessed | tf_op | source)
XLA Modules:
  0.0 763.1 jit_solution(8951887657408759057)
XLA Ops:
  7.2 0.8 copy.22
  8.1 0.8 copy.29
  8.9 0.7 multiply_convert_fusion
  9.6 39.0 %all_gather.19 = bf16[64,2048]{0,1:T(8,128)(2,1)S(1)} all-gather(bf16[64,64]{0,1:T(8,128)(2,1)S(1)} %get-tuple-element.538), channel_id=1, replica_groups=mesh['row'=32,'col'=16] {'row'}, dimensions={1}, use_global_device_ids=true | all-gather | bytes 270336 | tf_op jit(solution)/shard_map/all_gather | solution.py:58
  49.1 18.9 %all_gather.20 = bf16[64,1024]{0,1:T(8,128)(2,1)S(1)} all-gather(bf16[64,64]{0,1:T(8,128)(2,1)S(1)} %get-tuple-element.538), channel_id=1, replica_groups=mesh['row'=32,'col'=16] {'col'}, dimensions={1}, use_global_device_ids=true | all-gather | bytes 139264 | tf_op jit(solution)/shard_map/all_gather | solution.py:55
  68.3 32.8 %all-gather = f32[32,64,16]{1,2,0:T(8,128)S(1)} all-gather(f32[1,64,16]{1,2,0:T(8,128)S(1)} %bitcast.37), channel_id=1, replica_groups=mesh['row'=32,'col'=16] {'row'}, dimensions={0}, use_global_device_ids=true | all-gather | bytes 135168 | tf_op jit(solution)/shard_map/all_gather | solution.py:77
  101.3 11.9 %while.42 = (s32[]{:T(128)}, f32[16,1024]{1,0:T(8,128)S(1)}, f32[16,2048]{1,0:T(8,128)S(1)}, f32[2048]{0:T(1024)S(1)}, f32[1024]{0:T(1024)S(1)}, /*index=5*/bf16...) while((s32[]{:T(128)}, f32[16,1024]{1,0:T(8,128)S(1)}, ...), condition=%wide.region_5.0_spmd.clone, body=%wide.region_4.0_spmd.clone.sunk | while | flops 173047808 | bytes 4565169 | solution.py:48
  101.3 0.5 fusion.131
  101.9 2.4 fusion.132
  104.3 0.5 fusion.131
  104.8 2.4 fusion.132
  107.3 0.5 fusion.131
  107.8 2.4 fusion.132
  110.2 0.5 fusion.131
  110.8 2.4 fusion.132
  113.2 1.0 copy.32
  114.3 81.5 %reduce-scatter.10.cloned.1.call-done = f32[64,16]{1,0:T(8,128)} async-done(((f32[1024,16]{1,0:T(8,128)}), f32[64,16]{1,0:T(8,128)}) %reduce-scatter.10.cloned.1.call-update) | async-done | bytes 4112
  195.8 0.8 copy.33
  196.8 105.4 %all-reduce = (f32[16]{0:T(128)S(1)}, f32[16]{0:T(128)S(1)}) all-reduce(f32[16]{0:T(128)S(1)} %get-tuple-element.492, f32[16]{0:T(128)S(1)} %get-tuple-element.491), channel_id=1, replica_groups=mesh['row'=32,'col'=16] {'row','col'}, use_global_device_ids=true, to_apply=%region_1.0 | all-reduce | flops 32 | bytes 256 | tf_op jit(solution)/shard_map/psum | solution.py:68
  302.3 99.4 %psum.30 = f32[16]{0:T(128)S(1)} all-reduce(f32[16]{0:T(128)S(1)} %multiply_reduce_fusion.4), channel_id=1, replica_groups=mesh['row'=32,'col'=16] {'row','col'}, use_global_device_ids=true, to_apply=%region_10.0 | all-reduce | flops 16 | bytes 128 | tf_op jit(solution)/shard_map/psum | solution.py:68
  401.8 29.1 %all-gather.1 = f32[32,64,16]{1,2,0:T(8,128)S(1)} all-gather(f32[1,64,16]{1,2,0:T(8,128)S(1)} %fusion.105), channel_id=1, replica_groups=mesh['row'=32,'col'=16] {'row'}, dimensions={0}, use_global_device_ids=true | all-gather | bytes 135168 | tf_op jit(solution)/shard_map/all_gather | solution.py:77
  431.2 11.9 %while.43 = (s32[]{:T(128)}, f32[16,1024]{1,0:T(8,128)S(1)}, f32[16,2048]{1,0:T(8,128)S(1)}, f32[2048]{0:T(1024)S(1)}, f32[1024]{0:T(1024)S(1)}, /*index=5*/bf16...) while((s32[]{:T(128)}, f32[16,1024]{1,0:T(8,128)S(1)}, ...), condition=%wide.region_12.0_spmd.clone, body=%wide.region_11.0_spmd.clone.sunk | while | flops 173047808 | bytes 4565169 | solution.py:48
  431.2 0.5 fusion.137
  431.7 2.4 fusion.138
  434.1 0.5 fusion.137
  434.7 2.4 fusion.138
  437.1 0.5 fusion.137
  437.7 2.4 fusion.138
  440.1 0.5 fusion.137
  440.6 2.4 fusion.138
  443.1 1.0 copy.34
  444.2 17.2 %all_gather.23 = bf16[64,1024]{0,1:T(8,128)(2,1)S(1)} all-gather(bf16[64,64]{0,1:T(8,128)(2,1)S(1)} %get-tuple-element.537), channel_id=1, replica_groups=mesh['row'=32,'col'=16] {'col'}, dimensions={1}, use_global_device_ids=true | all-gather | bytes 139264 | tf_op jit(solution)/shard_map/all_gather | solution.py:56
  461.7 63.0 %reduce-scatter.12.cloned.1.call-done = f32[64,16]{1,0:T(8,128)} async-done(((f32[1024,16]{1,0:T(8,128)}), f32[64,16]{1,0:T(8,128)}) %reduce-scatter.12.cloned.1.call-update) | async-done | bytes 4112
  524.7 0.8 copy.35
  525.7 105.6 %psum.31 = f32[16]{0:T(128)S(1)} all-reduce(f32[16]{0:T(128)S(1)} %multiply_reduce_fusion.3), channel_id=1, replica_groups=mesh['row'=32,'col'=16] {'row','col'}, use_global_device_ids=true, to_apply=%region_15.0 | all-reduce | flops 16 | bytes 128 | tf_op jit(solution)/shard_map/psum | solution.py:81
  631.4 29.8 %all-gather.2 = f32[32,64,16]{1,2,0:T(8,128)S(1)} all-gather(f32[1,64,16]{1,2,0:T(8,128)S(1)} %bitcast.44), channel_id=1, replica_groups=mesh['row'=32,'col'=16] {'row'}, dimensions={0}, use_global_device_ids=true | all-gather | bytes 135168 | tf_op jit(solution)/shard_map/all_gather | solution.py:89
  661.4 11.9 %while.44 = (s32[]{:T(128)}, f32[16,1024]{1,0:T(8,128)S(1)}, f32[16,2048]{1,0:T(8,128)S(1)}, f32[2048]{0:T(1024)S(1)}, f32[1024]{0:T(1024)S(1)}, /*index=5*/bf16...) while((s32[]{:T(128)}, f32[16,1024]{1,0:T(8,128)S(1)}, ...), condition=%wide.region_18.0_spmd.clone, body=%wide.region_17.0_spmd.clone.sunk | while | flops 173047808 | bytes 4565169 | solution.py:48
  661.4 0.5 fusion.143
  661.9 2.4 fusion.144
  664.3 0.5 fusion.143
  664.9 2.4 fusion.144
  667.3 0.5 fusion.143
  667.9 2.4 fusion.144
  670.3 0.5 fusion.143
  670.8 2.4 fusion.144
  673.3 1.0 copy.36
  674.3 80.9 %reduce-scatter.14.cloned.1.call-done = f32[64,16]{1,0:T(8,128)} async-done(((f32[1024,16]{1,0:T(8,128)}), f32[64,16]{1,0:T(8,128)}) %reduce-scatter.14.cloned.1.call-update) | async-done | bytes 4112
  755.2 1.4 copy.37
  (47 shorter events, 3.6 us)
Async XLA Ops:
  7.2 61.1 %copy-start = (f32[16,64]{1,0:T(8,128)S(1)}, f32[16,64]{1,0:T(8,128)}, u32[]{:S(2)}) copy-start(f32[16,64]{1,0:T(8,128)} %param.15) | copy-start | bytes 12292
  7.2 188.7 %reduce-scatter.10.cloned.1.call-start = ((), (), s32[]{:S(2)}) async-start(), calls=%async_computation.3 | async-start | bytes 557056
  101.3 95.4 %copy-start.2 = (f32[64]{0:T(128)S(1)}, f32[64]{0:T(128)}, u32[]{:S(2)}) copy-start(f32[64]{0:T(128)} %param.14) | copy-start | bytes 772
  114.3 410.4 %reduce-scatter.12.cloned.1.call-start = ((), (), s32[]{:S(2)}) async-start(), calls=%async_computation.4 | async-start | bytes 557056
  444.1 311.1 %reduce-scatter.14.cloned.1.call-start = ((), (), s32[]{:S(2)}) async-start(), calls=%async_computation.5 | async-start | bytes 557056
  631.4 30.0 %copy-start.1 = (f32[16,64]{1,0:T(8,128)}, f32[16,64]{1,0:T(8,128)S(1)}, u32[]{:S(2)}) copy-start(f32[16,64]{1,0:T(8,128)S(1)} %multiply_add_fusion) | copy-start | bytes 12292
Sparse Core Ops, SparseCore 0:
  114.4 81.4 reduce-scatter.9
  444.2 80.4 reduce-scatter.11
  674.4 80.7 reduce-scatter.13
where the time goes:
time: 764 us; the launch traced here: 763 us
  blocking collectives  477 us (62%)
  waiting for transfers between devices  225 us (29%)
  matrix products  34.7 us (5%)
  between operations  13.9 us (2%)
  local copies, waits for them, and re-layouts  9.76 us (1%)
    unnamed x6, waiting for transfers between devices  225 us
    psum x2, blocking collectives, squares(): return lax.psum(jnp.sum(residual * residual, axis=1), ('row', 'col'))  205 us
    psum x1, blocking collectives, per_device(): lax.psum(jnp.sum(direction * image, axis=1), ('row', 'col'))  106 us
    all_gather x2, blocking collectives, per_device(): lax.all_gather(direction, 'row', axis=1, tiled=True)  61.9 us
    all_gather x1, blocking collectives, per_device(): col_train = lax.all_gather(scaled_train, 'row', axis=1, tiled=True)  39 us
    all_gather x1, blocking collectives, per_device(): lax.all_gather(solution, 'row', axis=1, tiled=True)  29.8 us
    dot_general x12, matrix products, advance(): jnp.dot(sub_vector, kernel_tile, precision=lax.Precision.HIGHEST, preferr...  29.1 us
    all_gather x1, blocking collectives, per_device(): lax.all_gather(scaled_train, 'col', axis=1, tiled=True)  18.9 us
  transfers between devices with their start and end apart: 3, of which 3 were waited for; matrix products, arithmetic and copies ran while one was open for 0% of the time, Pallas kernels for 0%

commit v1 on v0

v1 whole, which is shorter than its diff:
```python
import functools
import math

import jax
import jax.numpy as jnp
from jax import lax
from jax.experimental import pallas as pl
from jax.experimental.pallas import tpu as pltpu
from jax.sharding import Mesh, PartitionSpec as P

F32 = jnp.float32
BF16 = jnp.bfloat16

D = 64
S = 64
RHS = 16
NQ = 16
NZ = 16
ROWS = NQ * S
COLS = 2 * NZ * S
LOG2E = math.log2(math.e)
PARAMS = pltpu.CompilerParams(vmem_limit_bytes=24 * 1024 * 1024)


def halves(value):
    high = value.astype(BF16)
    return high, (value - high.astype(F32)).astype(BF16)


def thirds(value):
    high = value.astype(BF16).astype(F32)
    rest = value - high
    middle = rest.astype(BF16).astype(F32)
    low = (rest - middle).astype(BF16).astype(F32)
    return high, middle, low


def rows_of(width, pieces):
    index = lax.broadcasted_iota(jnp.int32, (16, width), 0)
    total = jnp.zeros((16, width), F32)
    for i, piece in enumerate(pieces):
        total = jnp.where(index == i, piece, total)
    return total


def column(row, start):
    lane = lax.broadcasted_iota(jnp.int32, (RHS, 128), 1)
    index = lax.broadcasted_iota(jnp.int32, (RHS, 128), 0)
    return jnp.sum(jnp.where(lane == index + start, row, 0.0), axis=1, keepdims=True)


def prepare(train_ref, cand_ref, inv_ref, target_ref, y_ref, z_ref):
    eye = lax.broadcasted_iota(jnp.int32, (D, D), 0) == lax.broadcasted_iota(
        jnp.int32, (D, D), 1
    )
    inv = jnp.sum(jnp.where(eye, inv_ref[...], 0.0), axis=1, keepdims=True)
    train = train_ref[...] * inv
    cand = cand_ref[...] * inv
    b_high, b_low = halves(target_ref[...])
    b = jnp.concatenate([b_high, b_low], axis=1)
    both = jnp.concatenate([train.astype(BF16), cand.astype(BF16)], axis=1)
    folded = jnp.concatenate([train[:32].astype(BF16), train[32:].astype(BF16)], axis=1)
    for i in range(NQ):
        y_ref[i, 0:64, :] = both
        y_ref[i, 64:80, :] = b
        z_ref[i, 0:32, :] = folded
        z_ref[i, 32:48, :] = b


def row_side(y_ref, j, first):
    points = jnp.concatenate(
        [y_ref[2 * j, 0:64, first : first + 64], y_ref[2 * j + 1, 0:64, first : first + 64]],
        axis=1,
    ).astype(F32)
    norm = jnp.sum(points * points, axis=0, keepdims=True)
    extra = rows_of(128, [*thirds(norm), 1.0, 1.0, 1.0])
    return jnp.concatenate(
        [-2.0 * points, extra, jnp.zeros((48, 128), F32)], axis=0
    ).astype(BF16)


def col_side(z_ref, z):
    low = z_ref[0, z, 0:32, :]
    high = z_ref[1, z, 0:32, :]
    points = jnp.concatenate(
        [
            jnp.concatenate([low[:, :64], high[:, :64]], axis=1),
            jnp.concatenate([low[:, 64:], high[:, 64:]], axis=1),
        ],
        axis=0,
    ).astype(F32)
    norm = jnp.sum(points * points, axis=0, keepdims=True)
    extra = rows_of(128, [1.0, 1.0, 1.0, *thirds(norm)])
    full = jnp.concatenate([points, extra, jnp.zeros((48, 128), F32)], axis=0)
    return full.T.astype(BF16)


def matern_of(inner):
    five_dist = jnp.maximum(inner, 1e-30) * 5.0
    scaled = five_dist * lax.rsqrt(five_dist)
    return (1.0 + scaled + five_dist * (1.0 / 3.0)) * jnp.exp2(scaled * (-LOG2E))


def tile(points, b, row_aug, kern_ref, acc_ref, z):
    offset = pl.multiple_of(z * 128, 128)
    for part in range(ROWS // 256):
        span = slice(part * 256, part * 256 + 256)
        inner = jnp.dot(points, row_aug[:, span], preferred_element_type=F32)
        kern = matern_of(inner).astype(BF16)
        kern_ref[pl.ds(offset, 128), span] = kern
        acc_ref[:, span] += jnp.dot(b, kern, preferred_element_type=F32)


def own_block(q):
    return pl.ds(pl.multiple_of((q // 2) * 128, 128), 128)


def own_mask(q):
    lane = lax.broadcasted_iota(jnp.int32, (RHS, 128), 1)
    return (lane // 64) == (q % 2)


def position():
    return lax.axis_index("y") * 4 + lax.axis_index("x")


def first_apply(
    y_ref, z_ref, target_ref, noise_ref, kern_ref, col_ref, b_ref, out_ref, acc_ref, row_ref
):
    q = position()
    for j in range(NQ // 2):
        row_ref[:, j * 128 : j * 128 + 128] = row_side(y_ref, j, 0)
    acc_ref[...] = jnp.zeros_like(acc_ref)

    def step(z, _):
        points = col_side(z_ref, z)
        offset = pl.multiple_of(z * 128, 128)
        col_ref[pl.ds(offset, 128), :] = points
        low, high = z_ref[0, z, 32:48, :], z_ref[1, z, 32:48, :]
        b = jnp.concatenate(
            [
                jnp.concatenate([low[:, :64], high[:, :64]], axis=1),
                jnp.concatenate([low[:, 64:], high[:, 64:]], axis=1),
            ],
            axis=0,
        )
        b_ref[z] = b
        tile(points, b, row_ref, kern_ref, acc_ref, z)
        return 0

    lax.fori_loop(0, NZ, step, 0)
    own = target_ref[...] * noise_ref[...]
    twice = jnp.concatenate([own, own], axis=1)
    acc_ref[0:16, own_block(q)] += jnp.where(own_mask(q), twice, 0.0)
    image = (acc_ref[0:16, :] + acc_ref[16:32, :]).astype(BF16)
    for i in range(NQ):
        out_ref[i] = image


def cand_apply(y_ref, col_ref, b_ref, kern_ref, out_ref, acc_ref, row_ref):
    for j in range(NQ // 2):
        row_ref[:, j * 128 : j * 128 + 128] = row_side(y_ref, j, 64)
    acc_ref[...] = jnp.zeros_like(acc_ref)

    def step(z, _):
        offset = pl.multiple_of(z * 128, 128)
        tile(col_ref[pl.ds(offset, 128), :], b_ref[z], row_ref, kern_ref, acc_ref, z)
        return 0

    lax.fori_loop(0, NZ, step, 0)
    out_ref[...] = acc_ref[0:16, :] + acc_ref[16:32, :]


def merge_image(part_ref, y_ref, out_ref, w_ref, br_ref):
    q = position()
    total = part_ref[0].astype(F32)
    for i in range(1, NQ):
        total = total + part_ref[i].astype(F32)
    w_ref[...] = total
    for j in range(NQ // 2):
        even, odd = y_ref[2 * j, 64:80, :].astype(F32), y_ref[2 * j + 1, 64:80, :].astype(F32)
        br_ref[:, j * 128 : j * 128 + 128] = jnp.concatenate(
            [even[:, :64] + even[:, 64:], odd[:, :64] + odd[:, 64:]], axis=1
        )
    b = br_ref[...]
    bw = jnp.sum(b * total, axis=1, keepdims=True)
    bb = jnp.sum(b * b, axis=1, keepdims=True)
    block = w_ref[:, own_block(q)]
    own = jnp.where(q % 2 == 0, block[:, :64], block[:, 64:])
    lane = lax.broadcasted_iota(jnp.int32, (RHS, 64), 1)
    scalars = jnp.zeros((RHS, 64), F32)
    for i, piece in enumerate([*thirds(bw), *thirds(bb)]):
        scalars = jnp.where(lane == i, piece, scalars)
    message = jnp.concatenate([own, scalars], axis=1).astype(BF16)
    for i in range(NZ):
        out_ref[i] = message


def second_apply(
    s_ref, b_ref, w_ref, br_ref, kern_ref, cand_ref, mean_ref, target_ref, noise_ref,
    out_ref, own_ref, r_ref,
):
    q = position()
    sums = s_ref[0, 0, :, 64:128].astype(F32)
    for c in range(2):
        for z in range(NZ):
            if c or z:
                sums = sums + s_ref[c, z, :, 64:128].astype(F32)
    lane = lax.broadcasted_iota(jnp.int32, (RHS, 64), 1)
    bw = jnp.sum(jnp.where(lane < 3, sums, 0.0), axis=1, keepdims=True)
    bb = jnp.sum(jnp.where((lane >= 3) & (lane < 6), sums, 0.0), axis=1, keepdims=True)
    alpha = bb / bw
    for z in range(NZ):
        w = jnp.concatenate([s_ref[0, z, :, 0:64], s_ref[1, z, :, 0:64]], axis=1).astype(F32)
        b = b_ref[z, 0:16, :].astype(F32) + b_ref[z, 16:32, :].astype(F32)
        high, low = halves(b - alpha * w)
        r_ref[:, z * 128 : z * 128 + 128] = jnp.concatenate([high, low], axis=0)
    r = r_ref[...]
    applied = jnp.dot(r, kern_ref[...], preferred_element_type=F32)
    applied = applied[0:16] + applied[16:32]
    mean = jnp.dot(r, cand_ref[...], preferred_element_type=F32)
    mean = mean[0:16] + mean[16:32]
    mean0 = mean_ref[...]
    for i in range(NQ):
        span = slice(i * 64, i * 64 + 64)
        out_ref[i, 0:16, :] = jnp.concatenate([mean0[:, span], mean[:, span]], axis=1)
    r_row = br_ref[...] - alpha * w_ref[...]
    block = w_ref[:, own_block(q)]
    own_w = jnp.where(q % 2 == 0, block[:, :64], block[:, 64:])
    target = target_ref[...]
    own_r = target - alpha * own_w
    s = jnp.sum(r_row * applied, axis=1, keepdims=True) + jnp.sum(
        noise_ref[...] * own_r * own_r, axis=1, keepdims=True
    )
    t = jnp.sum(own_r * own_w, axis=1, keepdims=True)
    rr = jnp.sum(own_r * own_r, axis=1, keepdims=True)
    wide = lax.broadcasted_iota(jnp.int32, (RHS, 128), 1)
    index = lax.broadcasted_iota(jnp.int32, (RHS, 128), 0)
    spread = (
        jnp.where(wide == index, s, 0.0)
        + jnp.where(wide == index + 16, t, 0.0)
        + jnp.where(wide == index + 32, rr, 0.0)
    )
    spread = jnp.sum(spread, axis=0, keepdims=True)
    eight = lax.broadcasted_iota(jnp.int32, (8, 128), 0)
    spread = jnp.where(eight == 0, spread, 0.0)
    for i in range(NQ):
        out_ref[i, 16:24, :] = spread
    side = jnp.where(lane == 0, bb, jnp.where(lane == 1, bw, 0.0))
    own_ref[...] = jnp.concatenate([own_r, side], axis=1)


def merge_mean(part_ref, mean_ref, out_ref):
    total = part_ref[0]
    for i in range(1, NQ):
        total = total + part_ref[i]
    mean_ref[...] = total[0:16]
    for i in range(NZ):
        out_ref[i] = total[16:17]


def finish(s_ref, own_ref, mean_ref, target_ref, solution_ref, post_ref):
    total = s_ref[0, 0]
    for c in range(2):
        for z in range(NZ):
            if c or z:
                total = total + s_ref[c, z]
    s, t, rr = column(total, 0), column(total, 16), column(total, 32)
    own_r = own_ref[:, 0:64]
    bb, bw = own_ref[:, 64:65], own_ref[:, 65:66]
    alpha0 = bb / bw
    beta = rr / bb
    alpha1 = rr / (s + 2.0 * beta * t + beta * beta * bw)
    target = target_ref[...]
    solution_ref[...] = alpha0 * target + alpha1 * (own_r + beta * target)
    mean = mean_ref[...]
    post_ref[...] = (alpha0 + alpha1 * beta) * mean[:, :64] + alpha1 * mean[:, 64:]


def shape(*dims, dtype=F32):
    return jax.ShapeDtypeStruct(dims, dtype)


def per_device(train_points, cand_points, inv_length, noise, targets):
    noise = noise.reshape(1, S)
    call = functools.partial(pl.pallas_call, compiler_params=PARAMS)
    y_out, z_out = call(
        prepare,
        out_shape=(shape(NQ, 80, 128, dtype=BF16), shape(NZ, 48, 128, dtype=BF16)),
    )(train_points, cand_points, inv_length.reshape(1, D), targets)
    y_in = lax.all_to_all(y_out, ("y", "x"), 0, 0)
    z_in = lax.all_gather(lax.all_to_all(z_out, "z", 0, 0), "c", axis=0)
    cost = pl.CostEstimate(
        flops=2 * ROWS * COLS * 160, bytes_accessed=2 * ROWS * COLS, transcendentals=2 * ROWS * COLS
    )
    kern, col, b_col, image_out = call(
        first_apply,
        out_shape=(
            shape(COLS, ROWS, dtype=BF16),
            shape(COLS, 128, dtype=BF16),
            shape(NZ, 32, 128, dtype=BF16),
            shape(NQ, RHS, ROWS, dtype=BF16),
        ),
        scratch_shapes=[pltpu.VMEM((32, ROWS), F32), pltpu.VMEM((128, ROWS), BF16)],
        cost_estimate=cost,
    )(y_in, z_in, targets, noise)
    image_in = lax.all_to_all(image_out, ("y", "x"), 0, 0)
    kern_cand, mean0 = call(
        cand_apply,
        out_shape=(shape(COLS, ROWS, dtype=BF16), shape(RHS, ROWS)),
        scratch_shapes=[pltpu.VMEM((32, ROWS), F32), pltpu.VMEM((128, ROWS), BF16)],
        cost_estimate=cost,
    )(y_in, col, b_col)
    w_out, w_row, b_row = call(
        merge_image,
        out_shape=(shape(NZ, RHS, 128, dtype=BF16), shape(RHS, ROWS), shape(RHS, ROWS)),
    )(image_in, y_in)
    w_in = lax.all_gather(lax.all_to_all(w_out, "z", 0, 0), "c", axis=0)
    mean_out, own = call(
        second_apply,
        out_shape=(shape(NQ, 24, 128), shape(RHS, 128)),
        scratch_shapes=[pltpu.VMEM((32, COLS), BF16)],
    )(w_in, b_col, w_row, b_row, kern, kern_cand, mean0, targets, noise)
    mean_in = lax.all_to_all(mean_out, ("y", "x"), 0, 0)
    mean, scalar_out = call(
        merge_mean, out_shape=(shape(RHS, 128), shape(NZ, 1, 128))
    )(mean_in)
    scalar_in = lax.all_gather(lax.all_to_all(scalar_out, "z", 0, 0), "c", axis=0)
    return call(finish, out_shape=(shape(RHS, S), shape(RHS, S)))(
        scalar_in, own, mean, targets
    )


def solution(mesh):
    fine = Mesh(mesh.devices.reshape(16, 2, 4, 4), ("z", "c", "y", "x"))
    every = ("z", "c", "y", "x")
    wide = P(None, every)
    return jax.shard_map(
        per_device,
        mesh=fine,
        in_specs=(wide, wide, P(), P(every), wide),
        out_specs=(wide, wide),
        check_vma=False,
    )
```

time: 764 us -> 156 us (0.20)
  blocking collectives: 477 us -> 91.2 us
  waiting for transfers between devices: 225 us -> 1.06 us
  Pallas kernels: 0 us -> 35 us
  matrix products: 34.7 us -> 0 us
  starting transfers between devices: 0.12 us -> 14.5 us
  between operations: 13.9 us -> 0.71 us
    psum x3 -> x0, blocking collectives: 310 us -> none  [the longest x2 205 us: squares(): return lax.psum(jnp.sum(residual * residual, axis=1), ('row', 'col'))]
    unnamed x6 -> x0, waiting for transfers between devices: 225 us -> none
    all_gather x6 -> x3, blocking collectives: 167 us -> 15.9 us  [the longest x1 6.83 us: per_device(): z_in = lax.all_gather(lax.all_to_all(z_out, 'z', 0, 0), 'c', axis=0)]
    all_to_all x0 -> x4, blocking collectives: none -> 75.4 us  [the longest x1 28 us: per_device(): z_in = lax.all_gather(lax.all_to_all(z_out, 'z', 0, 0), 'c', axis=0)]
    pallas_call x0 -> x7, Pallas kernels: none -> 35 us  [the longest x1 16.3 us: per_device(): call(first_apply, out_shape=(shape(COLS, ROWS, dtype=BF16), shape(COLS, 1...]
    dot_general x24 -> x0, matrix products: 34.7 us -> none  [the longest x12 29.1 us: advance(): jnp.dot(sub_vector, kernel_tile, precision=lax.Precision.HIGHEST, preferr...]
    all_to_all x0 -> x2, starting transfers between devices: none -> 14.5 us  [the longest x1 7.78 us: per_device(): w_in = lax.all_gather(lax.all_to_all(w_out, 'z', 0, 0), 'c', axis=0)]
  transfers between devices with their start and end apart: 3 -> 2, of which waited for: 3 -> 1; matrix products, arithmetic and copies ran while one was open for 0% -> 0% of each run, Pallas kernels for 0% -> 9%
where the time goes in v1:
time: 156 us; the launch traced here: 155 us
  blocking collectives  91.2 us (58%)
  Pallas kernels  35 us (22%)
  starting transfers between devices  14.5 us (9%)
  local copies, waits for them, and re-layouts  12.5 us (8%)
    all_to_all x1, blocking collectives, per_device(): z_in = lax.all_gather(lax.all_to_all(z_out, 'z', 0, 0), 'c', axis=0)  28 us
    all_to_all x1, blocking collectives, per_device(): lax.all_to_all(scalar_out, 'z', 0, 0)  22.9 us
    pallas_call x1, Pallas kernels, per_device(): call(first_apply, out_shape=(shape(COLS, ROWS, dtype=BF16), shape(COLS, 1...  16.3 us
    all_to_all x1, blocking collectives, per_device(): image_in = lax.all_to_all(image_out, ('y', 'x'), 0, 0)  14.7 us
    pallas_call x1, Pallas kernels, per_device(): call(cand_apply, out_shape=(shape(COLS, ROWS, dtype=BF16), shape(RHS, ROW...  14.2 us
    unnamed x24, local copies, waits for them, and re-layouts  12.5 us
    all_to_all x1, blocking collectives, per_device(): mean_in = lax.all_to_all(mean_out, ('y', 'x'), 0, 0)  9.82 us
    all_to_all x1, starting transfers between devices, per_device(): w_in = lax.all_gather(lax.all_to_all(w_out, 'z', 0, 0), 'c', axis=0)  7.78 us
  transfers between devices with their start and end apart: 2, of which 1 were waited for; matrix products, arithmetic and copies ran while one was open for 0% of the time, Pallas kernels for 9%

profile of v1, /device:TPU:1, one launch (start us, length us, event | category | flops | bytes accessed | tf_op | source)
XLA Modules:
  0.0 155.1 jit_solution(2088580616174355935)
XLA Ops:
  0.6 0.0 copy-start.4
  0.6 0.7 copy-done.4
  1.3 0.0 copy-start.7
  1.3 0.8 copy-done.7
  2.1 0.0 copy-start.8
  2.1 0.8 copy-done.8
  2.8 0.0 copy-start.9
  2.8 0.7 copy-done.9
  3.5 0.9 shard_map.68
  4.4 28.0 %all_to_all.30 = bf16[16,48,128]{2,1,0:T(8,128)(2,1)S(1)} all-to-all(bf16[16,48,128]{2,1,0:T(8,128)(2,1)S(1)} %get-tuple-element.18), channel_id=1, replica_groups=mesh['z'=16,'c'=2,'y'=4,'x'=4] {'z'}, dimensions={0} | all-to-all | bytes 393216 | tf_op jit(solution)/shard_map/all_to_all | solution.py:292
  32.4 6.8 %all-to-all-start = ((bf16[16,80,128]{2,1,0:T(8,128)(2,1)}), bf16[16,80,128]{2,1,0:T(8,128)(2,1)S(1)}, u32[]{:S(2)}, u32[]{:S(2)}) async-start(bf16[16,80,128]{2,1,0:T(8,128)(2,1)} %get-tuple-element.17), calls=%async_computation | async-start | bytes 655360 | tf_op jit(solution)/shard_map/all_to_all | solution.py:291
  39.2 6.8 %all-gather = bf16[32,48,128]{2,1,0:T(8,128)(2,1)S(1)} all-gather(bf16[16,48,128]{2,1,0:T(8,128)(2,1)S(1)} %all_to_all.30), channel_id=2, replica_groups=mesh['z'=16,'c'=2,'y'=4,'x'=4] {'c'}, dimensions={0}, use_global_device_ids=true | all-gather | bytes 589824 | tf_op jit(solution)/shard_map/all_gather | solution.py:292
  46.0 1.1 all-to-all-done.y_ref
  47.1 0.0 copy-start.5
  47.1 0.7 copy-done.5
  47.8 0.0 copy-start.10
  47.8 0.7 copy-done.10
  48.4 16.3 %shard_map.69 = (bf16[2048,1024]{1,0:T(8,128)(2,1)S(1)}, bf16[2048,128]{1,0:T(8,128)(2,1)S(1)}, bf16[16,32,128]{2,1,0:T(8,128)(2,1)S(1)}, bf16[16,16,1024]{2,1,0:T(8,128)(2,1)S(1)}) custom-call(bf16[16,80,128]{2,1,0:T(8,128)(2,1)S(1)} %all-to-all-done.y_ref, bf16[2,16,48,128]{3,2,1,0:T(8,128)(2,1)S(1)} %bitcast.6, f32[16,64]{1,0:T(8,128)S(1)} %copy-done.5, ...), custom_call_target="tpu_custom_call" | custom-call | flops 671088640 | bytes 4194304 | tf_op jit(solution)/shard_map/pallas_call | solution.py:296
  64.8 0.0 copy-start
  64.8 1.9 %copy-done = bf16[2048,1024]{1,0:T(8,128)(2,1)} copy-done((bf16[2048,1024]{1,0:T(8,128)(2,1)}, bf16[2048,1024]{1,0:T(8,128)(2,1)S(1)}, u32[]{:S(2)}) %copy-start) | copy-done | bytes 4194328
  66.7 14.7 %all_to_all.31.part_ref = bf16[16,16,1024]{2,1,0:T(8,128)(2,1)S(1)} all-to-all(bf16[16,16,1024]{2,1,0:T(8,128)(2,1)S(1)} %get-tuple-element.19), channel_id=1, replica_groups=mesh['z'=16,'c'=2,'y'=4,'x'=4] {'y','x'}, dimensions={0} | all-to-all | bytes 1048576 | tf_op jit(solution)/shard_map/all_to_all | solution.py:307
  81.4 1.0 shard_map.70
  82.4 0.0 copy-start.6
  82.4 0.0 copy-start.11
  82.4 7.8 %all-to-all-start.3 = ((bf16[16,16,128]{2,1,0:T(8,128)(2,1)}), bf16[16,16,128]{2,1,0:T(8,128)(2,1)S(1)}, u32[]{:S(2)}, u32[]{:S(2)}) async-start(bf16[16,16,128]{2,1,0:T(8,128)(2,1)} %get-tuple-element.20), calls=%async_computation.3 | async-start | bytes 131072 | tf_op jit(solution)/shard_map/all_to_all | solution.py:318
  90.1 14.2 %shard_map.71 = (bf16[2048,1024]{1,0:T(8,128)(2,1)S(1)}, f32[16,1024]{1,0:T(8,128)S(1)}) custom-call(bf16[16,80,128]{2,1,0:T(8,128)(2,1)S(1)} %all-to-all-done.y_ref, bf16[2048,128]{1,0:T(8,128)(2,1)S(1)} %get-tuple-element.25.col_ref, bf16[16,32,128]{2,1,0:T(8,128)(2,1)S(1)} %get-tuple-element.21.b_ref), custom_call_target="tpu_custom_call" | custom-call | flops 671088640 | bytes 4194304 | tf_op jit(solution)/shard_map/pallas_call | solution.py:308
  104.3 0.0 copy-start.2
  104.3 2.0 %copy-done.2 = bf16[2048,1024]{1,0:T(8,128)(2,1)} copy-done((bf16[2048,1024]{1,0:T(8,128)(2,1)}, bf16[2048,1024]{1,0:T(8,128)(2,1)S(1)}, u32[]{:S(2)}) %copy-start.2) | copy-done | bytes 4194328
  106.3 0.0 all-to-all-done.3
  106.3 4.4 %all-gather.1 = bf16[32,16,128]{2,1,0:T(8,128)(2,1)S(1)} all-gather(bf16[16,16,128]{2,1,0:T(8,128)(2,1)S(1)} %all-to-all-done.3), channel_id=3, replica_groups=mesh['z'=16,'c'=2,'y'=4,'x'=4] {'c'}, dimensions={0}, use_global_device_ids=true | all-gather | bytes 196608 | tf_op jit(solution)/shard_map/all_gather | solution.py:318
  110.7 0.0 copy-done.6
  110.7 0.0 copy-done.11
  110.7 0.0 copy-start.1
  110.7 2.2 %copy-done.1 = bf16[2048,1024]{1,0:T(8,128)(2,1)S(1)} copy-done((bf16[2048,1024]{1,0:T(8,128)(2,1)S(1)}, bf16[2048,1024]{1,0:T(8,128)(2,1)}, u32[]{:S(2)}) %copy-start.1) | copy-done | bytes 4194328
  112.9 0.0 copy-start.3
  112.9 2.2 %copy-done.3 = bf16[2048,1024]{1,0:T(8,128)(2,1)S(1)} copy-done((bf16[2048,1024]{1,0:T(8,128)(2,1)S(1)}, bf16[2048,1024]{1,0:T(8,128)(2,1)}, u32[]{:S(2)}) %copy-start.3) | copy-done | bytes 4194328
  115.1 1.7 %shard_map.72 = (f32[16,24,128]{2,1,0:T(8,128)S(1)}, f32[16,128]{1,0:T(8,128)S(1)}) custom-call(bf16[2,16,16,128]{3,2,1,0:T(8,128)(2,1)S(1)} %bitcast.5, bf16[16,32,128]{2,1,0:T(8,128)(2,1)S(1)} %get-tuple-element.21.b_ref, f32[16,1024]{1,0:T(8,128)S(1)} %get-tuple-element.22.w_ref, f32[16,1024]{1,0:T(8,128)S(1)} %get-tuple-element.23.br_ref, ...), custom_call_target="tpu_custom_call" | custom-call | tf_op jit(solution)/shard_map/pallas_call | solution.py:319
  116.8 9.8 %all_to_all.32.part_ref = f32[16,24,128]{2,1,0:T(8,128)S(1)} all-to-all(f32[16,24,128]{2,1,0:T(8,128)S(1)} %get-tuple-element.28), channel_id=1, replica_groups=mesh['z'=16,'c'=2,'y'=4,'x'=4] {'y','x'}, dimensions={0} | all-to-all | bytes 393216 | tf_op jit(solution)/shard_map/all_to_all | solution.py:324
  126.6 22.9 %all_to_all.33 = f32[16,1,128]{2,1,0:T(1,128)S(1)} all-to-all(f32[16,1,128]{2,1,0:T(1,128)S(1)} %get-tuple-element.29), channel_id=1, replica_groups=mesh['z'=16,'c'=2,'y'=4,'x'=4] {'z'}, dimensions={0} | all-to-all | bytes 16384 | tf_op jit(solution)/shard_map/all_to_all | solution.py:328
  149.5 4.7 %all-gather.2 = f32[32,1,128]{2,1,0:T(1,128)S(1)} all-gather(f32[16,1,128]{2,1,0:T(1,128)S(1)} %all_to_all.33), channel_id=4, replica_groups=mesh['z'=16,'c'=2,'y'=4,'x'=4] {'c'}, dimensions={0}, use_global_device_ids=true | all-gather | bytes 24576 | tf_op jit(solution)/shard_map/all_gather | solution.py:328
  154.2 0.9 shard_map.74
  (1 shorter events, 0.0 us)
Async XLA Ops:
  0.6 0.7 copy-start.4
  1.3 0.8 copy-start.7
  2.1 0.8 copy-start.8
  2.8 0.7 copy-start.9
  32.4 14.7 %all-to-all-start = ((bf16[16,80,128]{2,1,0:T(8,128)(2,1)}), bf16[16,80,128]{2,1,0:T(8,128)(2,1)S(1)}, u32[]{:S(2)}, u32[]{:S(2)}) async-start(bf16[16,80,128]{2,1,0:T(8,128)(2,1)} %get-tuple-element.17), calls=%async_computation | async-start | bytes 655360 | tf_op jit(solution)/shard_map/all_to_all | solution.py:291
  47.1 0.7 copy-start.5
  47.8 0.7 copy-start.10
  64.8 1.9 %copy-start = (bf16[2048,1024]{1,0:T(8,128)(2,1)}, bf16[2048,1024]{1,0:T(8,128)(2,1)S(1)}, u32[]{:S(2)}) copy-start(bf16[2048,1024]{1,0:T(8,128)(2,1)S(1)} %get-tuple-element.24.kern_ref) | copy-start | bytes 12582916
  82.4 28.3 %copy-start.6 = (f32[16,64]{1,0:T(8,128)S(1)}, f32[16,64]{1,0:T(8,128)}, u32[]{:S(2)}) copy-start(f32[16,64]{1,0:T(8,128)} %target_ref.7) | copy-start | bytes 12292
  82.4 28.3 %copy-start.11 = (f32[64]{0:T(128)S(1)}, f32[64]{0:T(128)}, u32[]{:S(2)}) copy-start(f32[64]{0:T(128)} %param.8) | copy-start | bytes 772
  82.4 24.0 %all-to-all-start.3 = ((bf16[16,16,128]{2,1,0:T(8,128)(2,1)}), bf16[16,16,128]{2,1,0:T(8,128)(2,1)S(1)}, u32[]{:S(2)}, u32[]{:S(2)}) async-start(bf16[16,16,128]{2,1,0:T(8,128)(2,1)} %get-tuple-element.20), calls=%async_computation.3 | async-start | bytes 131072 | tf_op jit(solution)/shard_map/all_to_all | solution.py:318
  104.3 2.0 %copy-start.2 = (bf16[2048,1024]{1,0:T(8,128)(2,1)}, bf16[2048,1024]{1,0:T(8,128)(2,1)S(1)}, u32[]{:S(2)}) copy-start(bf16[2048,1024]{1,0:T(8,128)(2,1)S(1)} %get-tuple-element.26.cand_ref) | copy-start | bytes 12582916
  110.7 2.2 %copy-start.1 = (bf16[2048,1024]{1,0:T(8,128)(2,1)S(1)}, bf16[2048,1024]{1,0:T(8,128)(2,1)}, u32[]{:S(2)}) copy-start(bf16[2048,1024]{1,0:T(8,128)(2,1)} %copy-done) | copy-start | bytes 12582916
  112.9 2.2 %copy-start.3 = (bf16[2048,1024]{1,0:T(8,128)(2,1)S(1)}, bf16[2048,1024]{1,0:T(8,128)(2,1)}, u32[]{:S(2)}) copy-start(bf16[2048,1024]{1,0:T(8,128)(2,1)} %copy-done.2) | copy-start | bytes 12582916

commit v2 on v1

v2 whole, which is shorter than its diff:
```python
import math

import jax
import jax.numpy as jnp
from jax import lax
from jax.experimental import pallas as pl
from jax.experimental.pallas import tpu as pltpu
from jax.sharding import Mesh, PartitionSpec as P

F32 = jnp.float32
BF16 = jnp.bfloat16

D = 64
S = 64
RHS = 16
NQ = 16
NZ = 16
ROWS = NQ * S
COLS = 2 * NZ * S
LOG2E = math.log2(math.e)
CHUNKS = 8
PIECE = COLS // CHUNKS
SMALL = pltpu.CompilerParams(vmem_limit_bytes=24 * 1024 * 1024)
LARGE = pltpu.CompilerParams(vmem_limit_bytes=63_000_000)


def halves(value):
    high = value.astype(BF16)
    return high, (value - high.astype(F32)).astype(BF16)


def thirds(value):
    high = value.astype(BF16).astype(F32)
    rest = value - high
    middle = rest.astype(BF16).astype(F32)
    low = (rest - middle).astype(BF16).astype(F32)
    return high, middle, low


def rows_of(width, pieces):
    index = lax.broadcasted_iota(jnp.int32, (16, width), 0)
    total = jnp.zeros((16, width), F32)
    for i, piece in enumerate(pieces):
        total = jnp.where(index == i, piece, total)
    return total


def column(row, start):
    lane = lax.broadcasted_iota(jnp.int32, (RHS, 128), 1)
    index = lax.broadcasted_iota(jnp.int32, (RHS, 128), 0)
    return jnp.sum(jnp.where(lane == index + start, row, 0.0), axis=1, keepdims=True)


def prepare(
    train_hbm, cand_hbm, inv_hbm, noise_hbm, target_hbm, y_ref, z_ref, side_ref,
    train_ref, cand_ref, inv_ref, noise_ref, target_ref, sems,
):
    copies = [
        pltpu.make_async_copy(source, target, sems.at[i])
        for i, (source, target) in enumerate(
            [
                (train_hbm, train_ref),
                (inv_hbm, inv_ref),
                (target_hbm, target_ref),
                (cand_hbm, cand_ref),
                (noise_hbm, noise_ref),
            ]
        )
    ]
    for copy in copies:
        copy.start()
    for copy in copies:
        copy.wait()
    eye = lax.broadcasted_iota(jnp.int32, (D, D), 0) == lax.broadcasted_iota(
        jnp.int32, (D, D), 1
    )
    inv = jnp.sum(jnp.where(eye, inv_ref[...], 0.0), axis=1, keepdims=True)
    train = train_ref[...] * inv
    cand = cand_ref[...] * inv
    target = target_ref[...]
    b_high, b_low = halves(target)
    b = jnp.concatenate([b_high, b_low], axis=1)
    both = jnp.concatenate([train.astype(BF16), cand.astype(BF16)], axis=1)
    folded = jnp.concatenate([train[:32].astype(BF16), train[32:].astype(BF16)], axis=1)
    for i in range(NQ):
        z_ref[i, 0:32, :] = folded
        z_ref[i, 32:48, :] = b
        y_ref[i, 0:64, :] = both
        y_ref[i, 64:80, :] = b
    side_ref[...] = jnp.concatenate(
        [target, jnp.broadcast_to(noise_ref[...], (RHS, S))], axis=1
    )


def row_side(y_ref, j, first):
    points = jnp.concatenate(
        [y_ref[2 * j, 0:64, first : first + 64], y_ref[2 * j + 1, 0:64, first : first + 64]],
        axis=1,
    ).astype(F32)
    norm = jnp.sum(points * points, axis=0, keepdims=True)
    extra = rows_of(128, [*thirds(norm), 1.0, 1.0, 1.0])
    return jnp.concatenate(
        [-2.0 * points, extra, jnp.zeros((48, 128), F32)], axis=0
    ).astype(BF16)


def col_side(z_ref, col_ref, b_ref):
    for z in range(NZ):
        low, high = z_ref[0, z, 0:48, :], z_ref[1, z, 0:48, :]
        first = jnp.concatenate([low[:, :64], high[:, :64]], axis=1)
        second = jnp.concatenate([low[:, 64:], high[:, 64:]], axis=1)
        points = jnp.concatenate([first[0:32], second[0:32]], axis=0).astype(F32)
        b_ref[:, z * 128 : z * 128 + 128] = jnp.concatenate([first[32:48], second[32:48]], axis=0)
        norm = jnp.sum(points * points, axis=0, keepdims=True)
        extra = rows_of(128, [1.0, 1.0, 1.0, *thirds(norm)])
        full = jnp.concatenate([points, extra, jnp.zeros((48, 128), F32)], axis=0)
        col_ref[z * 128 : z * 128 + 128, :] = full.T.astype(BF16)


def matern_of(inner):
    five_dist = jnp.maximum(inner, 1e-30) * 5.0
    scaled = five_dist * lax.rsqrt(five_dist)
    return (1.0 + scaled + five_dist * (1.0 / 3.0)) * jnp.exp2(scaled * (-LOG2E))


def piece(tile_ref, hbm_ref, sems, i):
    span = pl.ds(pl.multiple_of(i * PIECE, PIECE), PIECE)
    return tile_ref.at[span, :], hbm_ref.at[span, :], sems.at[i]


def fill(col_ref, row_ref, kern_ref, hbm_ref, sems, even_ref, odd_ref):
    def inner(z, out_ref):
        points = col_ref[pl.ds(pl.multiple_of(z * 128, 128), 128), :]
        out_ref[...] = jnp.dot(points, row_ref[...], preferred_element_type=F32)

    def spread(z, in_ref):
        for i in range(8):
            kern_ref[pl.ds(pl.multiple_of(z * 128 + i * 16, 16), 16), :] = matern_of(
                in_ref[i * 16 : i * 16 + 16, :]
            ).astype(BF16)

    inner(0, even_ref)

    def send(i):
        pltpu.make_async_copy(*piece(kern_ref, hbm_ref, sems, i)).start()

    def step(i, _):
        @pl.when(i > 0)
        def _():
            send(i - 1)

        inner(2 * i + 1, odd_ref)
        spread(2 * i, even_ref)
        inner(jnp.minimum(2 * i + 2, NZ - 1), even_ref)
        spread(2 * i + 1, odd_ref)
        return 0

    lax.fori_loop(0, NZ // 2, step, 0)


def finish_fill(kern_ref, hbm_ref, sems):
    for i in range(CHUNKS):
        pltpu.make_async_copy(*piece(kern_ref, hbm_ref, sems, i)).wait()


def apply(vectors, kern_ref):
    total = jnp.dot(vectors, kern_ref[...], preferred_element_type=F32)
    return total[0:16] + total[16:32]


def own_block(q):
    return pl.ds(pl.multiple_of((q // 2) * 128, 128), 128)


def own_mask(q):
    lane = lax.broadcasted_iota(jnp.int32, (RHS, 128), 1)
    return (lane // 64) == (q % 2)


def position():
    return lax.axis_index("y") * 4 + lax.axis_index("x")


def first_apply(
    y_ref, col_ref, b_ref, side_ref, hbm_ref, out_ref,
    acc_ref, row_ref, even_ref, odd_ref, kern_ref, sems,
):
    q = position()
    for j in range(NQ // 2):
        row_ref[:, j * 128 : j * 128 + 128] = row_side(y_ref, j, 0)
    fill(col_ref, row_ref, kern_ref, hbm_ref, sems, even_ref, odd_ref)
    acc_ref[...] = apply(b_ref[...], kern_ref)
    pltpu.make_async_copy(*piece(kern_ref, hbm_ref, sems, CHUNKS - 1)).start()
    own = side_ref[:, 0:64] * side_ref[:, 64:128]
    twice = jnp.concatenate([own, own], axis=1)
    acc_ref[:, own_block(q)] += jnp.where(own_mask(q), twice, 0.0)
    image = acc_ref[...].astype(BF16)
    for i in range(NQ):
        out_ref[i] = image
    finish_fill(kern_ref, hbm_ref, sems)


def cand_apply(
    y_ref, col_ref, b_ref, hbm_ref, out_ref, row_ref, even_ref, odd_ref, kern_ref, sems
):
    for j in range(NQ // 2):
        row_ref[:, j * 128 : j * 128 + 128] = row_side(y_ref, j, 64)
    fill(col_ref, row_ref, kern_ref, hbm_ref, sems, even_ref, odd_ref)
    out_ref[...] = apply(b_ref[...], kern_ref)
    pltpu.make_async_copy(*piece(kern_ref, hbm_ref, sems, CHUNKS - 1)).start()
    finish_fill(kern_ref, hbm_ref, sems)


def merge_image(part_ref, y_ref, out_ref, w_ref, br_ref):
    q = position()
    total = part_ref[0].astype(F32)
    for i in range(1, NQ):
        total = total + part_ref[i].astype(F32)
    w_ref[...] = total
    for j in range(NQ // 2):
        even, odd = y_ref[2 * j, 64:80, :].astype(F32), y_ref[2 * j + 1, 64:80, :].astype(F32)
        br_ref[:, j * 128 : j * 128 + 128] = jnp.concatenate(
            [even[:, :64] + even[:, 64:], odd[:, :64] + odd[:, 64:]], axis=1
        )
    b = br_ref[...]
    bw = jnp.sum(b * total, axis=1, keepdims=True)
    bb = jnp.sum(b * b, axis=1, keepdims=True)
    block = w_ref[:, own_block(q)]
    own = jnp.where(q % 2 == 0, block[:, :64], block[:, 64:])
    lane = lax.broadcasted_iota(jnp.int32, (RHS, 64), 1)
    scalars = jnp.zeros((RHS, 64), F32)
    for i, piece in enumerate([*thirds(bw), *thirds(bb)]):
        scalars = jnp.where(lane == i, piece, scalars)
    message = jnp.concatenate([own, scalars], axis=1).astype(BF16)
    for i in range(NZ):
        out_ref[i] = message


def second_apply(
    s_ref, b_ref, w_ref, br_ref, kern_hbm, cand_hbm, mean_ref, side_ref, out_ref, own_ref,
    r_ref, kern_ref, cand_ref, kern_sems, cand_sems,
):
    def fetch(hbm_ref, tile_ref, sems, i):
        target, source, sem = piece(tile_ref, hbm_ref, sems, i)
        return pltpu.make_async_copy(source, target, sem)

    for i in range(CHUNKS):
        fetch(kern_hbm, kern_ref, kern_sems, i).start()
    for i in range(CHUNKS):
        fetch(cand_hbm, cand_ref, cand_sems, i).start()
    q = position()
    sums = s_ref[0, 0, :, 64:128].astype(F32)
    for c in range(2):
        for z in range(NZ):
            if c or z:
                sums = sums + s_ref[c, z, :, 64:128].astype(F32)
    lane = lax.broadcasted_iota(jnp.int32, (RHS, 64), 1)
    bw = jnp.sum(jnp.where(lane < 3, sums, 0.0), axis=1, keepdims=True)
    bb = jnp.sum(jnp.where((lane >= 3) & (lane < 6), sums, 0.0), axis=1, keepdims=True)
    alpha = bb / bw
    for z in range(NZ):
        w = jnp.concatenate([s_ref[0, z, :, 0:64], s_ref[1, z, :, 0:64]], axis=1).astype(F32)
        span = slice(z * 128, z * 128 + 128)
        b = b_ref[0:16, span].astype(F32) + b_ref[16:32, span].astype(F32)
        high, low = halves(b - alpha * w)
        r_ref[:, span] = jnp.concatenate([high, low], axis=0)
    def gathered(hbm_ref, tile_ref, sems):
        total = None
        for i in range(CHUNKS):
            fetch(hbm_ref, tile_ref, sems, i).wait()
            span = slice(i * PIECE, i * PIECE + PIECE)
            part = jnp.dot(r_ref[:, span], tile_ref[span, :], preferred_element_type=F32)
            total = part if total is None else total + part
        return total[0:16] + total[16:32]

    applied = gathered(kern_hbm, kern_ref, kern_sems)
    mean = gathered(cand_hbm, cand_ref, cand_sems)
    mean0 = mean_ref[...]
    for i in range(NQ):
        span = slice(i * 64, i * 64 + 64)
        out_ref[i, 0:16, :] = jnp.concatenate([mean0[:, span], mean[:, span]], axis=1)
    r_row = br_ref[...] - alpha * w_ref[...]
    block = w_ref[:, own_block(q)]
    own_w = jnp.where(q % 2 == 0, block[:, :64], block[:, 64:])
    target, noise = side_ref[:, 0:64], side_ref[:, 64:128]
    own_r = target - alpha * own_w
    s = jnp.sum(r_row * applied, axis=1, keepdims=True) + jnp.sum(
        noise * own_r * own_r, axis=1, keepdims=True
    )
    t = jnp.sum(own_r * own_w, axis=1, keepdims=True)
    rr = jnp.sum(own_r * own_r, axis=1, keepdims=True)
    wide = lax.broadcasted_iota(jnp.int32, (RHS, 128), 1)
    index = lax.broadcasted_iota(jnp.int32, (RHS, 128), 0)
    spread = (
        jnp.where(wide == index, s, 0.0)
        + jnp.where(wide == index + 16, t, 0.0)
        + jnp.where(wide == index + 32, rr, 0.0)
    )
    spread = jnp.sum(spread, axis=0, keepdims=True)
    eight = lax.broadcasted_iota(jnp.int32, (8, 128), 0)
    spread = jnp.where(eight == 0, spread, 0.0)
    for i in range(NQ):
        out_ref[i, 16:24, :] = spread
    side = jnp.where(lane == 0, bb, jnp.where(lane == 1, bw, 0.0))
    own_ref[...] = jnp.concatenate([own_r, side], axis=1)


def merge_mean(part_ref, mean_ref, out_ref):
    total = part_ref[0]
    for i in range(1, NQ):
        total = total + part_ref[i]
    mean_ref[...] = total[0:16]
    for i in range(NZ):
        out_ref[i] = total[16:17]


def finish(s_ref, own_ref, mean_ref, side_ref, solution_ref, post_ref):
    total = s_ref[0, 0]
    for c in range(2):
        for z in range(NZ):
            if c or z:
                total = total + s_ref[c, z]
    s, t, rr = column(total, 0), column(total, 16), column(total, 32)
    own_r = own_ref[:, 0:64]
    bb, bw = own_ref[:, 64:65], own_ref[:, 65:66]
    alpha0 = bb / bw
    beta = rr / bb
    alpha1 = rr / (s + 2.0 * beta * t + beta * beta * bw)
    target = side_ref[:, 0:64]
    solution_ref[...] = alpha0 * target + alpha1 * (own_r + beta * target)
    mean = mean_ref[...]
    post_ref[...] = (alpha0 + alpha1 * beta) * mean[:, :64] + alpha1 * mean[:, 64:]


def shape(*dims, dtype=F32):
    return jax.ShapeDtypeStruct(dims, dtype)


def per_device(train_points, cand_points, inv_length, noise, targets):
    call = pl.pallas_call
    y_out, z_out, side = call(
        prepare,
        in_specs=[pl.BlockSpec(memory_space=pltpu.HBM)] * 5,
        out_shape=(
            shape(NQ, 80, 128, dtype=BF16),
            shape(NZ, 48, 128, dtype=BF16),
            shape(RHS, 128),
        ),
        scratch_shapes=[
            pltpu.VMEM((D, S), F32),
            pltpu.VMEM((D, S), F32),
            pltpu.VMEM((1, D), F32),
            pltpu.VMEM((1, S), F32),
            pltpu.VMEM((RHS, S), F32),
            pltpu.SemaphoreType.DMA((5,)),
        ],
        compiler_params=pltpu.CompilerParams(vmem_limit_bytes=67043328),
    )(train_points, cand_points, inv_length.reshape(1, D), noise.reshape(1, S), targets)
    z_in = lax.all_gather(lax.all_to_all(z_out, "z", 0, 0), "c", axis=0)
    y_in = lax.all_to_all(y_out, ("y", "x"), 0, 0)
    col, b_col = call(
        col_side,
        compiler_params=SMALL,
        out_shape=(shape(COLS, 128, dtype=BF16), shape(32, COLS, dtype=BF16)),
        cost_estimate=pl.CostEstimate(
            flops=COLS * 1000, bytes_accessed=4 * COLS * 128, transcendentals=0
        ),
    )(z_in)
    cost = pl.CostEstimate(
        flops=2 * ROWS * COLS * 160, bytes_accessed=2 * ROWS * COLS, transcendentals=2 * ROWS * COLS
    )
    tiles = [
        pltpu.VMEM((128, ROWS), BF16),
        pltpu.VMEM((128, ROWS), F32),
        pltpu.VMEM((128, ROWS), F32),
        pltpu.VMEM((COLS, ROWS), BF16),
        pltpu.SemaphoreType.DMA((CHUNKS,)),
    ]
    vmem = pl.BlockSpec(memory_space=pltpu.VMEM)
    anywhere = pl.BlockSpec(memory_space=pl.ANY)
    kern, image_out = call(
        first_apply,
        compiler_params=LARGE,
        in_specs=[vmem] * 4,
        out_specs=(anywhere, vmem),
        out_shape=(
            shape(COLS, ROWS, dtype=BF16),
            shape(NQ, RHS, ROWS, dtype=BF16),
        ),
        scratch_shapes=[pltpu.VMEM((RHS, ROWS), F32), *tiles],
        cost_estimate=cost,
    )(y_in, col, b_col, side)
    image_in = lax.all_to_all(image_out, ("y", "x"), 0, 0)
    kern_cand, mean0 = call(
        cand_apply,
        compiler_params=LARGE,
        in_specs=[vmem] * 3,
        out_specs=(anywhere, vmem),
        out_shape=(shape(COLS, ROWS, dtype=BF16), shape(RHS, ROWS)),
        scratch_shapes=tiles,
        cost_estimate=cost,
    )(y_in, col, b_col)
    w_out, w_row, b_row = call(
        merge_image,
        compiler_params=SMALL,
        out_shape=(shape(NZ, RHS, 128, dtype=BF16), shape(RHS, ROWS), shape(RHS, ROWS)),
    )(image_in, y_in)
    w_in = lax.all_gather(lax.all_to_all(w_out, "z", 0, 0), "c", axis=0)
    mean_out, own = call(
        second_apply,
        compiler_params=LARGE,
        in_specs=[vmem] * 4 + [anywhere] * 2 + [vmem] * 2,
        out_shape=(shape(NQ, 24, 128), shape(RHS, 128)),
        scratch_shapes=[
            pltpu.VMEM((32, COLS), BF16),
            pltpu.VMEM((COLS, ROWS), BF16),
            pltpu.VMEM((COLS, ROWS), BF16),
            pltpu.SemaphoreType.DMA((CHUNKS,)),
            pltpu.SemaphoreType.DMA((CHUNKS,)),
        ],
    )(w_in, b_col, w_row, b_row, kern, kern_cand, mean0, side)
    mean_in = lax.all_to_all(mean_out, ("y", "x"), 0, 0)
    mean, scalar_out = call(
        merge_mean,
        compiler_params=SMALL,
        out_shape=(shape(RHS, 128), shape(NZ, 1, 128)),
    )(mean_in)
    scalar_in = lax.all_gather(lax.all_to_all(scalar_out, "z", 0, 0), "c", axis=0)
    return call(
        finish, compiler_params=SMALL, out_shape=(shape(RHS, S), shape(RHS, S))
    )(
        scalar_in, own, mean, side
    )


def solution(mesh):
    fine = Mesh(mesh.devices.reshape(16, 2, 4, 4), ("z", "c", "y", "x"))
    every = ("z", "c", "y", "x")
    wide = P(None, every)
    return jax.shard_map(
        per_device,
        mesh=fine,
        in_specs=(wide, wide, P(), P(every), wide),
        out_specs=(wide, wide),
        check_vma=False,
    )
```

time: 156 us -> 139 us (0.89)
  Pallas kernels: 35 us -> 25.7 us
  local copies, waits for them, and re-layouts: 12.5 us -> 5.18 us
  waiting for transfers between devices: 1.06 us -> 4.25 us
  starting transfers between devices: 14.5 us -> 12.2 us
    pallas_call x7 -> x8, Pallas kernels: 35 us -> 25.7 us  [the longest x1 7.99 us: per_device(): call(first_apply, compiler_params=LARGE, in_specs=[vmem] * 4, out_specs=(...]
    unnamed x24 -> x16, local copies, waits for them, and re-layouts: 12.5 us -> 5.18 us
    all_to_all x1, blocking collectives: 22.9 us -> 17.3 us  [per_device(): lax.all_to_all(scalar_out, 'z', 0, 0)]
    all_to_all x1, waiting for transfers between devices: 0.01 us -> 4.25 us  [per_device(): w_in = lax.all_gather(lax.all_to_all(w_out, 'z', 0, 0), 'c', axis=0)]
    all_to_all x1, starting transfers between devices: 7.78 us -> 5.43 us  [per_device(): w_in = lax.all_gather(lax.all_to_all(w_out, 'z', 0, 0), 'c', axis=0)]
    all_to_all x1, blocking collectives: 14.7 us -> 16.8 us  [per_device(): image_in = lax.all_to_all(image_out, ('y', 'x'), 0, 0)]
  transfers between devices with their start and end apart: 2 -> 2, of which waited for: 1 -> 1; matrix products, arithmetic and copies ran while one was open for 0% -> 0% of each run, Pallas kernels for 9% -> 6%
where the time goes in v2:
time: 139 us; the launch traced here: 138 us
  blocking collectives  90.2 us (65%)
  Pallas kernels  25.7 us (18%)
  starting transfers between devices  12.2 us (9%)
  local copies, waits for them, and re-layouts  5.18 us (4%)
  waiting for transfers between devices  4.25 us (3%)
    all_to_all x1, blocking collectives, per_device(): z_in = lax.all_gather(lax.all_to_all(z_out, 'z', 0, 0), 'c', axis=0)  28.2 us
    all_to_all x1, blocking collectives, per_device(): lax.all_to_all(scalar_out, 'z', 0, 0)  17.3 us
    all_to_all x1, blocking collectives, per_device(): image_in = lax.all_to_all(image_out, ('y', 'x'), 0, 0)  16.8 us
    all_to_all x1, blocking collectives, per_device(): mean_in = lax.all_to_all(mean_out, ('y', 'x'), 0, 0)  11.2 us
    pallas_call x1, Pallas kernels, per_device(): call(first_apply, compiler_params=LARGE, in_specs=[vmem] * 4, out_specs=(...  7.99 us
    pallas_call x1, Pallas kernels, per_device(): call(cand_apply, compiler_params=LARGE, in_specs=[vmem] * 3, out_specs=(a...  7.31 us
    all_gather x1, blocking collectives, per_device(): z_in = lax.all_gather(lax.all_to_all(z_out, 'z', 0, 0), 'c', axis=0)  6.83 us
    all_to_all x1, starting transfers between devices, per_device(): y_in = lax.all_to_all(y_out, ('y', 'x'), 0, 0)  6.76 us
  transfers between devices with their start and end apart: 2, of which 1 were waited for; matrix products, arithmetic and copies ran while one was open for 0% of the time, Pallas kernels for 6%

profile of v2, /device:TPU:1, one launch (start us, length us, event | category | flops | bytes accessed | tf_op | source)
XLA Modules:
  0.0 138.3 jit_solution(12051233447282050958)
XLA Ops:
  0.6 1.8 %shard_map.68 = (bf16[16,80,128]{2,1,0:T(8,128)(2,1)}, bf16[16,48,128]{2,1,0:T(8,128)(2,1)}, f32[16,128]{1,0:T(8,128)}) custom-call(f32[64,64]{1,0:T(8,128)} %train_hbm.1, f32[64,64]{1,0:T(8,128)} %cand_hbm.1, f32[1,64]{1,0:T(1,128)} %bitcast.8, f32[1,64]{1,0:T(1,128)} %bitcast.9, f32[16,64]{1,0:T(8,128)} %target_hbm.1), custom_call_target="tpu_custom_call" | custom-call | tf_op jit(solution)/shard_map/pallas_call | solution.py:341
  2.5 28.2 %all_to_all.30 = bf16[16,48,128]{2,1,0:T(8,128)(2,1)S(1)} all-to-all(bf16[16,48,128]{2,1,0:T(8,128)(2,1)} %get-tuple-element.19), channel_id=1, replica_groups=mesh['z'=16,'c'=2,'y'=4,'x'=4] {'z'}, dimensions={0} | all-to-all | bytes 393216 | tf_op jit(solution)/shard_map/all_to_all | solution.py:359
  30.7 6.8 %all-to-all-start = ((bf16[16,80,128]{2,1,0:T(8,128)(2,1)}), bf16[16,80,128]{2,1,0:T(8,128)(2,1)S(1)}, u32[]{:S(2)}, u32[]{:S(2)}) async-start(bf16[16,80,128]{2,1,0:T(8,128)(2,1)} %get-tuple-element.18), calls=%async_computation | async-start | bytes 655360 | tf_op jit(solution)/shard_map/all_to_all | solution.py:360
  37.5 6.8 %all-gather = bf16[32,48,128]{2,1,0:T(8,128)(2,1)S(1)} all-gather(bf16[16,48,128]{2,1,0:T(8,128)(2,1)S(1)} %all_to_all.30), channel_id=2, replica_groups=mesh['z'=16,'c'=2,'y'=4,'x'=4] {'c'}, dimensions={0}, use_global_device_ids=true | all-gather | bytes 589824 | tf_op jit(solution)/shard_map/all_gather | solution.py:359
  44.3 0.5 shard_map.69
  44.8 0.0 copy-start.2
  44.8 0.7 copy-done.2
  45.4 0.0 copy-start.7
  45.4 0.8 copy-done.7
  46.3 0.0 all-to-all-done.y_ref
  46.3 0.0 copy-start
  46.3 0.8 copy-done
  47.0 8.0 %shard_map.70 = (bf16[2048,1024]{1,0:T(8,128)(2,1)}, bf16[16,16,1024]{2,1,0:T(8,128)(2,1)}) custom-call(bf16[16,80,128]{2,1,0:T(8,128)(2,1)} %copy-done, bf16[2048,128]{1,0:T(8,128)(2,1)} %copy-done.7, bf16[32,2048]{1,0:T(8,128)(2,1)} %copy-done.2, f32[16,128]{1,0:T(8,128)} %get-tuple-element.22.side_ref), custom_call_target="tpu_custom_call" | custom-call | flops 671088640 | bytes 4194304 | tf_op jit(solution)/shard_map/pallas_call | solution.py:381
  55.0 16.8 %all_to_all.31.part_ref = bf16[16,16,1024]{2,1,0:T(8,128)(2,1)S(1)} all-to-all(bf16[16,16,1024]{2,1,0:T(8,128)(2,1)} %get-tuple-element.23), channel_id=1, replica_groups=mesh['z'=16,'c'=2,'y'=4,'x'=4] {'y','x'}, dimensions={0} | all-to-all | bytes 1048576 | tf_op jit(solution)/shard_map/all_to_all | solution.py:393
  71.8 0.0 copy-start.1
  71.8 1.0 copy-done.1
  72.8 1.0 shard_map.71
  73.8 0.0 copy-start.3
  73.8 0.6 copy-done.3
  74.4 0.0 copy-start.4
  74.4 0.6 copy-done.4
  75.0 5.4 %all-to-all-start.3 = ((bf16[16,16,128]{2,1,0:T(8,128)(2,1)}), bf16[16,16,128]{2,1,0:T(8,128)(2,1)S(1)}, u32[]{:S(2)}, u32[]{:S(2)}) async-start(bf16[16,16,128]{2,1,0:T(8,128)(2,1)} %get-tuple-element.24), calls=%async_computation.3 | async-start | bytes 131072 | tf_op jit(solution)/shard_map/all_to_all | solution.py:408
  80.4 7.3 %shard_map.72 = (bf16[2048,1024]{1,0:T(8,128)(2,1)}, f32[16,1024]{1,0:T(8,128)}) custom-call(bf16[16,80,128]{2,1,0:T(8,128)(2,1)} %copy-done, bf16[2048,128]{1,0:T(8,128)(2,1)} %copy-done.7, bf16[32,2048]{1,0:T(8,128)(2,1)} %copy-done.2), custom_call_target="tpu_custom_call" | custom-call | flops 671088640 | bytes 4194304 | tf_op jit(solution)/shard_map/pallas_call | solution.py:394
  87.8 4.2 %all-to-all-done.3 = bf16[16,16,128]{2,1,0:T(8,128)(2,1)S(1)} async-done(((bf16[16,16,128]{2,1,0:T(8,128)(2,1)}), bf16[16,16,128]{2,1,0:T(8,128)(2,1)S(1)}, u32[]{:S(2)}, u32[]{:S(2)}) %all-to-all-start.3) | async-done | bytes 65568 | tf_op jit(solution)/shard_map/all_to_all | solution.py:408
  92.0 5.7 %all-gather.1 = bf16[32,16,128]{2,1,0:T(8,128)(2,1)} all-gather(bf16[16,16,128]{2,1,0:T(8,128)(2,1)S(1)} %all-to-all-done.3), channel_id=3, replica_groups=mesh['z'=16,'c'=2,'y'=4,'x'=4] {'c'}, dimensions={0}, use_global_device_ids=true | all-gather | bytes 196608 | tf_op jit(solution)/shard_map/all_gather | solution.py:408
  97.7 0.0 copy-start.5
  97.7 6.3 %shard_map.73 = (f32[16,24,128]{2,1,0:T(8,128)}, f32[16,128]{1,0:T(8,128)}) custom-call(bf16[2,16,16,128]{3,2,1,0:T(8,128)(2,1)} %bitcast.7, bf16[32,2048]{1,0:T(8,128)(2,1)} %copy-done.2, f32[16,1024]{1,0:T(8,128)} %copy-done.3, f32[16,1024]{1,0:T(8,128)} %copy-done.4, bf16[2048,1024]{1,0:T(8,128)(2,1)} %get-tuple-element.27.kern_hbm, ...), custom_call_target="tpu_custom_call" | custom-call | tf_op jit(solution)/shard_map/pallas_call | solution.py:409
  104.0 11.2 %all_to_all.32.part_ref = f32[16,24,128]{2,1,0:T(8,128)S(1)} all-to-all(f32[16,24,128]{2,1,0:T(8,128)} %get-tuple-element.30), channel_id=1, replica_groups=mesh['z'=16,'c'=2,'y'=4,'x'=4] {'y','x'}, dimensions={0} | all-to-all | bytes 393216 | tf_op jit(solution)/shard_map/all_to_all | solution.py:422
  115.3 17.3 %all_to_all.33 = f32[16,1,128]{2,1,0:T(1,128)S(1)} all-to-all(f32[16,1,128]{2,1,0:T(1,128)S(1)} %get-tuple-element.31), channel_id=1, replica_groups=mesh['z'=16,'c'=2,'y'=4,'x'=4] {'z'}, dimensions={0} | all-to-all | bytes 16384 | tf_op jit(solution)/shard_map/all_to_all | solution.py:428
  132.6 4.1 %all-gather.2 = f32[32,1,128]{2,1,0:T(1,128)S(1)} all-gather(f32[16,1,128]{2,1,0:T(1,128)S(1)} %all_to_all.33), channel_id=4, replica_groups=mesh['z'=16,'c'=2,'y'=4,'x'=4] {'c'}, dimensions={0}, use_global_device_ids=true | all-gather | bytes 24576 | tf_op jit(solution)/shard_map/all_gather | solution.py:428
  136.7 0.0 copy-done.5
  136.7 0.0 copy-start.6
  136.7 0.7 copy-done.6
  137.4 0.9 shard_map.75
  (1 shorter events, 0.0 us)
Async XLA Ops:
  30.7 15.6 %all-to-all-start = ((bf16[16,80,128]{2,1,0:T(8,128)(2,1)}), bf16[16,80,128]{2,1,0:T(8,128)(2,1)S(1)}, u32[]{:S(2)}, u32[]{:S(2)}) async-start(bf16[16,80,128]{2,1,0:T(8,128)(2,1)} %get-tuple-element.18), calls=%async_computation | async-start | bytes 655360 | tf_op jit(solution)/shard_map/all_to_all | solution.py:360
  44.8 0.7 copy-start.2
  45.4 0.8 copy-start.7
  46.3 0.8 copy-start
  71.8 1.0 copy-start.1
  73.8 0.6 copy-start.3
  74.4 0.6 copy-start.4
  75.0 17.0 %all-to-all-start.3 = ((bf16[16,16,128]{2,1,0:T(8,128)(2,1)}), bf16[16,16,128]{2,1,0:T(8,128)(2,1)S(1)}, u32[]{:S(2)}, u32[]{:S(2)}) async-start(bf16[16,16,128]{2,1,0:T(8,128)(2,1)} %get-tuple-element.24), calls=%async_computation.3 | async-start | bytes 131072 | tf_op jit(solution)/shard_map/all_to_all | solution.py:408
  97.7 39.0 %copy-start.5 = (f32[16,128]{1,0:T(8,128)S(1)}, f32[16,128]{1,0:T(8,128)}, u32[]{:S(2)}) copy-start(f32[16,128]{1,0:T(8,128)} %get-tuple-element.22.side_ref) | copy-start | bytes 24580
  136.7 0.7 copy-start.6

commit v3 on v2

v3 whole, which is shorter than its diff:
```python
import math

import jax
import jax.numpy as jnp
from jax import lax
from jax.experimental import pallas as pl
from jax.experimental.pallas import tpu as pltpu
from jax.sharding import Mesh, PartitionSpec as P

F32 = jnp.float32
BF16 = jnp.bfloat16

D = 64
S = 64
RHS = 16
NQ = 16
NZ = 16
ROWS = NQ * S
COLS = 2 * NZ * S
LOG2E = math.log2(math.e)
CHUNKS = 8
PIECE = COLS // CHUNKS
PARAMS = pltpu.CompilerParams(vmem_limit_bytes=24 * 1024 * 1024)


def halves(value):
    high = value.astype(BF16)
    return high, (value - high.astype(F32)).astype(BF16)


def thirds(value):
    high = value.astype(BF16).astype(F32)
    rest = value - high
    middle = rest.astype(BF16).astype(F32)
    low = (rest - middle).astype(BF16).astype(F32)
    return high, middle, low


def rows_of(width, pieces):
    index = lax.broadcasted_iota(jnp.int32, (16, width), 0)
    total = jnp.zeros((16, width), F32)
    for i, piece in enumerate(pieces):
        total = jnp.where(index == i, piece, total)
    return total


def column(row, start):
    lane = lax.broadcasted_iota(jnp.int32, (RHS, 128), 1)
    index = lax.broadcasted_iota(jnp.int32, (RHS, 128), 0)
    return jnp.sum(jnp.where(lane == index + start, row, 0.0), axis=1, keepdims=True)


def prepare(
    train_hbm, cand_hbm, inv_hbm, noise_hbm, target_hbm, y_ref, z_ref, side_ref,
    train_ref, cand_ref, inv_ref, noise_ref, target_ref, sems,
):
    copies = [
        pltpu.make_async_copy(source, target, sems.at[i])
        for i, (source, target) in enumerate(
            [
                (train_hbm, train_ref),
                (inv_hbm, inv_ref),
                (target_hbm, target_ref),
                (cand_hbm, cand_ref),
                (noise_hbm, noise_ref),
            ]
        )
    ]
    for copy in copies:
        copy.start()
    for copy in copies:
        copy.wait()
    eye = lax.broadcasted_iota(jnp.int32, (D, D), 0) == lax.broadcasted_iota(
        jnp.int32, (D, D), 1
    )
    inv = jnp.sum(jnp.where(eye, inv_ref[...], 0.0), axis=1, keepdims=True)
    train = train_ref[...] * inv
    cand = cand_ref[...] * inv
    target = target_ref[...]
    b_high, b_low = halves(target)
    b = jnp.concatenate([b_high, b_low], axis=1)
    both = jnp.concatenate([train.astype(BF16), cand.astype(BF16)], axis=1)
    folded = jnp.concatenate([train[:32].astype(BF16), train[32:].astype(BF16)], axis=1)
    for i in range(NQ):
        z_ref[i, 0:32, :] = folded
        z_ref[i, 32:48, :] = b
        y_ref[i, 0:64, :] = both
        y_ref[i, 64:80, :] = b
    side_ref[...] = jnp.concatenate(
        [target, jnp.broadcast_to(noise_ref[...], (RHS, S))], axis=1
    )


def row_side(y_ref, j, first):
    points = jnp.concatenate(
        [y_ref[2 * j, 0:64, first : first + 64], y_ref[2 * j + 1, 0:64, first : first + 64]],
        axis=1,
    ).astype(F32)
    norm = jnp.sum(points * points, axis=0, keepdims=True)
    extra = rows_of(128, [*thirds(norm), 1.0, 1.0, 1.0])
    return jnp.concatenate(
        [-2.0 * points, extra, jnp.zeros((48, 128), F32)], axis=0
    ).astype(BF16)


def col_side(z_ref, col_ref, b_ref):
    for z in range(NZ):
        low, high = z_ref[0, z].astype(F32), z_ref[1, z].astype(F32)
        first = jnp.concatenate([low[:, :64], high[:, :64]], axis=1)
        second = jnp.concatenate([low[:, 64:], high[:, 64:]], axis=1)
        points = jnp.concatenate([first[0:32], second[0:32]], axis=0)
        b_ref[:, z * 128 : z * 128 + 128] = jnp.concatenate(
            [first[32:48], second[32:48]], axis=0
        ).astype(BF16)
        norm = jnp.sum(points * points, axis=0, keepdims=True)
        extra = rows_of(128, [1.0, 1.0, 1.0, *thirds(norm)])
        full = jnp.concatenate([points, extra, jnp.zeros((48, 128), F32)], axis=0)
        col_ref[z * 128 : z * 128 + 128, :] = full.T.astype(BF16)


def matern_of(inner):
    five_dist = jnp.maximum(inner, 1e-30) * 5.0
    scaled = five_dist * lax.rsqrt(five_dist)
    return (1.0 + scaled + five_dist * (1.0 / 3.0)) * jnp.exp2(scaled * (-LOG2E))


def piece(tile_ref, hbm_ref, sems, i):
    span = pl.ds(pl.multiple_of(i * PIECE, PIECE), PIECE)
    return tile_ref.at[span, :], hbm_ref.at[span, :], sems.at[i]


def fill(col_ref, row_ref, kern_ref, even_ref, odd_ref, send=None, low_ref=None):
    def inner(z, out_ref):
        points = col_ref[pl.ds(pl.multiple_of(z * 128, 128), 128), :]
        out_ref[...] = jnp.dot(points, row_ref[...], preferred_element_type=F32)

    def spread(z, in_ref):
        for i in range(8):
            span = pl.ds(pl.multiple_of(z * 128 + i * 16, 16), 16)
            kern = matern_of(in_ref[i * 16 : i * 16 + 16, :])
            high, low = halves(kern)
            kern_ref[span, :] = high
            if low_ref is not None:
                low_ref[span, :] = low

    inner(0, even_ref)

    def step(i, _):
        if send is not None:
            pl.when(i > 0)(lambda: send(i - 1))
        inner(2 * i + 1, odd_ref)
        spread(2 * i, even_ref)
        inner(jnp.minimum(2 * i + 2, NZ - 1), even_ref)
        spread(2 * i + 1, odd_ref)
        return 0

    lax.fori_loop(0, NZ // 2, step, 0)


def finish_fill(vectors_ref, kern_ref, hbm_ref, sems):
    total = None
    for i in range(CHUNKS):
        span = slice(i * PIECE, i * PIECE + PIECE)
        part = jnp.dot(vectors_ref[:, span], kern_ref[span, :], preferred_element_type=F32)
        total = part if total is None else total + part
        if i == 0:
            pltpu.make_async_copy(*piece(kern_ref, hbm_ref, sems, CHUNKS - 1)).start()
    return total[0:16] + total[16:32]


def drain(kern_ref, hbm_ref, sems):
    for i in range(CHUNKS):
        pltpu.make_async_copy(*piece(kern_ref, hbm_ref, sems, i)).wait()


def own_block(q):
    return pl.ds(pl.multiple_of((q // 2) * 128, 128), 128)


def own_mask(q):
    lane = lax.broadcasted_iota(jnp.int32, (RHS, 128), 1)
    return (lane // 64) == (q % 2)


def position():
    return lax.axis_index("y") * 4 + lax.axis_index("x")


def first_apply(
    y_ref, col_ref, b_ref, side_ref, hbm_ref, out_ref,
    acc_ref, row_ref, even_ref, odd_ref, kern_ref, sems,
):
    q = position()
    for j in range(NQ // 2):
        row_ref[:, j * 128 : j * 128 + 128] = row_side(y_ref, j, 0)

    def send(i):
        pltpu.make_async_copy(*piece(kern_ref, hbm_ref, sems, i)).start()

    fill(col_ref, row_ref, kern_ref, even_ref, odd_ref, send)
    acc_ref[...] = finish_fill(b_ref, kern_ref, hbm_ref, sems)
    own = side_ref[:, 0:64] * side_ref[:, 64:128]
    twice = jnp.concatenate([own, own], axis=1)
    acc_ref[:, own_block(q)] += jnp.where(own_mask(q), twice, 0.0)
    image = acc_ref[...].astype(BF16)
    for i in range(NQ):
        out_ref[i] = image
    drain(kern_ref, hbm_ref, sems)


def merge_image(part_ref, y_ref, out_ref, w_ref, br_ref):
    q = position()
    total = part_ref[0].astype(F32)
    for i in range(1, NQ):
        total = total + part_ref[i].astype(F32)
    w_ref[...] = total
    for j in range(NQ // 2):
        even, odd = y_ref[2 * j, 64:80, :].astype(F32), y_ref[2 * j + 1, 64:80, :].astype(F32)
        br_ref[:, j * 128 : j * 128 + 128] = jnp.concatenate(
            [even[:, :64] + even[:, 64:], odd[:, :64] + odd[:, 64:]], axis=1
        )
    b = br_ref[...]
    bw = jnp.sum(b * total, axis=1, keepdims=True)
    bb = jnp.sum(b * b, axis=1, keepdims=True)
    block = w_ref[:, own_block(q)]
    own = jnp.where(q % 2 == 0, block[:, :64], block[:, 64:])
    lane = lax.broadcasted_iota(jnp.int32, (RHS, 64), 1)
    scalars = jnp.zeros((RHS, 64), F32)
    for i, piece in enumerate([*thirds(bw), *thirds(bb)]):
        scalars = jnp.where(lane == i, piece, scalars)
    message = jnp.concatenate([own, scalars], axis=1).astype(BF16)
    for i in range(NZ):
        out_ref[i] = message


def fetch(hbm_ref, tile_ref, sems, i):
    target, source, sem = piece(tile_ref, hbm_ref, sems, i)
    return pltpu.make_async_copy(source, target, sem)


def streamed(r_ref, hbm_ref, tile_ref, sems):
    total = None
    for i in range(CHUNKS):
        fetch(hbm_ref, tile_ref, sems, i).wait()
        span = slice(i * PIECE, i * PIECE + PIECE)
        part = jnp.dot(r_ref[:, span], tile_ref[span, :], preferred_element_type=F32)
        total = part if total is None else total + part
    return total[0:16] + total[16:32]


def second_apply(
    s_ref, b_ref, w_ref, br_ref, kern_hbm, side_ref, out_ref, r_ref, own_ref, kern_ref, sems
):
    for i in range(CHUNKS):
        fetch(kern_hbm, kern_ref, sems, i).start()
    q = position()
    sums = s_ref[0, 0, :, 64:128].astype(F32)
    for c in range(2):
        for z in range(NZ):
            if c or z:
                sums = sums + s_ref[c, z, :, 64:128].astype(F32)
    lane = lax.broadcasted_iota(jnp.int32, (RHS, 64), 1)
    bw = jnp.sum(jnp.where(lane < 3, sums, 0.0), axis=1, keepdims=True)
    bb = jnp.sum(jnp.where((lane >= 3) & (lane < 6), sums, 0.0), axis=1, keepdims=True)
    alpha = bb / bw
    for z in range(NZ):
        span = slice(z * 128, z * 128 + 128)
        w = jnp.concatenate([s_ref[0, z, :, 0:64], s_ref[1, z, :, 0:64]], axis=1).astype(F32)
        b = b_ref[0:16, span].astype(F32) + b_ref[16:32, span].astype(F32)
        high, low = halves(b - alpha * w)
        r_ref[:, span] = jnp.concatenate([high, low], axis=0)
    r_row = br_ref[...] - alpha * w_ref[...]
    block = w_ref[:, own_block(q)]
    own_w = jnp.where(q % 2 == 0, block[:, :64], block[:, 64:])
    target, noise = side_ref[:, 0:64], side_ref[:, 64:128]
    own_r = target - alpha * own_w
    t = jnp.sum(own_r * own_w, axis=1, keepdims=True)
    rr = jnp.sum(own_r * own_r, axis=1, keepdims=True)
    side = jnp.where(lane == 0, bb, jnp.where(lane == 1, bw, 0.0))
    own_ref[...] = jnp.concatenate([own_r, side], axis=1)
    applied = streamed(r_ref, kern_hbm, kern_ref, sems)
    s = jnp.sum(r_row * applied, axis=1, keepdims=True) + jnp.sum(
        noise * own_r * own_r, axis=1, keepdims=True
    )
    wide = lax.broadcasted_iota(jnp.int32, (RHS, 128), 1)
    index = lax.broadcasted_iota(jnp.int32, (RHS, 128), 0)
    spread = (
        jnp.where(wide == index, s, 0.0)
        + jnp.where(wide == index + 16, t, 0.0)
        + jnp.where(wide == index + 32, rr, 0.0)
    )
    spread = jnp.sum(spread, axis=0, keepdims=True)
    for i in range(NZ):
        out_ref[i] = spread


def cand_mean(
    y_ref, col_ref, b_ref, r_ref, out_ref, row_ref, even_ref, odd_ref, kern_ref, low_ref
):
    for j in range(NQ // 2):
        row_ref[:, j * 128 : j * 128 + 128] = row_side(y_ref, j, 64)
    fill(col_ref, row_ref, kern_ref, even_ref, odd_ref, low_ref=low_ref)
    vectors = jnp.concatenate([b_ref[...], r_ref[...]], axis=0)
    total = jnp.dot(vectors, kern_ref[...], preferred_element_type=F32) + jnp.dot(
        vectors, low_ref[...], preferred_element_type=F32
    )
    mean0, mean = total[0:16] + total[16:32], total[32:48] + total[48:64]
    for i in range(NQ):
        span = slice(i * 64, i * 64 + 64)
        out_ref[i] = jnp.concatenate([mean0[:, span], mean[:, span]], axis=1)


def pack(s_ref, mean_ref, out_ref):
    total = s_ref[0, 0]
    for c in range(2):
        for z in range(NZ):
            if c or z:
                total = total + s_ref[c, z]
    eight = lax.broadcasted_iota(jnp.int32, (8, 128), 0)
    total = jnp.where(eight == 0, total, 0.0)
    for i in range(NQ):
        out_ref[i, 0:16, :] = mean_ref[i]
        out_ref[i, 16:24, :] = total


def finish(part_ref, own_ref, side_ref, solution_ref, post_ref):
    total = part_ref[0]
    for i in range(1, NQ):
        total = total + part_ref[i]
    mean, scalars = total[0:16], total[16:17]
    s, t, rr = column(scalars, 0), column(scalars, 16), column(scalars, 32)
    own_r = own_ref[:, 0:64]
    bb, bw = own_ref[:, 64:65], own_ref[:, 65:66]
    alpha0 = bb / bw
    beta = rr / bb
    alpha1 = rr / (s + 2.0 * beta * t + beta * beta * bw)
    target = side_ref[:, 0:64]
    solution_ref[...] = alpha0 * target + alpha1 * (own_r + beta * target)
    post_ref[...] = (alpha0 + alpha1 * beta) * mean[:, :64] + alpha1 * mean[:, 64:]


def shape(*dims, dtype=F32):
    return jax.ShapeDtypeStruct(dims, dtype)


def in_hbm(array):
    return pltpu.with_memory_space_constraint(array, pltpu.HBM)


def per_device(train_points, cand_points, inv_length, noise, targets):
    def call(kernel, **options):
        return pl.pallas_call(kernel, compiler_params=PARAMS, **options)

    vmem = pl.BlockSpec(memory_space=pltpu.VMEM)
    hbm = pl.BlockSpec(memory_space=pltpu.HBM)
    whole_tile = [pltpu.VMEM((COLS, ROWS), BF16), pltpu.SemaphoreType.DMA((CHUNKS,))]
    build = [
        pltpu.VMEM((128, ROWS), BF16),
        pltpu.VMEM((128, ROWS), F32),
        pltpu.VMEM((128, ROWS), F32),
    ]
    build_cost = pl.CostEstimate(
        flops=2 * ROWS * COLS * 160, bytes_accessed=2 * ROWS * COLS, transcendentals=2 * ROWS * COLS
    )

    y_out, z_out, side = call(
        prepare,
        in_specs=[hbm] * 5,
        out_shape=(
            shape(NQ, 80, 128, dtype=BF16),
            shape(NZ, 48, 128, dtype=BF16),
            shape(RHS, 128),
        ),
        scratch_shapes=[
            pltpu.VMEM((D, S), F32),
            pltpu.VMEM((D, S), F32),
            pltpu.VMEM((1, D), F32),
            pltpu.VMEM((1, S), F32),
            pltpu.VMEM((RHS, S), F32),
            pltpu.SemaphoreType.DMA((5,)),
        ],
    )(
        in_hbm(train_points),
        in_hbm(cand_points),
        in_hbm(inv_length.reshape(1, D)),
        in_hbm(noise.reshape(1, S)),
        in_hbm(targets),
    )
    z_in = lax.all_gather(lax.all_to_all(z_out, "z", 0, 0), "c", axis=0)
    y_in = lax.all_to_all(y_out, ("y", "x"), 0, 0)
    col, b_col = call(
        col_side,
        out_shape=(shape(COLS, 128, dtype=BF16), shape(32, COLS, dtype=BF16)),
        cost_estimate=pl.CostEstimate(
            flops=COLS * 1000, bytes_accessed=4 * COLS * 128, transcendentals=0
        ),
    )(z_in)
    kern, image_out = call(
        first_apply,
        out_specs=(hbm, vmem),
        out_shape=(pltpu.HBM((COLS, ROWS), BF16), shape(NQ, RHS, ROWS, dtype=BF16)),
        scratch_shapes=[pltpu.VMEM((RHS, ROWS), F32), *build, *whole_tile],
        cost_estimate=build_cost,
    )(y_in, col, b_col, side)
    image_in = lax.all_to_all(image_out, ("y", "x"), 0, 0)
    w_out, w_row, b_row = call(
        merge_image,
        out_shape=(shape(NZ, RHS, 128, dtype=BF16), shape(RHS, ROWS), shape(RHS, ROWS)),
    )(image_in, y_in)
    w_in = lax.all_gather(lax.all_to_all(w_out, "z", 0, 0), "c", axis=0)
    scalar_out, r_col, own = call(
        second_apply,
        in_specs=[vmem] * 4 + [hbm, vmem],
        out_shape=(shape(NZ, 1, 128), shape(32, COLS, dtype=BF16), shape(RHS, 128)),
        scratch_shapes=whole_tile,
    )(w_in, b_col, w_row, b_row, in_hbm(kern), side)
    scalar_in = lax.all_gather(lax.all_to_all(scalar_out, "z", 0, 0), "c", axis=0)
    mean_part = call(
        cand_mean,
        out_shape=shape(NQ, RHS, 128),
        scratch_shapes=[*build, *[pltpu.VMEM((COLS, ROWS), BF16)] * 2],
        cost_estimate=build_cost,
    )(y_in, col, b_col, r_col)
    mean_out = call(pack, out_shape=shape(NQ, 24, 128))(scalar_in, mean_part)
    mean_in = lax.all_to_all(mean_out, ("y", "x"), 0, 0)
    return call(finish, out_shape=(shape(RHS, S), shape(RHS, S)))(mean_in, own, side)


def solution(mesh):
    fine = Mesh(mesh.devices.reshape(16, 2, 4, 4), ("z", "c", "y", "x"))
    every = ("z", "c", "y", "x")
    wide = P(None, every)
    return jax.shard_map(
        per_device,
        mesh=fine,
        in_specs=(wide, wide, P(), P(every), wide),
        out_specs=(wide, wide),
        check_vma=False,
    )
```

time: 139 us -> 123 us (0.88)
  Pallas kernels: 25.7 us -> 19.8 us
  local copies, waits for them, and re-layouts: 5.18 us -> 0 us
  blocking collectives: 90.2 us -> 86.9 us
  starting transfers between devices: 12.2 us -> 10.2 us
    pallas_call x8, Pallas kernels: 25.7 us -> 19.8 us  [the longest x1 7.09 us: per_device(): call(cand_mean, out_shape=shape(NQ, RHS, 128), scratch_shapes=[*build, *[...]
    unnamed x16 -> x0, local copies, waits for them, and re-layouts: 5.18 us -> none
    all_to_all x1, starting transfers between devices: 5.43 us -> 3.48 us  [per_device(): lax.all_to_all(scalar_out, 'z', 0, 0)]
    all_to_all x1, blocking collectives: 16.8 us -> 15.1 us  [per_device(): image_in = lax.all_to_all(image_out, ('y', 'x'), 0, 0)]
  transfers between devices with their start and end apart: 2 -> 2, of which waited for: 1 -> 2; matrix products, arithmetic and copies ran while one was open for 0% -> 0% of each run, Pallas kernels for 6% -> 6%
where the time goes in v3:
time: 123 us; the launch traced here: 122 us
  blocking collectives  86.9 us (71%)
  Pallas kernels  19.8 us (16%)
  starting transfers between devices  10.2 us (8%)
  waiting for transfers between devices  4.64 us (4%)
    all_to_all x1, blocking collectives, per_device(): z_in = lax.all_gather(lax.all_to_all(z_out, 'z', 0, 0), 'c', axis=0)  28 us
    all_to_all x1, blocking collectives, per_device(): w_in = lax.all_gather(lax.all_to_all(w_out, 'z', 0, 0), 'c', axis=0)  18.5 us
    all_to_all x1, blocking collectives, per_device(): image_in = lax.all_to_all(image_out, ('y', 'x'), 0, 0)  15.1 us
    all_to_all x1, blocking collectives, per_device(): mean_in = lax.all_to_all(mean_out, ('y', 'x'), 0, 0)  9.83 us
    pallas_call x1, Pallas kernels, per_device(): call(cand_mean, out_shape=shape(NQ, RHS, 128), scratch_shapes=[*build, *[...  7.09 us
    all_gather x1, blocking collectives, per_device(): z_in = lax.all_gather(lax.all_to_all(z_out, 'z', 0, 0), 'c', axis=0)  6.83 us
    all_to_all x1, starting transfers between devices, per_device(): y_in = lax.all_to_all(y_out, ('y', 'x'), 0, 0)  6.76 us
    pallas_call x1, Pallas kernels, per_device(): call(first_apply, out_specs=(hbm, vmem), out_shape=(pltpu.HBM((COLS, ROWS...  6.06 us
  transfers between devices with their start and end apart: 2, of which 2 were waited for; matrix products, arithmetic and copies ran while one was open for 0% of the time, Pallas kernels for 6%

profile of v3, /device:TPU:1, one launch (start us, length us, event | category | flops | bytes accessed | tf_op | source)
XLA Modules:
  0.0 122.3 jit_solution(12022310062752878402)
XLA Ops:
  0.6 1.8 %shard_map.68 = (bf16[16,80,128]{2,1,0:T(8,128)(2,1)}, bf16[16,48,128]{2,1,0:T(8,128)(2,1)S(1)}, f32[16,128]{1,0:T(8,128)S(1)}) custom-call(f32[64,64]{1,0:T(8,128)} %train_hbm.1, f32[64,64]{1,0:T(8,128)} %cand_hbm.1, f32[1,64]{1,0:T(1,128)} %bitcast.8, f32[1,64]{1,0:T(1,128)} %bitcast.9, f32[16,64]{1,0:T(8,128)} %target_hbm.1), custom_call_target="tpu_custom_call" | custom-call | tf_op jit(solution)/shard_map/pallas_call | solution.py:366
  2.4 28.0 %all_to_all.30 = bf16[16,48,128]{2,1,0:T(8,128)(2,1)S(1)} all-to-all(bf16[16,48,128]{2,1,0:T(8,128)(2,1)S(1)} %get-tuple-element.16), channel_id=1, replica_groups=mesh['z'=16,'c'=2,'y'=4,'x'=4] {'z'}, dimensions={0} | all-to-all | bytes 393216 | tf_op jit(solution)/shard_map/all_to_all | solution.py:389
  30.4 6.8 %all-to-all-start = ((bf16[16,80,128]{2,1,0:T(8,128)(2,1)}), bf16[16,80,128]{2,1,0:T(8,128)(2,1)S(1)}, u32[]{:S(2)}, u32[]{:S(2)}) async-start(bf16[16,80,128]{2,1,0:T(8,128)(2,1)} %get-tuple-element.15), calls=%async_computation | async-start | bytes 655360 | tf_op jit(solution)/shard_map/all_to_all | solution.py:390
  37.2 6.8 %all-gather = bf16[32,48,128]{2,1,0:T(8,128)(2,1)S(1)} all-gather(bf16[16,48,128]{2,1,0:T(8,128)(2,1)S(1)} %all_to_all.30), channel_id=2, replica_groups=mesh['z'=16,'c'=2,'y'=4,'x'=4] {'c'}, dimensions={0}, use_global_device_ids=true | all-gather | bytes 589824 | tf_op jit(solution)/shard_map/all_gather | solution.py:389
  44.0 0.5 shard_map.69
  44.5 0.6 all-to-all-done.y_ref
  45.1 6.1 %shard_map.70 = (bf16[2048,1024]{1,0:T(8,128)(2,1)}, bf16[16,16,1024]{2,1,0:T(8,128)(2,1)S(1)}) custom-call(bf16[16,80,128]{2,1,0:T(8,128)(2,1)S(1)} %all-to-all-done.y_ref, bf16[2048,128]{1,0:T(8,128)(2,1)S(1)} %get-tuple-element.17.col_ref, bf16[32,2048]{1,0:T(8,128)(2,1)S(1)} %get-tuple-element.18.b_ref, f32[16,128]{1,0:T(8,128)S(1)} %get-tuple-element.19.side_ref), custom_call_target="tpu_custom_call" | custom-call | flops 671088640 | bytes 4194304 | tf_op jit(solution)/shard_map/pallas_call | solution.py:398
  51.2 15.1 %all_to_all.31.part_ref = bf16[16,16,1024]{2,1,0:T(8,128)(2,1)S(1)} all-to-all(bf16[16,16,1024]{2,1,0:T(8,128)(2,1)S(1)} %get-tuple-element.20), channel_id=1, replica_groups=mesh['z'=16,'c'=2,'y'=4,'x'=4] {'y','x'}, dimensions={0} | all-to-all | bytes 1048576 | tf_op jit(solution)/shard_map/all_to_all | solution.py:405
  66.3 0.3 shard_map.71
  66.6 18.5 %all_to_all.32 = bf16[16,16,128]{2,1,0:T(8,128)(2,1)S(1)} all-to-all(bf16[16,16,128]{2,1,0:T(8,128)(2,1)S(1)} %get-tuple-element.21), channel_id=1, replica_groups=mesh['z'=16,'c'=2,'y'=4,'x'=4] {'z'}, dimensions={0} | all-to-all | bytes 131072 | tf_op jit(solution)/shard_map/all_to_all | solution.py:410
  85.1 5.7 %all-gather.1 = bf16[32,16,128]{2,1,0:T(8,128)(2,1)S(1)} all-gather(bf16[16,16,128]{2,1,0:T(8,128)(2,1)S(1)} %all_to_all.32), channel_id=3, replica_groups=mesh['z'=16,'c'=2,'y'=4,'x'=4] {'c'}, dimensions={0}, use_global_device_ids=true | all-gather | bytes 196608 | tf_op jit(solution)/shard_map/all_gather | solution.py:410
  90.8 3.2 %shard_map.72 = (f32[16,1,128]{2,1,0:T(1,128)}, bf16[32,2048]{1,0:T(8,128)(2,1)S(1)}, f32[16,128]{1,0:T(8,128)S(1)}) custom-call(bf16[2,16,16,128]{3,2,1,0:T(8,128)(2,1)S(1)} %bitcast.6, bf16[32,2048]{1,0:T(8,128)(2,1)S(1)} %get-tuple-element.18.b_ref, f32[16,1024]{1,0:T(8,128)S(1)} %get-tuple-element.22.w_ref, f32[16,1024]{1,0:T(8,128)S(1)} %get-tuple-element.23.br_ref, ...), custom_call_target="tpu_custom_call" | custom-call | tf_op jit(solution)/shard_map/pallas_call | solution.py:411
  94.0 3.5 %all-to-all-start.4 = ((f32[16,1,128]{2,1,0:T(1,128)}), f32[16,1,128]{2,1,0:T(1,128)S(1)}, u32[]{:S(2)}, u32[]{:S(2)}) async-start(f32[16,1,128]{2,1,0:T(1,128)} %get-tuple-element.25), calls=%async_computation.4 | async-start | bytes 16384 | tf_op jit(solution)/shard_map/all_to_all | solution.py:417
  97.5 7.1 %shard_map.73.mean_ref = f32[16,16,128]{2,1,0:T(8,128)S(1)} custom-call(bf16[16,80,128]{2,1,0:T(8,128)(2,1)S(1)} %all-to-all-done.y_ref, bf16[2048,128]{1,0:T(8,128)(2,1)S(1)} %get-tuple-element.17.col_ref, bf16[32,2048]{1,0:T(8,128)(2,1)S(1)} %get-tuple-element.18.b_ref, bf16[32,2048]{1,0:T(8,128)(2,1)S(1)} %get-tuple-element.26.r_ref), custom_call_target="tpu_custom_call" | custom-call | flops 671088640 | bytes 4194304 | tf_op jit(solution)/shard_map/pallas_call | solution.py:418
  104.6 4.1 %all-to-all-done.4 = f32[16,1,128]{2,1,0:T(1,128)S(1)} async-done(((f32[16,1,128]{2,1,0:T(1,128)}), f32[16,1,128]{2,1,0:T(1,128)S(1)}, u32[]{:S(2)}, u32[]{:S(2)}) %all-to-all-start.4) | async-done | bytes 8224 | tf_op jit(solution)/shard_map/all_to_all | solution.py:417
  108.7 2.9 %all-gather.2 = f32[32,1,128]{2,1,0:T(1,128)S(1)} all-gather(f32[16,1,128]{2,1,0:T(1,128)S(1)} %all-to-all-done.4), channel_id=4, replica_groups=mesh['z'=16,'c'=2,'y'=4,'x'=4] {'c'}, dimensions={0}, use_global_device_ids=true | all-gather | bytes 24576 | tf_op jit(solution)/shard_map/all_gather | solution.py:417
  111.6 9.8 %all_to_all.33.part_ref = f32[16,24,128]{2,1,0:T(8,128)S(1)} all-to-all(f32[16,24,128]{2,1,0:T(8,128)S(1)} %shard_map.74), channel_id=1, replica_groups=mesh['z'=16,'c'=2,'y'=4,'x'=4] {'y','x'}, dimensions={0} | all-to-all | bytes 393216 | tf_op jit(solution)/shard_map/all_to_all | solution.py:425
  121.4 0.9 shard_map.75
  (1 shorter events, 0.0 us)
Async XLA Ops:
  30.4 14.7 %all-to-all-start = ((bf16[16,80,128]{2,1,0:T(8,128)(2,1)}), bf16[16,80,128]{2,1,0:T(8,128)(2,1)S(1)}, u32[]{:S(2)}, u32[]{:S(2)}) async-start(bf16[16,80,128]{2,1,0:T(8,128)(2,1)} %get-tuple-element.15), calls=%async_computation | async-start | bytes 655360 | tf_op jit(solution)/shard_map/all_to_all | solution.py:390
  94.0 14.7 %all-to-all-start.4 = ((f32[16,1,128]{2,1,0:T(1,128)}), f32[16,1,128]{2,1,0:T(1,128)S(1)}, u32[]{:S(2)}, u32[]{:S(2)}) async-start(f32[16,1,128]{2,1,0:T(1,128)} %get-tuple-element.25), calls=%async_computation.4 | async-start | bytes 16384 | tf_op jit(solution)/shard_map/all_to_all | solution.py:417

commit v4 on v3

--- a/solution.py
+++ b/solution.py
@@ -20,6 +20,7 @@
 LOG2E = math.log2(math.e)
 CHUNKS = 8
 PIECE = COLS // CHUNKS
+KEPT = 2
 PARAMS = pltpu.CompilerParams(vmem_limit_bytes=24 * 1024 * 1024)
 
 
@@ -50,44 +51,51 @@
     return jnp.sum(jnp.where(lane == index + start, row, 0.0), axis=1, keepdims=True)
 
 
-def prepare(
-    train_hbm, cand_hbm, inv_hbm, noise_hbm, target_hbm, y_ref, z_ref, side_ref,
-    train_ref, cand_ref, inv_ref, noise_ref, target_ref, sems,
-):
+def load(pairs, sems):
     copies = [
         pltpu.make_async_copy(source, target, sems.at[i])
-        for i, (source, target) in enumerate(
-            [
-                (train_hbm, train_ref),
-                (inv_hbm, inv_ref),
-                (target_hbm, target_ref),
-                (cand_hbm, cand_ref),
-                (noise_hbm, noise_ref),
-            ]
-        )
+        for i, (source, target) in enumerate(pairs)
     ]
     for copy in copies:
         copy.start()
     for copy in copies:
         copy.wait()
+
+
+def scale_column(inv_ref):
     eye = lax.broadcasted_iota(jnp.int32, (D, D), 0) == lax.broadcasted_iota(
         jnp.int32, (D, D), 1
     )
-    inv = jnp.sum(jnp.where(eye, inv_ref[...], 0.0), axis=1, keepdims=True)
-    train = train_ref[...] * inv
-    cand = cand_ref[...] * inv
-    target = target_ref[...]
-    b_high, b_low = halves(target)
-    b = jnp.concatenate([b_high, b_low], axis=1)
-    both = jnp.concatenate([train.astype(BF16), cand.astype(BF16)], axis=1)
+    return jnp.sum(jnp.where(eye, inv_ref[...], 0.0), axis=1, keepdims=True)
+
+
+def prepare_z(
+    train_hbm, inv_hbm, target_hbm, z_ref, scaled_ref, inv_ref, b_ref, train_ref, target_ref, sems
+):
+    load([(train_hbm, train_ref), (inv_hbm, inv_ref), (target_hbm, target_ref)], sems)
+    train = train_ref[...] * scale_column(inv_ref)
+    scaled_ref[...] = train.astype(BF16)
+    b = jnp.concatenate(halves(target_ref[...]), axis=1)
+    b_ref[...] = b
     folded = jnp.concatenate([train[:32].astype(BF16), train[32:].astype(BF16)], axis=1)
-    for i in range(NQ):
+    for i in range(NZ):
         z_ref[i, 0:32, :] = folded
         z_ref[i, 32:48, :] = b
+
+
+def prepare_y(
+    cand_hbm, noise_hbm, target_hbm, scaled_ref, inv_ref, b_ref, y_ref, side_ref,
+    cand_ref, noise_ref, target_ref, sems,
+):
+    load([(cand_hbm, cand_ref), (noise_hbm, noise_ref), (target_hbm, target_ref)], sems)
+    cand = (cand_ref[...] * scale_column(inv_ref)).astype(BF16)
+    both = jnp.concatenate([scaled_ref[...], cand], axis=1)
+    b = b_ref[...]
+    for i in range(NQ):
         y_ref[i, 0:64, :] = both
         y_ref[i, 64:80, :] = b
     side_ref[...] = jnp.concatenate(
-        [target, jnp.broadcast_to(noise_ref[...], (RHS, S))], axis=1
+        [target_ref[...], jnp.broadcast_to(noise_ref[...], (RHS, S))], axis=1
     )
 
 
@@ -129,7 +137,7 @@
     return tile_ref.at[span, :], hbm_ref.at[span, :], sems.at[i]
 
 
-def fill(col_ref, row_ref, kern_ref, even_ref, odd_ref, send=None, low_ref=None):
+def fill(col_ref, row_ref, kern_ref, even_ref, odd_ref, send, stored, low_ref=None):
     def inner(z, out_ref):
         points = col_ref[pl.ds(pl.multiple_of(z * 128, 128), 128), :]
         out_ref[...] = jnp.dot(points, row_ref[...], preferred_element_type=F32)
@@ -146,8 +154,7 @@
     inner(0, even_ref)
 
     def step(i, _):
-        if send is not None:
-            pl.when(i > 0)(lambda: send(i - 1))
+        pl.when((i > 0) & (i <= stored))(lambda: send(i - 1))
         inner(2 * i + 1, odd_ref)
         spread(2 * i, even_ref)
         inner(jnp.minimum(2 * i + 2, NZ - 1), even_ref)
@@ -157,19 +164,15 @@
     lax.fori_loop(0, NZ // 2, step, 0)
 
 
-def finish_fill(vectors_ref, kern_ref, hbm_ref, sems):
-    total = None
-    for i in range(CHUNKS):
-        span = slice(i * PIECE, i * PIECE + PIECE)
-        part = jnp.dot(vectors_ref[:, span], kern_ref[span, :], preferred_element_type=F32)
-        total = part if total is None else total + part
-        if i == 0:
-            pltpu.make_async_copy(*piece(kern_ref, hbm_ref, sems, CHUNKS - 1)).start()
-    return total[0:16] + total[16:32]
-
-
-def drain(kern_ref, hbm_ref, sems):
-    for i in range(CHUNKS):
+def sender(kern_ref, hbm_ref, sems):
+    def send(i):
+        pltpu.make_async_copy(*piece(kern_ref, hbm_ref, sems, i)).start()
+
+    return send
+
+
+def drain(kern_ref, hbm_ref, sems, stored):
+    for i in range(stored):
         pltpu.make_async_copy(*piece(kern_ref, hbm_ref, sems, i)).wait()
 
 
@@ -187,25 +190,39 @@
 
 
 def first_apply(
-    y_ref, col_ref, b_ref, side_ref, hbm_ref, out_ref,
+    y_ref, col_ref, b_ref, side_ref, hbm_ref, kept_ref, out_ref,
     acc_ref, row_ref, even_ref, odd_ref, kern_ref, sems,
 ):
     q = position()
+    stored = CHUNKS - KEPT
     for j in range(NQ // 2):
         row_ref[:, j * 128 : j * 128 + 128] = row_side(y_ref, j, 0)
-
-    def send(i):
-        pltpu.make_async_copy(*piece(kern_ref, hbm_ref, sems, i)).start()
-
-    fill(col_ref, row_ref, kern_ref, even_ref, odd_ref, send)
-    acc_ref[...] = finish_fill(b_ref, kern_ref, hbm_ref, sems)
+    send = sender(kern_ref, hbm_ref, sems)
+    fill(col_ref, row_ref, kern_ref, even_ref, odd_ref, send, stored)
+    total = jnp.dot(b_ref[...], kern_ref[...], preferred_element_type=F32)
+    acc_ref[...] = total[0:16] + total[16:32]
+    kept_ref[...] = kern_ref[stored * PIECE :, :]
     own = side_ref[:, 0:64] * side_ref[:, 64:128]
     twice = jnp.concatenate([own, own], axis=1)
     acc_ref[:, own_block(q)] += jnp.where(own_mask(q), twice, 0.0)
     image = acc_ref[...].astype(BF16)
     for i in range(NQ):
         out_ref[i] = image
-    drain(kern_ref, hbm_ref, sems)
+    drain(kern_ref, hbm_ref, sems, stored)
+
+
+def cand_apply(
+    y_ref, col_ref, b_ref, hbm_ref, mean_ref, row_ref, even_ref, odd_ref, low_ref, kern_ref, sems
+):
+    for j in range(NQ // 2):
+        row_ref[:, j * 128 : j * 128 + 128] = row_side(y_ref, j, 64)
+    send = sender(kern_ref, hbm_ref, sems)
+    fill(col_ref, row_ref, kern_ref, even_ref, odd_ref, send, CHUNKS, low_ref)
+    total = jnp.dot(b_ref[...], low_ref[...], preferred_element_type=F32)
+    send(CHUNKS - 1)
+    total = total + jnp.dot(b_ref[...], kern_ref[...], preferred_element_type=F32)
+    mean_ref[...] = total[0:16] + total[16:32]
+    drain(kern_ref, hbm_ref, sems, CHUNKS)
 
 
 def merge_image(part_ref, y_ref, out_ref, w_ref, br_ref):
@@ -238,20 +255,23 @@
     return pltpu.make_async_copy(source, target, sem)
 
 
-def streamed(r_ref, hbm_ref, tile_ref, sems):
-    total = None
-    for i in range(CHUNKS):
+def streamed(r_ref, hbm_ref, tile_ref, sems, stored, kept_ref=None):
+    total = jnp.zeros((32, ROWS), F32)
+    if kept_ref is not None:
+        total = jnp.dot(r_ref[:, stored * PIECE :], kept_ref[...], preferred_element_type=F32)
+    for i in range(stored):
         fetch(hbm_ref, tile_ref, sems, i).wait()
         span = slice(i * PIECE, i * PIECE + PIECE)
-        part = jnp.dot(r_ref[:, span], tile_ref[span, :], preferred_element_type=F32)
-        total = part if total is None else total + part
+        total = total + jnp.dot(r_ref[:, span], tile_ref[span, :], preferred_element_type=F32)
     return total[0:16] + total[16:32]
 
 
 def second_apply(
-    s_ref, b_ref, w_ref, br_ref, kern_hbm, side_ref, out_ref, r_ref, own_ref, kern_ref, sems
+    s_ref, b_ref, w_ref, br_ref, kern_hbm, kept_ref, side_ref, mean_ref,
+    out_ref, r_ref, own_ref, kern_ref, sems,
 ):
-    for i in range(CHUNKS):
+    stored = CHUNKS - KEPT
+    for i in range(stored):
         fetch(kern_hbm, kern_ref, sems, i).start()
     q = position()
     sums = s_ref[0, 0, :, 64:128].astype(F32)
@@ -278,7 +298,7 @@
     rr = jnp.sum(own_r * own_r, axis=1, keepdims=True)
     side = jnp.where(lane == 0, bb, jnp.where(lane == 1, bw, 0.0))
     own_ref[...] = jnp.concatenate([own_r, side], axis=1)
-    applied = streamed(r_ref, kern_hbm, kern_ref, sems)
+    applied = streamed(r_ref, kern_hbm, kern_ref, sems, stored, kept_ref)
     s = jnp.sum(r_row * applied, axis=1, keepdims=True) + jnp.sum(
         noise * own_r * own_r, axis=1, keepdims=True
     )
@@ -290,32 +310,24 @@
         + jnp.where(wide == index + 32, rr, 0.0)
     )
     spread = jnp.sum(spread, axis=0, keepdims=True)
-    for i in range(NZ):
+    for i in range(2 * NZ):
         out_ref[i] = spread
 
 
-def cand_mean(
-    y_ref, col_ref, b_ref, r_ref, out_ref, row_ref, even_ref, odd_ref, kern_ref, low_ref
-):
-    for j in range(NQ // 2):
-        row_ref[:, j * 128 : j * 128 + 128] = row_side(y_ref, j, 64)
-    fill(col_ref, row_ref, kern_ref, even_ref, odd_ref, low_ref=low_ref)
-    vectors = jnp.concatenate([b_ref[...], r_ref[...]], axis=0)
-    total = jnp.dot(vectors, kern_ref[...], preferred_element_type=F32) + jnp.dot(
-        vectors, low_ref[...], preferred_element_type=F32
-    )
-    mean0, mean = total[0:16] + total[16:32], total[32:48] + total[48:64]
+def cand_mean(r_ref, cand_hbm, mean_ref, out_ref, cand_ref, sems):
+    for i in range(CHUNKS):
+        fetch(cand_hbm, cand_ref, sems, i).start()
+    mean0 = mean_ref[...]
+    mean = streamed(r_ref, cand_hbm, cand_ref, sems, CHUNKS)
     for i in range(NQ):
         span = slice(i * 64, i * 64 + 64)
         out_ref[i] = jnp.concatenate([mean0[:, span], mean[:, span]], axis=1)
 
 
 def pack(s_ref, mean_ref, out_ref):
-    total = s_ref[0, 0]
-    for c in range(2):
-        for z in range(NZ):
-            if c or z:
-                total = total + s_ref[c, z]
+    total = s_ref[0]
+    for i in range(1, 2 * NZ):
+        total = total + s_ref[i]
     eight = lax.broadcasted_iota(jnp.int32, (8, 128), 0)
     total = jnp.where(eight == 0, total, 0.0)
     for i in range(NQ):
@@ -363,30 +375,30 @@
         flops=2 * ROWS * COLS * 160, bytes_accessed=2 * ROWS * COLS, transcendentals=2 * ROWS * COLS
     )
 
-    y_out, z_out, side = call(
-        prepare,
-        in_specs=[hbm] * 5,
+    points = pltpu.VMEM((D, S), F32)
+    row = pltpu.VMEM((1, S), F32)
+    rows = pltpu.VMEM((RHS, S), F32)
+    three = pltpu.SemaphoreType.DMA((3,))
+    inv_length, noise = inv_length.reshape(1, D), noise.reshape(1, S)
+    z_out, scaled, inv, b = call(
+        prepare_z,
+        in_specs=[hbm] * 3,
         out_shape=(
-            shape(NQ, 80, 128, dtype=BF16),
             shape(NZ, 48, 128, dtype=BF16),
-            shape(RHS, 128),
+            shape(D, S, dtype=BF16),
+            shape(1, D),
+            shape(RHS, 128, dtype=BF16),
         ),
-        scratch_shapes=[
-            pltpu.VMEM((D, S), F32),
-            pltpu.VMEM((D, S), F32),
-            pltpu.VMEM((1, D), F32),
-            pltpu.VMEM((1, S), F32),
-            pltpu.VMEM((RHS, S), F32),
-            pltpu.SemaphoreType.DMA((5,)),
-        ],
-    )(
-        in_hbm(train_points),
-        in_hbm(cand_points),
-        in_hbm(inv_length.reshape(1, D)),
-        in_hbm(noise.reshape(1, S)),
-        in_hbm(targets),
-    )
+        scratch_shapes=[points, rows, three],
+    )(in_hbm(train_points), in_hbm(inv_length), in_hbm(targets))
     z_in = lax.all_gather(lax.all_to_all(z_out, "z", 0, 0), "c", axis=0)
+    y_out, side = call(
+        prepare_y,
+        in_specs=[hbm] * 3 + [vmem] * 3,
+        out_shape=(shape(NQ, 80, 128, dtype=BF16), shape(RHS, 128)),
+        scratch_shapes=[points, row, rows, three],
+        cost_estimate=pl.CostEstimate(flops=100000, bytes_accessed=500000, transcendentals=0),
+    )(in_hbm(cand_points), in_hbm(noise), in_hbm(targets), scaled, inv, b)
     y_in = lax.all_to_all(y_out, ("y", "x"), 0, 0)
     col, b_col = call(
         col_side,
@@ -395,14 +407,26 @@
             flops=COLS * 1000, bytes_accessed=4 * COLS * 128, transcendentals=0
         ),
     )(z_in)
-    kern, image_out = call(
+    stored = (CHUNKS - KEPT) * PIECE
+    kern, kept, image_out = call(
         first_apply,
-        out_specs=(hbm, vmem),
-        out_shape=(pltpu.HBM((COLS, ROWS), BF16), shape(NQ, RHS, ROWS, dtype=BF16)),
+        out_specs=(hbm, vmem, vmem),
+        out_shape=(
+            pltpu.HBM((stored, ROWS), BF16),
+            shape(COLS - stored, ROWS, dtype=BF16),
+            shape(NQ, RHS, ROWS, dtype=BF16),
+        ),
         scratch_shapes=[pltpu.VMEM((RHS, ROWS), F32), *build, *whole_tile],
         cost_estimate=build_cost,
     )(y_in, col, b_col, side)
     image_in = lax.all_to_all(image_out, ("y", "x"), 0, 0)
+    kern_cand, mean0 = call(
+        cand_apply,
+        out_specs=(hbm, vmem),
+        out_shape=(pltpu.HBM((COLS, ROWS), BF16), shape(RHS, ROWS)),
+        scratch_shapes=[*build, pltpu.VMEM((COLS, ROWS), BF16), *whole_tile],
+        cost_estimate=build_cost,
+    )(y_in, col, b_col)
     w_out, w_row, b_row = call(
         merge_image,
         out_shape=(shape(NZ, RHS, 128, dtype=BF16), shape(RHS, ROWS), shape(RHS, ROWS)),
@@ -410,17 +434,20 @@
     w_in = lax.all_gather(lax.all_to_all(w_out, "z", 0, 0), "c", axis=0)
     scalar_out, r_col, own = call(
         second_apply,
-        in_specs=[vmem] * 4 + [hbm, vmem],
-        out_shape=(shape(NZ, 1, 128), shape(32, COLS, dtype=BF16), shape(RHS, 128)),
-        scratch_shapes=whole_tile,
-    )(w_in, b_col, w_row, b_row, in_hbm(kern), side)
-    scalar_in = lax.all_gather(lax.all_to_all(scalar_out, "z", 0, 0), "c", axis=0)
+        in_specs=[vmem] * 4 + [hbm] + [vmem] * 3,
+        out_shape=(shape(2 * NZ, 1, 128), shape(32, COLS, dtype=BF16), shape(RHS, 128)),
+        scratch_shapes=[pltpu.VMEM((stored, ROWS), BF16), pltpu.SemaphoreType.DMA((CHUNKS,))],
+    )(w_in, b_col, w_row, b_row, in_hbm(kern), kept, side, mean0)
+    scalar_in = lax.all_to_all(scalar_out, ("z", "c"), 0, 0)
     mean_part = call(
         cand_mean,
+        in_specs=[vmem, hbm, vmem],
         out_shape=shape(NQ, RHS, 128),
-        scratch_shapes=[*build, *[pltpu.VMEM((COLS, ROWS), BF16)] * 2],
-        cost_estimate=build_cost,
-    )(y_in, col, b_col, r_col)
+        scratch_shapes=whole_tile,
+        cost_estimate=pl.CostEstimate(
+            flops=2 * ROWS * COLS * 32, bytes_accessed=2 * ROWS * COLS, transcendentals=0
+        ),
+    )(r_col, in_hbm(kern_cand), mean0)
     mean_out = call(pack, out_shape=shape(NQ, 24, 128))(scalar_in, mean_part)
     mean_in = lax.all_to_all(mean_out, ("y", "x"), 0, 0)
     return call(finish, out_shape=(shape(RHS, S), shape(RHS, S)))(mean_in, own, side)

time: 123 us -> 124 us (level)
  blocking collectives: 86.9 us -> 37.6 us
  starting transfers between devices: 10.2 us -> 36.5 us
  waiting for transfers between devices: 4.64 us -> 25 us
  Pallas kernels: 19.8 us -> 23.7 us
    all_to_all x2 -> x0, blocking collectives: 46.5 us -> none  [the longest x1 28 us: per_device(): z_in = lax.all_gather(lax.all_to_all(z_out, 'z', 0, 0), 'c', axis=0)]
    all_to_all x1 -> x3, starting transfers between devices: 3.48 us -> 29.7 us  [the longest x1 15.7 us: per_device(): z_in = lax.all_gather(lax.all_to_all(z_out, 'z', 0, 0), 'c', axis=0)]
    all_to_all x1 -> x3, waiting for transfers between devices: 4.06 us -> 24.5 us  [the longest x1 10.8 us: per_device(): z_in = lax.all_gather(lax.all_to_all(z_out, 'z', 0, 0), 'c', axis=0)]
    pallas_call x4 -> x6, Pallas kernels: 18.1 us -> 21.4 us  [the longest x1 7.19 us: per_device(): call(cand_apply, out_specs=(hbm, vmem), out_shape=(pltpu.HBM((COLS, ROWS)...]
    all_gather x1 -> x0, blocking collectives: 2.92 us -> none  [per_device(): lax.all_gather(lax.all_to_all(scalar_out, 'z', 0, 0), 'c', axis=0)]
  transfers between devices with their start and end apart: 2 -> 4, of which waited for: 2 -> 4; matrix products, arithmetic and copies ran while one was open for 0% -> 0% of each run, Pallas kernels for 6% -> 10%
where the time goes in v4:
time: 124 us; the launch traced here: 123 us
  blocking collectives  37.6 us (30%)
  starting transfers between devices  36.5 us (29%)
  waiting for transfers between devices  25 us (20%)
  Pallas kernels  23.7 us (19%)
    all_to_all x1, starting transfers between devices, per_device(): z_in = lax.all_gather(lax.all_to_all(z_out, 'z', 0, 0), 'c', axis=0)  15.7 us
    all_to_all x1, blocking collectives, per_device(): image_in = lax.all_to_all(image_out, ('y', 'x'), 0, 0)  15.2 us
    all_to_all x1, waiting for transfers between devices, per_device(): z_in = lax.all_gather(lax.all_to_all(z_out, 'z', 0, 0), 'c', axis=0)  10.8 us
    all_to_all x1, blocking collectives, per_device(): mean_in = lax.all_to_all(mean_out, ('y', 'x'), 0, 0)  9.91 us
    all_to_all x1, waiting for transfers between devices, per_device(): scalar_in = lax.all_to_all(scalar_out, ('z', 'c'), 0, 0)  9.3 us
    pallas_call x1, Pallas kernels, per_device(): call(cand_apply, out_specs=(hbm, vmem), out_shape=(pltpu.HBM((COLS, ROWS)...  7.19 us
    all_to_all x1, starting transfers between devices, per_device(): w_in = lax.all_gather(lax.all_to_all(w_out, 'z', 0, 0), 'c', axis=0)  7.17 us
    all_gather x1, blocking collectives, per_device(): z_in = lax.all_gather(lax.all_to_all(z_out, 'z', 0, 0), 'c', axis=0)  6.83 us
  transfers between devices with their start and end apart: 4, of which 4 were waited for; matrix products, arithmetic and copies ran while one was open for 0% of the time, Pallas kernels for 10%

profile of v4, /device:TPU:1, one launch (start us, length us, event | category | flops | bytes accessed | tf_op | source)
XLA Modules:
  0.0 123.5 jit_solution(13478702626272348702)
XLA Ops:
  0.6 1.6 %shard_map.68 = (bf16[16,48,128]{2,1,0:T(8,128)(2,1)}, bf16[64,64]{1,0:T(8,128)(2,1)S(1)}, f32[1,64]{1,0:T(1,128)S(1)}, bf16[16,128]{1,0:T(8,128)(2,1)S(1)}) custom-call(f32[64,64]{1,0:T(8,128)} %train_hbm.1, f32[1,64]{1,0:T(1,128)} %bitcast.7, f32[16,64]{1,0:T(8,128)} %target_hbm.3), custom_call_target="tpu_custom_call" | custom-call | tf_op jit(solution)/shard_map/pallas_call | solution.py:383
  2.3 15.7 %all-to-all-start.1 = ((bf16[16,48,128]{2,1,0:T(8,128)(2,1)}), bf16[16,48,128]{2,1,0:T(8,128)(2,1)S(1)}, u32[]{:S(2)}, u32[]{:S(2)}) async-start(bf16[16,48,128]{2,1,0:T(8,128)(2,1)} %get-tuple-element.25), calls=%async_computation.1 | async-start | bytes 393216 | tf_op jit(solution)/shard_map/all_to_all | solution.py:394
  18.0 1.7 %shard_map.69 = (bf16[16,80,128]{2,1,0:T(8,128)(2,1)}, f32[16,128]{1,0:T(8,128)S(1)}) custom-call(f32[64,64]{1,0:T(8,128)} %cand_hbm.1, f32[1,64]{1,0:T(1,128)} %bitcast.6, f32[16,64]{1,0:T(8,128)} %target_hbm.3, bf16[64,64]{1,0:T(8,128)(2,1)S(1)} %get-tuple-element.21.scaled_ref, f32[1,64]{1,0:T(1,128)S(1)} %get-tuple-element.22.inv_ref, ...), custom_call_target="tpu_custom_call" | custom-call | flops 100000 | bytes 500000 | tf_op jit(solution)/shard_map/pallas_call | solution.py:395
  19.7 10.8 %all-to-all-done.1 = bf16[16,48,128]{2,1,0:T(8,128)(2,1)S(1)} async-done(((bf16[16,48,128]{2,1,0:T(8,128)(2,1)}), bf16[16,48,128]{2,1,0:T(8,128)(2,1)S(1)}, u32[]{:S(2)}, u32[]{:S(2)}) %all-to-all-start.1) | async-done | bytes 196640 | tf_op jit(solution)/shard_map/all_to_all | solution.py:394
  30.5 6.8 %all-to-all-start = ((bf16[16,80,128]{2,1,0:T(8,128)(2,1)}), bf16[16,80,128]{2,1,0:T(8,128)(2,1)S(1)}, u32[]{:S(2)}, u32[]{:S(2)}) async-start(bf16[16,80,128]{2,1,0:T(8,128)(2,1)} %get-tuple-element.24), calls=%async_computation | async-start | bytes 655360 | tf_op jit(solution)/shard_map/all_to_all | solution.py:402
  37.3 6.8 %all-gather = bf16[32,48,128]{2,1,0:T(8,128)(2,1)S(1)} all-gather(bf16[16,48,128]{2,1,0:T(8,128)(2,1)S(1)} %all-to-all-done.1), channel_id=2, replica_groups=mesh['z'=16,'c'=2,'y'=4,'x'=4] {'c'}, dimensions={0}, use_global_device_ids=true | all-gather | bytes 589824 | tf_op jit(solution)/shard_map/all_gather | solution.py:394
  44.1 0.5 shard_map.70
  44.6 0.6 all-to-all-done.y_ref
  45.2 5.5 %shard_map.71 = (bf16[1536,1024]{1,0:T(8,128)(2,1)}, bf16[512,1024]{1,0:T(8,128)(2,1)S(1)}, bf16[16,16,1024]{2,1,0:T(8,128)(2,1)S(1)}) custom-call(bf16[16,80,128]{2,1,0:T(8,128)(2,1)S(1)} %all-to-all-done.y_ref, bf16[2048,128]{1,0:T(8,128)(2,1)S(1)} %get-tuple-element.26.col_ref, bf16[32,2048]{1,0:T(8,128)(2,1)S(1)} %get-tuple-element.27.b_ref, ...), custom_call_target="tpu_custom_call" | custom-call | flops 671088640 | bytes 4194304 | tf_op jit(solution)/shard_map/pallas_call | solution.py:411
  50.7 15.2 %all_to_all.30.part_ref = bf16[16,16,1024]{2,1,0:T(8,128)(2,1)S(1)} all-to-all(bf16[16,16,1024]{2,1,0:T(8,128)(2,1)S(1)} %get-tuple-element.29), channel_id=1, replica_groups=mesh['z'=16,'c'=2,'y'=4,'x'=4] {'y','x'}, dimensions={0} | all-to-all | bytes 1048576 | tf_op jit(solution)/shard_map/all_to_all | solution.py:422
  65.9 1.0 shard_map.72
  66.8 7.2 %all-to-all-start.3 = ((bf16[16,16,128]{2,1,0:T(8,128)(2,1)}), bf16[16,16,128]{2,1,0:T(8,128)(2,1)S(1)}, u32[]{:S(2)}, u32[]{:S(2)}) async-start(bf16[16,16,128]{2,1,0:T(8,128)(2,1)} %get-tuple-element.30), calls=%async_computation.3 | async-start | bytes 131072 | tf_op jit(solution)/shard_map/all_to_all | solution.py:434
  74.0 7.2 %shard_map.73 = (bf16[2048,1024]{1,0:T(8,128)(2,1)}, f32[16,1024]{1,0:T(8,128)S(1)}) custom-call(bf16[16,80,128]{2,1,0:T(8,128)(2,1)S(1)} %all-to-all-done.y_ref, bf16[2048,128]{1,0:T(8,128)(2,1)S(1)} %get-tuple-element.26.col_ref, bf16[32,2048]{1,0:T(8,128)(2,1)S(1)} %get-tuple-element.27.b_ref), custom_call_target="tpu_custom_call" | custom-call | flops 671088640 | bytes 4194304 | tf_op jit(solution)/shard_map/pallas_call | solution.py:423
  81.2 4.4 %all-to-all-done.3 = bf16[16,16,128]{2,1,0:T(8,128)(2,1)S(1)} async-done(((bf16[16,16,128]{2,1,0:T(8,128)(2,1)}), bf16[16,16,128]{2,1,0:T(8,128)(2,1)S(1)}, u32[]{:S(2)}, u32[]{:S(2)}) %all-to-all-start.3) | async-done | bytes 65568 | tf_op jit(solution)/shard_map/all_to_all | solution.py:434
  85.6 5.7 %all-gather.1 = bf16[32,16,128]{2,1,0:T(8,128)(2,1)S(1)} all-gather(bf16[16,16,128]{2,1,0:T(8,128)(2,1)S(1)} %all-to-all-done.3), channel_id=3, replica_groups=mesh['z'=16,'c'=2,'y'=4,'x'=4] {'c'}, dimensions={0}, use_global_device_ids=true | all-gather | bytes 196608 | tf_op jit(solution)/shard_map/all_gather | solution.py:434
  91.2 2.8 %shard_map.74 = (f32[32,1,128]{2,1,0:T(1,128)}, bf16[32,2048]{1,0:T(8,128)(2,1)S(1)}, f32[16,128]{1,0:T(8,128)S(1)}) custom-call(bf16[2,16,16,128]{3,2,1,0:T(8,128)(2,1)S(1)} %bitcast.5, bf16[32,2048]{1,0:T(8,128)(2,1)S(1)} %get-tuple-element.27.b_ref, f32[16,1024]{1,0:T(8,128)S(1)} %get-tuple-element.31.w_ref, f32[16,1024]{1,0:T(8,128)S(1)} %get-tuple-element.32.br_ref, ...), custom_call_target="tpu_custom_call" | custom-call | tf_op jit(solution)/shard_map/pallas_call | solution.py:435
  94.1 6.8 %all-to-all-start.4 = ((f32[32,1,128]{2,1,0:T(1,128)}), f32[32,1,128]{2,1,0:T(1,128)S(1)}, u32[]{:S(2)}, u32[]{:S(2)}) async-start(f32[32,1,128]{2,1,0:T(1,128)} %get-tuple-element.36), calls=%async_computation.4 | async-start | bytes 32768 | tf_op jit(solution)/shard_map/all_to_all | solution.py:441
  100.9 2.5 %shard_map.75.mean_ref = f32[16,16,128]{2,1,0:T(8,128)S(1)} custom-call(bf16[32,2048]{1,0:T(8,128)(2,1)S(1)} %get-tuple-element.37.r_ref, bf16[2048,1024]{1,0:T(8,128)(2,1)} %get-tuple-element.38.cand_hbm, f32[16,1024]{1,0:T(8,128)S(1)} %get-tuple-element.35.mean_ref), custom_call_target="tpu_custom_call" | custom-call | flops 134217728 | bytes 4194304 | tf_op jit(solution)/shard_map/pallas_call | solution.py:442
  103.4 9.3 %all-to-all-done.4.s_ref = f32[32,1,128]{2,1,0:T(1,128)S(1)} async-done(((f32[32,1,128]{2,1,0:T(1,128)}), f32[32,1,128]{2,1,0:T(1,128)S(1)}, u32[]{:S(2)}, u32[]{:S(2)}) %all-to-all-start.4) | async-done | bytes 16416 | tf_op jit(solution)/shard_map/all_to_all | solution.py:441
  112.7 9.9 %all_to_all.31.part_ref = f32[16,24,128]{2,1,0:T(8,128)S(1)} all-to-all(f32[16,24,128]{2,1,0:T(8,128)S(1)} %shard_map.76), channel_id=1, replica_groups=mesh['z'=16,'c'=2,'y'=4,'x'=4] {'y','x'}, dimensions={0} | all-to-all | bytes 393216 | tf_op jit(solution)/shard_map/all_to_all | solution.py:452
  122.6 0.9 shard_map.77
  (1 shorter events, 0.0 us)
Async XLA Ops:
  2.3 28.2 %all-to-all-start.1 = ((bf16[16,48,128]{2,1,0:T(8,128)(2,1)}), bf16[16,48,128]{2,1,0:T(8,128)(2,1)S(1)}, u32[]{:S(2)}, u32[]{:S(2)}) async-start(bf16[16,48,128]{2,1,0:T(8,128)(2,1)} %get-tuple-element.25), calls=%async_computation.1 | async-start | bytes 393216 | tf_op jit(solution)/shard_map/all_to_all | solution.py:394
  30.5 14.7 %all-to-all-start = ((bf16[16,80,128]{2,1,0:T(8,128)(2,1)}), bf16[16,80,128]{2,1,0:T(8,128)(2,1)S(1)}, u32[]{:S(2)}, u32[]{:S(2)}) async-start(bf16[16,80,128]{2,1,0:T(8,128)(2,1)} %get-tuple-element.24), calls=%async_computation | async-start | bytes 655360 | tf_op jit(solution)/shard_map/all_to_all | solution.py:402
  66.8 18.7 %all-to-all-start.3 = ((bf16[16,16,128]{2,1,0:T(8,128)(2,1)}), bf16[16,16,128]{2,1,0:T(8,128)(2,1)S(1)}, u32[]{:S(2)}, u32[]{:S(2)}) async-start(bf16[16,16,128]{2,1,0:T(8,128)(2,1)} %get-tuple-element.30), calls=%async_computation.3 | async-start | bytes 131072 | tf_op jit(solution)/shard_map/all_to_all | solution.py:434
  94.1 18.6 %all-to-all-start.4 = ((f32[32,1,128]{2,1,0:T(1,128)}), f32[32,1,128]{2,1,0:T(1,128)S(1)}, u32[]{:S(2)}, u32[]{:S(2)}) async-start(f32[32,1,128]{2,1,0:T(1,128)} %get-tuple-element.36), calls=%async_computation.4 | async-start | bytes 32768 | tf_op jit(solution)/shard_map/all_to_all | solution.py:441

commit v5 on v3

--- a/solution.py
+++ b/solution.py
@@ -18,8 +18,12 @@
 ROWS = NQ * S
 COLS = 2 * NZ * S
 LOG2E = math.log2(math.e)
-CHUNKS = 8
+CHUNKS = 4
 PIECE = COLS // CHUNKS
+KEPT = 1
+STORED = CHUNKS - KEPT
+READ = 256
+READS = STORED * PIECE // READ
 PARAMS = pltpu.CompilerParams(vmem_limit_bytes=24 * 1024 * 1024)
 
 
@@ -129,7 +133,7 @@
     return tile_ref.at[span, :], hbm_ref.at[span, :], sems.at[i]
 
 
-def fill(col_ref, row_ref, kern_ref, even_ref, odd_ref, send=None, low_ref=None):
+def fill(col_ref, row_ref, kern_ref, even_ref, odd_ref, before=None, low_ref=None):
     def inner(z, out_ref):
         points = col_ref[pl.ds(pl.multiple_of(z * 128, 128), 128), :]
         out_ref[...] = jnp.dot(points, row_ref[...], preferred_element_type=F32)
@@ -138,39 +142,25 @@
         for i in range(8):
             span = pl.ds(pl.multiple_of(z * 128 + i * 16, 16), 16)
             kern = matern_of(in_ref[i * 16 : i * 16 + 16, :])
-            high, low = halves(kern)
-            kern_ref[span, :] = high
-            if low_ref is not None:
+            if low_ref is None:
+                kern_ref[span, :] = kern.astype(BF16)
+            else:
+                high, low = halves(kern)
+                kern_ref[span, :] = high
                 low_ref[span, :] = low
 
+    def step(i, _):
+        if before is not None:
+            before(i)
+        buffers = [even_ref, odd_ref]
+        for k in range(4):
+            z = 4 * i + k
+            inner(jnp.minimum(z + 1, NZ - 1), buffers[(k + 1) % 2])
+            spread(z, buffers[k % 2])
+        return 0
+
     inner(0, even_ref)
-
-    def step(i, _):
-        if send is not None:
-            pl.when(i > 0)(lambda: send(i - 1))
-        inner(2 * i + 1, odd_ref)
-        spread(2 * i, even_ref)
-        inner(jnp.minimum(2 * i + 2, NZ - 1), even_ref)
-        spread(2 * i + 1, odd_ref)
-        return 0
-
-    lax.fori_loop(0, NZ // 2, step, 0)
-
-
-def finish_fill(vectors_ref, kern_ref, hbm_ref, sems):
-    total = None
-    for i in range(CHUNKS):
-        span = slice(i * PIECE, i * PIECE + PIECE)
-        part = jnp.dot(vectors_ref[:, span], kern_ref[span, :], preferred_element_type=F32)
-        total = part if total is None else total + part
-        if i == 0:
-            pltpu.make_async_copy(*piece(kern_ref, hbm_ref, sems, CHUNKS - 1)).start()
-    return total[0:16] + total[16:32]
-
-
-def drain(kern_ref, hbm_ref, sems):
-    for i in range(CHUNKS):
-        pltpu.make_async_copy(*piece(kern_ref, hbm_ref, sems, i)).wait()
+    lax.fori_loop(0, NZ // 4, step, 0)
 
 
 def own_block(q):
@@ -187,25 +177,30 @@
 
 
 def first_apply(
-    y_ref, col_ref, b_ref, side_ref, hbm_ref, out_ref,
+    y_ref, col_ref, b_ref, side_ref, hbm_ref, kept_ref, out_ref,
     acc_ref, row_ref, even_ref, odd_ref, kern_ref, sems,
 ):
     q = position()
     for j in range(NQ // 2):
         row_ref[:, j * 128 : j * 128 + 128] = row_side(y_ref, j, 0)
 
-    def send(i):
-        pltpu.make_async_copy(*piece(kern_ref, hbm_ref, sems, i)).start()
-
-    fill(col_ref, row_ref, kern_ref, even_ref, odd_ref, send)
-    acc_ref[...] = finish_fill(b_ref, kern_ref, hbm_ref, sems)
+    def before(i):
+        @pl.when(i > 0)
+        def _():
+            pltpu.make_async_copy(*piece(kern_ref, hbm_ref, sems, i - 1)).start()
+
+    fill(col_ref, row_ref, kern_ref, even_ref, odd_ref, before)
+    total = jnp.dot(b_ref[...], kern_ref[...], preferred_element_type=F32)
+    acc_ref[...] = total[0:16] + total[16:32]
+    kept_ref[...] = kern_ref[STORED * PIECE :, :]
     own = side_ref[:, 0:64] * side_ref[:, 64:128]
     twice = jnp.concatenate([own, own], axis=1)
     acc_ref[:, own_block(q)] += jnp.where(own_mask(q), twice, 0.0)
     image = acc_ref[...].astype(BF16)
     for i in range(NQ):
         out_ref[i] = image
-    drain(kern_ref, hbm_ref, sems)
+    for i in range(STORED):
+        pltpu.make_async_copy(*piece(kern_ref, hbm_ref, sems, i)).wait()
 
 
 def merge_image(part_ref, y_ref, out_ref, w_ref, br_ref):
@@ -234,24 +229,24 @@
 
 
 def fetch(hbm_ref, tile_ref, sems, i):
-    target, source, sem = piece(tile_ref, hbm_ref, sems, i)
-    return pltpu.make_async_copy(source, target, sem)
-
-
-def streamed(r_ref, hbm_ref, tile_ref, sems):
-    total = None
-    for i in range(CHUNKS):
+    span = slice(i * READ, i * READ + READ)
+    return pltpu.make_async_copy(hbm_ref.at[span, :], tile_ref.at[span, :], sems.at[i])
+
+
+def streamed(r_ref, hbm_ref, tile_ref, sems, kept_ref):
+    total = jnp.dot(r_ref[:, STORED * PIECE :], kept_ref[...], preferred_element_type=F32)
+    for i in range(READS):
         fetch(hbm_ref, tile_ref, sems, i).wait()
-        span = slice(i * PIECE, i * PIECE + PIECE)
-        part = jnp.dot(r_ref[:, span], tile_ref[span, :], preferred_element_type=F32)
-        total = part if total is None else total + part
+        span = slice(i * READ, i * READ + READ)
+        total = total + jnp.dot(r_ref[:, span], tile_ref[span, :], preferred_element_type=F32)
     return total[0:16] + total[16:32]
 
 
 def second_apply(
-    s_ref, b_ref, w_ref, br_ref, kern_hbm, side_ref, out_ref, r_ref, own_ref, kern_ref, sems
+    s_ref, b_ref, w_ref, br_ref, kern_hbm, kept_ref, side_ref, out_ref, r_ref, own_ref,
+    kern_ref, sems,
 ):
-    for i in range(CHUNKS):
+    for i in range(READS):
         fetch(kern_hbm, kern_ref, sems, i).start()
     q = position()
     sums = s_ref[0, 0, :, 64:128].astype(F32)
@@ -278,7 +273,7 @@
     rr = jnp.sum(own_r * own_r, axis=1, keepdims=True)
     side = jnp.where(lane == 0, bb, jnp.where(lane == 1, bw, 0.0))
     own_ref[...] = jnp.concatenate([own_r, side], axis=1)
-    applied = streamed(r_ref, kern_hbm, kern_ref, sems)
+    applied = streamed(r_ref, kern_hbm, kern_ref, sems, kept_ref)
     s = jnp.sum(r_row * applied, axis=1, keepdims=True) + jnp.sum(
         noise * own_r * own_r, axis=1, keepdims=True
     )
@@ -353,7 +348,6 @@
 
     vmem = pl.BlockSpec(memory_space=pltpu.VMEM)
     hbm = pl.BlockSpec(memory_space=pltpu.HBM)
-    whole_tile = [pltpu.VMEM((COLS, ROWS), BF16), pltpu.SemaphoreType.DMA((CHUNKS,))]
     build = [
         pltpu.VMEM((128, ROWS), BF16),
         pltpu.VMEM((128, ROWS), F32),
@@ -395,11 +389,20 @@
             flops=COLS * 1000, bytes_accessed=4 * COLS * 128, transcendentals=0
         ),
     )(z_in)
-    kern, image_out = call(
+    kern, kept, image_out = call(
         first_apply,
-        out_specs=(hbm, vmem),
-        out_shape=(pltpu.HBM((COLS, ROWS), BF16), shape(NQ, RHS, ROWS, dtype=BF16)),
-        scratch_shapes=[pltpu.VMEM((RHS, ROWS), F32), *build, *whole_tile],
+        out_specs=(hbm, vmem, vmem),
+        out_shape=(
+            pltpu.HBM((STORED * PIECE, ROWS), BF16),
+            shape(KEPT * PIECE, ROWS, dtype=BF16),
+            shape(NQ, RHS, ROWS, dtype=BF16),
+        ),
+        scratch_shapes=[
+            pltpu.VMEM((RHS, ROWS), F32),
+            *build,
+            pltpu.VMEM((COLS, ROWS), BF16),
+            pltpu.SemaphoreType.DMA((STORED,)),
+        ],
         cost_estimate=build_cost,
     )(y_in, col, b_col, side)
     image_in = lax.all_to_all(image_out, ("y", "x"), 0, 0)
@@ -410,10 +413,13 @@
     w_in = lax.all_gather(lax.all_to_all(w_out, "z", 0, 0), "c", axis=0)
     scalar_out, r_col, own = call(
         second_apply,
-        in_specs=[vmem] * 4 + [hbm, vmem],
+        in_specs=[vmem] * 4 + [hbm, vmem, vmem],
         out_shape=(shape(NZ, 1, 128), shape(32, COLS, dtype=BF16), shape(RHS, 128)),
-        scratch_shapes=whole_tile,
-    )(w_in, b_col, w_row, b_row, in_hbm(kern), side)
+        scratch_shapes=[
+            pltpu.VMEM((STORED * PIECE, ROWS), BF16),
+            pltpu.SemaphoreType.DMA((READS,)),
+        ],
+    )(w_in, b_col, w_row, b_row, in_hbm(kern), kept, side)
     scalar_in = lax.all_gather(lax.all_to_all(scalar_out, "z", 0, 0), "c", axis=0)
     mean_part = call(
         cand_mean,

time: 123 us -> 122 us (level)
  Pallas kernels: 19.8 us -> 18.3 us
where the time goes in v5:
time: 122 us; the launch traced here: 121 us
  blocking collectives  87 us (71%)
  Pallas kernels  18.3 us (15%)
  starting transfers between devices  10.2 us (8%)
  waiting for transfers between devices  4.91 us (4%)
    all_to_all x1, blocking collectives, per_device(): z_in = lax.all_gather(lax.all_to_all(z_out, 'z', 0, 0), 'c', axis=0)  28 us
    all_to_all x1, blocking collectives, per_device(): w_in = lax.all_gather(lax.all_to_all(w_out, 'z', 0, 0), 'c', axis=0)  18.5 us
    all_to_all x1, blocking collectives, per_device(): image_in = lax.all_to_all(image_out, ('y', 'x'), 0, 0)  15.2 us
    all_to_all x1, blocking collectives, per_device(): mean_in = lax.all_to_all(mean_out, ('y', 'x'), 0, 0)  9.87 us
    all_gather x1, blocking collectives, per_device(): z_in = lax.all_gather(lax.all_to_all(z_out, 'z', 0, 0), 'c', axis=0)  6.83 us
    pallas_call x1, Pallas kernels, per_device(): call(cand_mean, out_shape=shape(NQ, RHS, 128), scratch_shapes=[*build, *[...  6.82 us
    all_to_all x1, starting transfers between devices, per_device(): y_in = lax.all_to_all(y_out, ('y', 'x'), 0, 0)  6.76 us
    all_gather x1, blocking collectives, per_device(): w_in = lax.all_gather(lax.all_to_all(w_out, 'z', 0, 0), 'c', axis=0)  5.66 us
  transfers between devices with their start and end apart: 2, of which 2 were waited for; matrix products, arithmetic and copies ran while one was open for 0% of the time, Pallas kernels for 6%

profile of v5, /device:TPU:1, one launch (start us, length us, event | category | flops | bytes accessed | tf_op | source)
XLA Modules:
  0.0 121.2 jit_solution(14204249286063183698)
XLA Ops:
  0.6 1.8 %shard_map.68 = (bf16[16,80,128]{2,1,0:T(8,128)(2,1)}, bf16[16,48,128]{2,1,0:T(8,128)(2,1)S(1)}, f32[16,128]{1,0:T(8,128)S(1)}) custom-call(f32[64,64]{1,0:T(8,128)} %train_hbm.1, f32[64,64]{1,0:T(8,128)} %cand_hbm.1, f32[1,64]{1,0:T(1,128)} %bitcast.8, f32[1,64]{1,0:T(1,128)} %bitcast.9, f32[16,64]{1,0:T(8,128)} %target_hbm.1), custom_call_target="tpu_custom_call" | custom-call | tf_op jit(solution)/shard_map/pallas_call | solution.py:360
  2.4 28.0 %all_to_all.30 = bf16[16,48,128]{2,1,0:T(8,128)(2,1)S(1)} all-to-all(bf16[16,48,128]{2,1,0:T(8,128)(2,1)S(1)} %get-tuple-element.17), channel_id=1, replica_groups=mesh['z'=16,'c'=2,'y'=4,'x'=4] {'z'}, dimensions={0} | all-to-all | bytes 393216 | tf_op jit(solution)/shard_map/all_to_all | solution.py:383
  30.4 6.8 %all-to-all-start = ((bf16[16,80,128]{2,1,0:T(8,128)(2,1)}), bf16[16,80,128]{2,1,0:T(8,128)(2,1)S(1)}, u32[]{:S(2)}, u32[]{:S(2)}) async-start(bf16[16,80,128]{2,1,0:T(8,128)(2,1)} %get-tuple-element.16), calls=%async_computation | async-start | bytes 655360 | tf_op jit(solution)/shard_map/all_to_all | solution.py:384
  37.2 6.8 %all-gather = bf16[32,48,128]{2,1,0:T(8,128)(2,1)S(1)} all-gather(bf16[16,48,128]{2,1,0:T(8,128)(2,1)S(1)} %all_to_all.30), channel_id=2, replica_groups=mesh['z'=16,'c'=2,'y'=4,'x'=4] {'c'}, dimensions={0}, use_global_device_ids=true | all-gather | bytes 589824 | tf_op jit(solution)/shard_map/all_gather | solution.py:383
  44.0 0.5 shard_map.69
  44.5 0.6 all-to-all-done.y_ref
  45.1 5.3 %shard_map.70 = (bf16[1536,1024]{1,0:T(8,128)(2,1)}, bf16[512,1024]{1,0:T(8,128)(2,1)S(1)}, bf16[16,16,1024]{2,1,0:T(8,128)(2,1)S(1)}) custom-call(bf16[16,80,128]{2,1,0:T(8,128)(2,1)S(1)} %all-to-all-done.y_ref, bf16[2048,128]{1,0:T(8,128)(2,1)S(1)} %get-tuple-element.18.col_ref, bf16[32,2048]{1,0:T(8,128)(2,1)S(1)} %get-tuple-element.19.b_ref, ...), custom_call_target="tpu_custom_call" | custom-call | flops 671088640 | bytes 4194304 | tf_op jit(solution)/shard_map/pallas_call | solution.py:392
  50.3 15.2 %all_to_all.31.part_ref = bf16[16,16,1024]{2,1,0:T(8,128)(2,1)S(1)} all-to-all(bf16[16,16,1024]{2,1,0:T(8,128)(2,1)S(1)} %get-tuple-element.21), channel_id=1, replica_groups=mesh['z'=16,'c'=2,'y'=4,'x'=4] {'y','x'}, dimensions={0} | all-to-all | bytes 1048576 | tf_op jit(solution)/shard_map/all_to_all | solution.py:408
  65.5 0.3 shard_map.71
  65.8 18.5 %all_to_all.32 = bf16[16,16,128]{2,1,0:T(8,128)(2,1)S(1)} all-to-all(bf16[16,16,128]{2,1,0:T(8,128)(2,1)S(1)} %get-tuple-element.22), channel_id=1, replica_groups=mesh['z'=16,'c'=2,'y'=4,'x'=4] {'z'}, dimensions={0} | all-to-all | bytes 131072 | tf_op jit(solution)/shard_map/all_to_all | solution.py:413
  84.3 5.7 %all-gather.1 = bf16[32,16,128]{2,1,0:T(8,128)(2,1)S(1)} all-gather(bf16[16,16,128]{2,1,0:T(8,128)(2,1)S(1)} %all_to_all.32), channel_id=3, replica_groups=mesh['z'=16,'c'=2,'y'=4,'x'=4] {'c'}, dimensions={0}, use_global_device_ids=true | all-gather | bytes 196608 | tf_op jit(solution)/shard_map/all_gather | solution.py:413
  90.0 2.8 %shard_map.72 = (f32[16,1,128]{2,1,0:T(1,128)}, bf16[32,2048]{1,0:T(8,128)(2,1)S(1)}, f32[16,128]{1,0:T(8,128)S(1)}) custom-call(bf16[2,16,16,128]{3,2,1,0:T(8,128)(2,1)S(1)} %bitcast.6, bf16[32,2048]{1,0:T(8,128)(2,1)S(1)} %get-tuple-element.19.b_ref, f32[16,1024]{1,0:T(8,128)S(1)} %get-tuple-element.23.w_ref, f32[16,1024]{1,0:T(8,128)S(1)} %get-tuple-element.24.br_ref, ...), custom_call_target="tpu_custom_call" | custom-call | tf_op jit(solution)/shard_map/pallas_call | solution.py:414
  92.8 3.5 %all-to-all-start.4 = ((f32[16,1,128]{2,1,0:T(1,128)}), f32[16,1,128]{2,1,0:T(1,128)S(1)}, u32[]{:S(2)}, u32[]{:S(2)}) async-start(f32[16,1,128]{2,1,0:T(1,128)} %get-tuple-element.27), calls=%async_computation.4 | async-start | bytes 16384 | tf_op jit(solution)/shard_map/all_to_all | solution.py:423
  96.3 6.8 %shard_map.73.mean_ref = f32[16,16,128]{2,1,0:T(8,128)S(1)} custom-call(bf16[16,80,128]{2,1,0:T(8,128)(2,1)S(1)} %all-to-all-done.y_ref, bf16[2048,128]{1,0:T(8,128)(2,1)S(1)} %get-tuple-element.18.col_ref, bf16[32,2048]{1,0:T(8,128)(2,1)S(1)} %get-tuple-element.19.b_ref, bf16[32,2048]{1,0:T(8,128)(2,1)S(1)} %get-tuple-element.28.r_ref), custom_call_target="tpu_custom_call" | custom-call | flops 671088640 | bytes 4194304 | tf_op jit(solution)/shard_map/pallas_call | solution.py:424
  103.1 4.3 %all-to-all-done.4 = f32[16,1,128]{2,1,0:T(1,128)S(1)} async-done(((f32[16,1,128]{2,1,0:T(1,128)}), f32[16,1,128]{2,1,0:T(1,128)S(1)}, u32[]{:S(2)}, u32[]{:S(2)}) %all-to-all-start.4) | async-done | bytes 8224 | tf_op jit(solution)/shard_map/all_to_all | solution.py:423
  107.5 2.9 %all-gather.2 = f32[32,1,128]{2,1,0:T(1,128)S(1)} all-gather(f32[16,1,128]{2,1,0:T(1,128)S(1)} %all-to-all-done.4), channel_id=4, replica_groups=mesh['z'=16,'c'=2,'y'=4,'x'=4] {'c'}, dimensions={0}, use_global_device_ids=true | all-gather | bytes 24576 | tf_op jit(solution)/shard_map/all_gather | solution.py:423
  110.4 9.9 %all_to_all.33.part_ref = f32[16,24,128]{2,1,0:T(8,128)S(1)} all-to-all(f32[16,24,128]{2,1,0:T(8,128)S(1)} %shard_map.74), channel_id=1, replica_groups=mesh['z'=16,'c'=2,'y'=4,'x'=4] {'y','x'}, dimensions={0} | all-to-all | bytes 393216 | tf_op jit(solution)/shard_map/all_to_all | solution.py:431
  120.3 0.9 shard_map.75
  (1 shorter events, 0.0 us)
Async XLA Ops:
  30.4 14.7 %all-to-all-start = ((bf16[16,80,128]{2,1,0:T(8,128)(2,1)}), bf16[16,80,128]{2,1,0:T(8,128)(2,1)S(1)}, u32[]{:S(2)}, u32[]{:S(2)}) async-start(bf16[16,80,128]{2,1,0:T(8,128)(2,1)} %get-tuple-element.16), calls=%async_computation | async-start | bytes 655360 | tf_op jit(solution)/shard_map/all_to_all | solution.py:384
  92.8 14.7 %all-to-all-start.4 = ((f32[16,1,128]{2,1,0:T(1,128)}), f32[16,1,128]{2,1,0:T(1,128)S(1)}, u32[]{:S(2)}, u32[]{:S(2)}) async-start(f32[16,1,128]{2,1,0:T(1,128)} %get-tuple-element.27), calls=%async_computation.4 | async-start | bytes 16384 | tf_op jit(solution)/shard_map/all_to_all | solution.py:423

commit v6 on v5

--- a/solution.py
+++ b/solution.py
@@ -85,19 +85,29 @@
     b = jnp.concatenate([b_high, b_low], axis=1)
     both = jnp.concatenate([train.astype(BF16), cand.astype(BF16)], axis=1)
     folded = jnp.concatenate([train[:32].astype(BF16), train[32:].astype(BF16)], axis=1)
-    for i in range(NQ):
+    for i in range(NZ):
         z_ref[i, 0:32, :] = folded
         z_ref[i, 32:48, :] = b
-        y_ref[i, 0:64, :] = both
-        y_ref[i, 64:80, :] = b
+    y_ref[0:64, :] = both
+    y_ref[64:80, :] = b
     side_ref[...] = jnp.concatenate(
         [target, jnp.broadcast_to(noise_ref[...], (RHS, S))], axis=1
     )
 
 
+def order(own_ref, one_ref, two_ref, three_ref, out_ref):
+    y = lax.axis_index("y")
+    for k, ref in enumerate([own_ref, one_ref, two_ref, three_ref]):
+        value = ref[...]
+        for x in range(4):
+            out_ref[x, (y + k) % 4] = value
+
+
 def row_side(y_ref, j, first):
     points = jnp.concatenate(
-        [y_ref[2 * j, 0:64, first : first + 64], y_ref[2 * j + 1, 0:64, first : first + 64]],
+        [y_ref[(2 * j) % 4, j // 2, 0:64, first : first + 64],
+            y_ref[(2 * j + 1) % 4, j // 2, 0:64, first : first + 64],
+       ],
         axis=1,
     ).astype(F32)
     norm = jnp.sum(points * points, axis=0, keepdims=True)
@@ -210,7 +220,8 @@
         total = total + part_ref[i].astype(F32)
     w_ref[...] = total
     for j in range(NQ // 2):
-        even, odd = y_ref[2 * j, 64:80, :].astype(F32), y_ref[2 * j + 1, 64:80, :].astype(F32)
+        even = y_ref[(2 * j) % 4, j // 2, 64:80, :].astype(F32)
+        odd = y_ref[(2 * j + 1) % 4, j // 2, 64:80, :].astype(F32)
         br_ref[:, j * 128 : j * 128 + 128] = jnp.concatenate(
             [even[:, :64] + even[:, 64:], odd[:, :64] + odd[:, 64:]], axis=1
         )
@@ -361,7 +372,7 @@
         prepare,
         in_specs=[hbm] * 5,
         out_shape=(
-            shape(NQ, 80, 128, dtype=BF16),
+            shape(80, 128, dtype=BF16),
             shape(NZ, 48, 128, dtype=BF16),
             shape(RHS, 128),
         ),
@@ -381,7 +392,15 @@
         in_hbm(targets),
     )
     z_in = lax.all_gather(lax.all_to_all(z_out, "z", 0, 0), "c", axis=0)
-    y_in = lax.all_to_all(y_out, ("y", "x"), 0, 0)
+    along_y = [
+        lax.ppermute(y_out, "y", [((d + k) % 4, d) for d in range(4)]) for k in (1, 2, 3)
+    ]
+    y_half = call(
+        order,
+        out_shape=shape(4, 4, 80, 128, dtype=BF16),
+        cost_estimate=pl.CostEstimate(flops=0, bytes_accessed=400000, transcendentals=0),
+    )(y_out, *along_y)
+    y_in = lax.all_to_all(y_half, "x", 0, 0)
     col, b_col = call(
         col_side,
         out_shape=(shape(COLS, 128, dtype=BF16), shape(32, COLS, dtype=BF16)),

time: 122 us -> 123 us (level)
  blocking collectives: 87 us -> 62.6 us
  starting transfers between devices: 10.2 us -> 34 us
  waiting for transfers between devices: 4.91 us -> 6.16 us
    all_to_all x1 -> x0, blocking collectives: 28 us -> none  [per_device(): z_in = lax.all_gather(lax.all_to_all(z_out, 'z', 0, 0), 'c', axis=0)]
    all_to_all x1 -> x2, starting transfers between devices: 6.76 us -> 19.8 us  [the longest x1 15.7 us: per_device(): z_in = lax.all_gather(lax.all_to_all(z_out, 'z', 0, 0), 'c', axis=0)]
    ppermute x0 -> x3, starting transfers between devices: none -> 10.7 us  [per_device(): lax.ppermute(y_out, 'y', [((d + k) % 4, d) for d in range(4)])]
    all_to_all x1, blocking collectives: 18.5 us -> 20.8 us  [per_device(): w_in = lax.all_gather(lax.all_to_all(w_out, 'z', 0, 0), 'c', axis=0)]
    ppermute x0 -> x3, waiting for transfers between devices: none -> 1.82 us  [per_device(): lax.ppermute(y_out, 'y', [((d + k) % 4, d) for d in range(4)])]
  transfers between devices with their start and end apart: 2 -> 6, of which waited for: 2 -> 2; matrix products, arithmetic and copies ran while one was open for 0% -> 0% of each run, Pallas kernels for 6% -> 7%
where the time goes in v6:
time: 123 us
  blocking collectives  62.6 us (51%)
  starting transfers between devices  34 us (28%)
  Pallas kernels  19 us (15%)
  waiting for transfers between devices  6.16 us (5%)
    all_to_all x1, blocking collectives, per_device(): w_in = lax.all_gather(lax.all_to_all(w_out, 'z', 0, 0), 'c', axis=0)  20.8 us
    all_to_all x1, blocking collectives, per_device(): image_in = lax.all_to_all(image_out, ('y', 'x'), 0, 0)  16.1 us
    all_to_all x1, starting transfers between devices, per_device(): z_in = lax.all_gather(lax.all_to_all(z_out, 'z', 0, 0), 'c', axis=0)  15.7 us
    ppermute x3, starting transfers between devices, per_device(): lax.ppermute(y_out, 'y', [((d + k) % 4, d) for d in range(4)])  10.7 us
    all_to_all x1, blocking collectives, per_device(): mean_in = lax.all_to_all(mean_out, ('y', 'x'), 0, 0)  9.89 us
    all_gather x1, blocking collectives, per_device(): w_in = lax.all_gather(lax.all_to_all(w_out, 'z', 0, 0), 'c', axis=0)  6.88 us
    pallas_call x1, Pallas kernels, per_device(): call(cand_mean, out_shape=shape(NQ, RHS, 128), scratch_shapes=[*build, *[...  6.82 us
    all_gather x1, blocking collectives, per_device(): z_in = lax.all_gather(lax.all_to_all(z_out, 'z', 0, 0), 'c', axis=0)  5.98 us
  transfers between devices with their start and end apart: 6, of which 2 were waited for; matrix products, arithmetic and copies ran while one was open for 0% of the time, Pallas kernels for 7%

profile of v6, /device:TPU:1, one launch (start us, length us, event | category | flops | bytes accessed | tf_op | source)
XLA Modules:
  0.0 122.5 jit_solution(16948185462681456310)
XLA Ops:
  0.6 1.7 %shard_map.68 = (bf16[80,128]{1,0:T(8,128)(2,1)S(1)}, bf16[16,48,128]{2,1,0:T(8,128)(2,1)}, f32[16,128]{1,0:T(8,128)S(1)}) custom-call(f32[64,64]{1,0:T(8,128)} %train_hbm.1, f32[64,64]{1,0:T(8,128)} %cand_hbm.1, f32[1,64]{1,0:T(1,128)} %bitcast.8, f32[1,64]{1,0:T(1,128)} %bitcast.9, f32[16,64]{1,0:T(8,128)} %target_hbm.1), custom_call_target="tpu_custom_call" | custom-call | tf_op jit(solution)/shard_map/pallas_call | solution.py:371
  2.3 15.7 %all-to-all-start.1 = ((bf16[16,48,128]{2,1,0:T(8,128)(2,1)}), bf16[16,48,128]{2,1,0:T(8,128)(2,1)S(1)}, u32[]{:S(2)}, u32[]{:S(2)}) async-start(bf16[16,48,128]{2,1,0:T(8,128)(2,1)} %get-tuple-element.17), calls=%async_computation.1 | async-start | bytes 393216 | tf_op jit(solution)/shard_map/all_to_all | solution.py:394
  18.1 3.2 %collective-permute-start.2 = (bf16[80,128]{1,0:T(8,128)(2,1)S(1)}, bf16[80,128]{1,0:T(8,128)(2,1)S(1)}, u32[]{:S(2)}, u32[]{:S(2)}) collective-permute-start(bf16[80,128]{1,0:T(8,128)(2,1)S(1)} %get-tuple-element.16.own_ref), channel_id=1, source_target_pairs={{12,0},{0,4},{4,8},{8,12},{13,1},{1,5},{5,9},{9,13},{14,2},{2,6},{... | collective-permute-start | bytes 61448 | tf_op jit(solution)/shard_map/ppermute | solution.py:396
  21.3 4.5 %collective-permute-start.1 = (bf16[80,128]{1,0:T(8,128)(2,1)S(1)}, bf16[80,128]{1,0:T(8,128)(2,1)S(1)}, u32[]{:S(2)}, u32[]{:S(2)}) collective-permute-start(bf16[80,128]{1,0:T(8,128)(2,1)S(1)} %get-tuple-element.16.own_ref), channel_id=1, source_target_pairs={{8,0},{12,4},{0,8},{4,12},{9,1},{13,5},{1,9},{5,13},{10,2},{14,6},... | collective-permute-start | bytes 61448 | tf_op jit(solution)/shard_map/ppermute | solution.py:396
  25.8 3.0 %collective-permute-start = (bf16[80,128]{1,0:T(8,128)(2,1)S(1)}, bf16[80,128]{1,0:T(8,128)(2,1)S(1)}, u32[]{:S(2)}, u32[]{:S(2)}) collective-permute-start(bf16[80,128]{1,0:T(8,128)(2,1)S(1)} %get-tuple-element.16.own_ref), channel_id=1, source_target_pairs={{4,0},{8,4},{12,8},{0,12},{5,1},{9,5},{13,9},{1,13},{6,2},{10,6},{... | collective-permute-start | bytes 61448 | tf_op jit(solution)/shard_map/ppermute | solution.py:396
  28.8 0.0 collective-permute-done.2.three_ref
  28.8 0.0 collective-permute-done.1.two_ref
  28.8 1.8 %collective-permute-done.one_ref = bf16[80,128]{1,0:T(8,128)(2,1)S(1)} collective-permute-done((bf16[80,128]{1,0:T(8,128)(2,1)S(1)}, bf16[80,128]{1,0:T(8,128)(2,1)S(1)}, u32[]{:S(2)}, u32[]{:S(2)}) %collective-permute-start) | collective-permute-done | bytes 20512 | tf_op jit(solution)/shard_map/ppermute | solution.py:396
  30.7 0.8 shard_map.69
  31.4 0.0 all-to-all-done.1
  31.4 4.0 %all-to-all-start = ((bf16[4,4,80,128]{3,2,1,0:T(8,128)(2,1)}), bf16[4,4,80,128]{3,2,1,0:T(8,128)(2,1)S(1)}, u32[]{:S(2)}, u32[]{:S(2)}) async-start(bf16[4,4,80,128]{3,2,1,0:T(8,128)(2,1)} %shard_map.69), calls=%async_computation | async-start | bytes 655360 | tf_op jit(solution)/shard_map/all_to_all | solution.py:403
  35.4 6.0 %all-gather = bf16[32,48,128]{2,1,0:T(8,128)(2,1)S(1)} all-gather(bf16[16,48,128]{2,1,0:T(8,128)(2,1)S(1)} %all-to-all-done.1), channel_id=2, replica_groups=mesh['z'=16,'c'=2,'y'=4,'x'=4] {'c'}, dimensions={0}, use_global_device_ids=true | all-gather | bytes 589824 | tf_op jit(solution)/shard_map/all_gather | solution.py:394
  41.4 0.5 shard_map.70
  41.9 0.0 all-to-all-done.y_ref
  41.9 5.3 %shard_map.71 = (bf16[1536,1024]{1,0:T(8,128)(2,1)}, bf16[512,1024]{1,0:T(8,128)(2,1)S(1)}, bf16[16,16,1024]{2,1,0:T(8,128)(2,1)S(1)}) custom-call(bf16[4,4,80,128]{3,2,1,0:T(8,128)(2,1)S(1)} %all-to-all-done.y_ref, bf16[2048,128]{1,0:T(8,128)(2,1)S(1)} %get-tuple-element.18.col_ref, bf16[32,2048]{1,0:T(8,128)(2,1)S(1)} %get-tuple-element.19.b_ref, ...), custom_call_target="tpu_custom_call" | custom-call | flops 671088640 | bytes 4194304 | tf_op jit(solution)/shard_map/pallas_call | solution.py:411
  47.2 16.1 %all_to_all.30.part_ref = bf16[16,16,1024]{2,1,0:T(8,128)(2,1)S(1)} all-to-all(bf16[16,16,1024]{2,1,0:T(8,128)(2,1)S(1)} %get-tuple-element.21), channel_id=1, replica_groups=mesh['z'=16,'c'=2,'y'=4,'x'=4] {'y','x'}, dimensions={0} | all-to-all | bytes 1048576 | tf_op jit(solution)/shard_map/all_to_all | solution.py:427
  63.3 0.3 shard_map.72
  63.6 20.8 %all_to_all.31 = bf16[16,16,128]{2,1,0:T(8,128)(2,1)S(1)} all-to-all(bf16[16,16,128]{2,1,0:T(8,128)(2,1)S(1)} %get-tuple-element.22), channel_id=1, replica_groups=mesh['z'=16,'c'=2,'y'=4,'x'=4] {'z'}, dimensions={0} | all-to-all | bytes 131072 | tf_op jit(solution)/shard_map/all_to_all | solution.py:432
  84.5 6.9 %all-gather.1 = bf16[32,16,128]{2,1,0:T(8,128)(2,1)S(1)} all-gather(bf16[16,16,128]{2,1,0:T(8,128)(2,1)S(1)} %all_to_all.31), channel_id=3, replica_groups=mesh['z'=16,'c'=2,'y'=4,'x'=4] {'c'}, dimensions={0}, use_global_device_ids=true | all-gather | bytes 196608 | tf_op jit(solution)/shard_map/all_gather | solution.py:432
  91.4 2.8 %shard_map.73 = (f32[16,1,128]{2,1,0:T(1,128)}, bf16[32,2048]{1,0:T(8,128)(2,1)S(1)}, f32[16,128]{1,0:T(8,128)S(1)}) custom-call(bf16[2,16,16,128]{3,2,1,0:T(8,128)(2,1)S(1)} %bitcast.6, bf16[32,2048]{1,0:T(8,128)(2,1)S(1)} %get-tuple-element.19.b_ref, f32[16,1024]{1,0:T(8,128)S(1)} %get-tuple-element.23.w_ref, f32[16,1024]{1,0:T(8,128)S(1)} %get-tuple-element.24.br_ref, ...), custom_call_target="tpu_custom_call" | custom-call | tf_op jit(solution)/shard_map/pallas_call | solution.py:433
  94.2 3.5 %all-to-all-start.4 = ((f32[16,1,128]{2,1,0:T(1,128)}), f32[16,1,128]{2,1,0:T(1,128)S(1)}, u32[]{:S(2)}, u32[]{:S(2)}) async-start(f32[16,1,128]{2,1,0:T(1,128)} %get-tuple-element.27), calls=%async_computation.4 | async-start | bytes 16384 | tf_op jit(solution)/shard_map/all_to_all | solution.py:442
  97.7 6.8 %shard_map.74.mean_ref = f32[16,16,128]{2,1,0:T(8,128)S(1)} custom-call(bf16[4,4,80,128]{3,2,1,0:T(8,128)(2,1)S(1)} %all-to-all-done.y_ref, bf16[2048,128]{1,0:T(8,128)(2,1)S(1)} %get-tuple-element.18.col_ref, bf16[32,2048]{1,0:T(8,128)(2,1)S(1)} %get-tuple-element.19.b_ref, bf16[32,2048]{1,0:T(8,128)(2,1)S(1)} %get-tuple-element.28.r_ref), custom_call_target="tpu_custom_call" | custom-call | flops 671088640 | bytes 4194304 | tf_op jit(solution)/shard_map/pallas_call | solution.py:443
  104.5 4.3 %all-to-all-done.4 = f32[16,1,128]{2,1,0:T(1,128)S(1)} async-done(((f32[16,1,128]{2,1,0:T(1,128)}), f32[16,1,128]{2,1,0:T(1,128)S(1)}, u32[]{:S(2)}, u32[]{:S(2)}) %all-to-all-start.4) | async-done | bytes 8224 | tf_op jit(solution)/shard_map/all_to_all | solution.py:442
  108.8 2.9 %all-gather.2 = f32[32,1,128]{2,1,0:T(1,128)S(1)} all-gather(f32[16,1,128]{2,1,0:T(1,128)S(1)} %all-to-all-done.4), channel_id=4, replica_groups=mesh['z'=16,'c'=2,'y'=4,'x'=4] {'c'}, dimensions={0}, use_global_device_ids=true | all-gather | bytes 24576 | tf_op jit(solution)/shard_map/all_gather | solution.py:442
  111.8 9.9 %all_to_all.32.part_ref = f32[16,24,128]{2,1,0:T(8,128)S(1)} all-to-all(f32[16,24,128]{2,1,0:T(8,128)S(1)} %shard_map.75), channel_id=1, replica_groups=mesh['z'=16,'c'=2,'y'=4,'x'=4] {'y','x'}, dimensions={0} | all-to-all | bytes 393216 | tf_op jit(solution)/shard_map/all_to_all | solution.py:450
  121.7 0.9 shard_map.76
  (1 shorter events, 0.0 us)
Async XLA Ops:
  2.3 29.1 %all-to-all-start.1 = ((bf16[16,48,128]{2,1,0:T(8,128)(2,1)}), bf16[16,48,128]{2,1,0:T(8,128)(2,1)S(1)}, u32[]{:S(2)}, u32[]{:S(2)}) async-start(bf16[16,48,128]{2,1,0:T(8,128)(2,1)} %get-tuple-element.17), calls=%async_computation.1 | async-start | bytes 393216 | tf_op jit(solution)/shard_map/all_to_all | solution.py:394
  18.1 10.7 %collective-permute-start.2 = (bf16[80,128]{1,0:T(8,128)(2,1)S(1)}, bf16[80,128]{1,0:T(8,128)(2,1)S(1)}, u32[]{:S(2)}, u32[]{:S(2)}) collective-permute-start(bf16[80,128]{1,0:T(8,128)(2,1)S(1)} %get-tuple-element.16.own_ref), channel_id=1, source_target_pairs={{12,0},{0,4},{4,8},{8,12},{13,1},{1,5},{5,9},{9,13},{14,2},{2,6},{... | collective-permute-start | bytes 61448 | tf_op jit(solution)/shard_map/ppermute | solution.py:396
  21.3 7.5 %collective-permute-start.1 = (bf16[80,128]{1,0:T(8,128)(2,1)S(1)}, bf16[80,128]{1,0:T(8,128)(2,1)S(1)}, u32[]{:S(2)}, u32[]{:S(2)}) collective-permute-start(bf16[80,128]{1,0:T(8,128)(2,1)S(1)} %get-tuple-element.16.own_ref), channel_id=1, source_target_pairs={{8,0},{12,4},{0,8},{4,12},{9,1},{13,5},{1,9},{5,13},{10,2},{14,6},... | collective-permute-start | bytes 61448 | tf_op jit(solution)/shard_map/ppermute | solution.py:396
  25.8 4.8 %collective-permute-start = (bf16[80,128]{1,0:T(8,128)(2,1)S(1)}, bf16[80,128]{1,0:T(8,128)(2,1)S(1)}, u32[]{:S(2)}, u32[]{:S(2)}) collective-permute-start(bf16[80,128]{1,0:T(8,128)(2,1)S(1)} %get-tuple-element.16.own_ref), channel_id=1, source_target_pairs={{4,0},{8,4},{12,8},{0,12},{5,1},{9,5},{13,9},{1,13},{6,2},{10,6},{... | collective-permute-start | bytes 61448 | tf_op jit(solution)/shard_map/ppermute | solution.py:396
  31.4 10.5 %all-to-all-start = ((bf16[4,4,80,128]{3,2,1,0:T(8,128)(2,1)}), bf16[4,4,80,128]{3,2,1,0:T(8,128)(2,1)S(1)}, u32[]{:S(2)}, u32[]{:S(2)}) async-start(bf16[4,4,80,128]{3,2,1,0:T(8,128)(2,1)} %shard_map.69), calls=%async_computation | async-start | bytes 655360 | tf_op jit(solution)/shard_map/all_to_all | solution.py:403
  94.2 14.7 %all-to-all-start.4 = ((f32[16,1,128]{2,1,0:T(1,128)}), f32[16,1,128]{2,1,0:T(1,128)S(1)}, u32[]{:S(2)}, u32[]{:S(2)}) async-start(f32[16,1,128]{2,1,0:T(1,128)} %get-tuple-element.27), calls=%async_computation.4 | async-start | bytes 16384 | tf_op jit(solution)/shard_map/all_to_all | solution.py:442

commit v7 on v5

--- a/solution.py
+++ b/solution.py
@@ -85,19 +85,35 @@
     b = jnp.concatenate([b_high, b_low], axis=1)
     both = jnp.concatenate([train.astype(BF16), cand.astype(BF16)], axis=1)
     folded = jnp.concatenate([train[:32].astype(BF16), train[32:].astype(BF16)], axis=1)
-    for i in range(NQ):
+    for i in range(NZ):
         z_ref[i, 0:32, :] = folded
         z_ref[i, 32:48, :] = b
-        y_ref[i, 0:64, :] = both
-        y_ref[i, 64:80, :] = b
+    y_ref[0:64, :] = both
+    y_ref[64:80, :] = b
     side_ref[...] = jnp.concatenate(
         [target, jnp.broadcast_to(noise_ref[...], (RHS, S))], axis=1
     )
 
 
+def order(own_ref, far_ref, out_ref):
+    far = lax.axis_index("far")
+    for k, ref in enumerate([own_ref, far_ref]):
+        value = ref[...]
+        for i in range(8):
+            out_ref[i, (far + k) % 2] = value
+
+
+def shard(ref, q, rows, lanes=slice(None)):
+    y, x = q // 4, q % 4
+    return ref[(y % 2) * 4 + x, y // 2, rows, lanes]
+
+
 def row_side(y_ref, j, first):
     points = jnp.concatenate(
-        [y_ref[2 * j, 0:64, first : first + 64], y_ref[2 * j + 1, 0:64, first : first + 64]],
+        [
+            shard(y_ref, 2 * j, slice(0, 64), slice(first, first + 64)),
+            shard(y_ref, 2 * j + 1, slice(0, 64), slice(first, first + 64)),
+        ],
         axis=1,
     ).astype(F32)
     norm = jnp.sum(points * points, axis=0, keepdims=True)
@@ -173,7 +189,7 @@
 
 
 def position():
-    return lax.axis_index("y") * 4 + lax.axis_index("x")
+    return (lax.axis_index("far") * 2 + lax.axis_index("near")) * 4 + lax.axis_index("x")
 
 
 def first_apply(
@@ -210,7 +226,8 @@
         total = total + part_ref[i].astype(F32)
     w_ref[...] = total
     for j in range(NQ // 2):
-        even, odd = y_ref[2 * j, 64:80, :].astype(F32), y_ref[2 * j + 1, 64:80, :].astype(F32)
+        even = shard(y_ref, 2 * j, slice(64, 80)).astype(F32)
+        odd = shard(y_ref, 2 * j + 1, slice(64, 80)).astype(F32)
         br_ref[:, j * 128 : j * 128 + 128] = jnp.concatenate(
             [even[:, :64] + even[:, 64:], odd[:, :64] + odd[:, 64:]], axis=1
         )
@@ -361,7 +378,7 @@
         prepare,
         in_specs=[hbm] * 5,
         out_shape=(
-            shape(NQ, 80, 128, dtype=BF16),
+            shape(80, 128, dtype=BF16),
             shape(NZ, 48, 128, dtype=BF16),
             shape(RHS, 128),
         ),
@@ -381,7 +398,13 @@
         in_hbm(targets),
     )
     z_in = lax.all_gather(lax.all_to_all(z_out, "z", 0, 0), "c", axis=0)
-    y_in = lax.all_to_all(y_out, ("y", "x"), 0, 0)
+    far = lax.ppermute(y_out, "far", [(0, 1), (1, 0)])
+    y_half = call(
+        order,
+        out_shape=shape(8, 2, 80, 128, dtype=BF16),
+        cost_estimate=pl.CostEstimate(flops=0, bytes_accessed=400000, transcendentals=0),
+    )(y_out, far)
+    y_in = lax.all_to_all(y_half, ("near", "x"), 0, 0)
     col, b_col = call(
         col_side,
         out_shape=(shape(COLS, 128, dtype=BF16), shape(32, COLS, dtype=BF16)),
@@ -405,7 +428,7 @@
         ],
         cost_estimate=build_cost,
     )(y_in, col, b_col, side)
-    image_in = lax.all_to_all(image_out, ("y", "x"), 0, 0)
+    image_in = lax.all_to_all(image_out, ("far", "near", "x"), 0, 0)
     w_out, w_row, b_row = call(
         merge_image,
         out_shape=(shape(NZ, RHS, 128, dtype=BF16), shape(RHS, ROWS), shape(RHS, ROWS)),
@@ -428,13 +451,13 @@
         cost_estimate=build_cost,
     )(y_in, col, b_col, r_col)
     mean_out = call(pack, out_shape=shape(NQ, 24, 128))(scalar_in, mean_part)
-    mean_in = lax.all_to_all(mean_out, ("y", "x"), 0, 0)
+    mean_in = lax.all_to_all(mean_out, ("far", "near", "x"), 0, 0)
     return call(finish, out_shape=(shape(RHS, S), shape(RHS, S)))(mean_in, own, side)
 
 
 def solution(mesh):
-    fine = Mesh(mesh.devices.reshape(16, 2, 4, 4), ("z", "c", "y", "x"))
-    every = ("z", "c", "y", "x")
+    fine = Mesh(mesh.devices.reshape(16, 2, 2, 2, 4), ("z", "c", "far", "near", "x"))
+    every = ("z", "c", "far", "near", "x")
     wide = P(None, every)
     return jax.shard_map(
         per_device,

time: 122 us -> 121 us (level)
  blocking collectives: 87 us -> 59.9 us
  starting transfers between devices: 10.2 us -> 29.1 us
  waiting for transfers between devices: 4.91 us -> 11.2 us
    all_to_all x3 -> x2, blocking collectives: 53.1 us -> 25.7 us  [the longest x1 15.8 us: per_device(): image_in = lax.all_to_all(image_out, ('far', 'near', 'x'), 0, 0)]
    all_to_all x1 -> x2, starting transfers between devices: 6.76 us -> 20.8 us  [the longest x1 15.7 us: per_device(): z_in = lax.all_gather(lax.all_to_all(z_out, 'z', 0, 0), 'c', axis=0)]
    all_to_all x1 -> x2, waiting for transfers between devices: 0.58 us -> 5.69 us  [the longest x1 5.69 us: per_device(): z_in = lax.all_gather(lax.all_to_all(z_out, 'z', 0, 0), 'c', axis=0)]
    ppermute x0 -> x1, starting transfers between devices: none -> 4.82 us  [per_device(): far = lax.ppermute(y_out, 'far', [(0, 1), (1, 0)])]
    pallas_call x1 -> x2, Pallas kernels: 1.76 us -> 2.47 us  [the longest x1 1.7 us: per_device(): call(prepare, in_specs=[hbm] * 5, out_shape=(shape(80, 128, dtype=BF16),...]
  transfers between devices with their start and end apart: 2 -> 4, of which waited for: 2 -> 3; matrix products, arithmetic and copies ran while one was open for 0% -> 0% of each run, Pallas kernels for 6% -> 7%
where the time goes in v7:
time: 121 us; the launch traced here: 120 us
  blocking collectives  59.9 us (50%)
  starting transfers between devices  29.1 us (24%)
  Pallas kernels  19 us (16%)
  waiting for transfers between devices  11.2 us (9%)
    all_to_all x1, blocking collectives, per_device(): w_in = lax.all_gather(lax.all_to_all(w_out, 'z', 0, 0), 'c', axis=0)  19 us
    all_to_all x1, blocking collectives, per_device(): image_in = lax.all_to_all(image_out, ('far', 'near', 'x'), 0, 0)  15.8 us
    all_to_all x1, starting transfers between devices, per_device(): z_in = lax.all_gather(lax.all_to_all(z_out, 'z', 0, 0), 'c', axis=0)  15.7 us
    all_to_all x1, blocking collectives, per_device(): mean_in = lax.all_to_all(mean_out, ('far', 'near', 'x'), 0, 0)  9.9 us
    pallas_call x1, Pallas kernels, per_device(): call(cand_mean, out_shape=shape(NQ, RHS, 128), scratch_shapes=[*build, *[...  6.83 us
    all_gather x1, blocking collectives, per_device(): z_in = lax.all_gather(lax.all_to_all(z_out, 'z', 0, 0), 'c', axis=0)  6.82 us
    all_to_all x1, waiting for transfers between devices, per_device(): z_in = lax.all_gather(lax.all_to_all(z_out, 'z', 0, 0), 'c', axis=0)  5.69 us
    all_gather x1, blocking collectives, per_device(): w_in = lax.all_gather(lax.all_to_all(w_out, 'z', 0, 0), 'c', axis=0)  5.52 us
  transfers between devices with their start and end apart: 4, of which 3 were waited for; matrix products, arithmetic and copies ran while one was open for 0% of the time, Pallas kernels for 7%

profile of v7, /device:TPU:1, one launch (start us, length us, event | category | flops | bytes accessed | tf_op | source)
XLA Modules:
  0.0 119.9 jit_solution(3280438878373966872)
XLA Ops:
  0.6 1.7 %shard_map.68 = (bf16[80,128]{1,0:T(8,128)(2,1)S(1)}, bf16[16,48,128]{2,1,0:T(8,128)(2,1)}, f32[16,128]{1,0:T(8,128)S(1)}) custom-call(f32[64,64]{1,0:T(8,128)} %train_hbm.1, f32[64,64]{1,0:T(8,128)} %cand_hbm.1, f32[1,64]{1,0:T(1,128)} %bitcast.8, f32[1,64]{1,0:T(1,128)} %bitcast.9, f32[16,64]{1,0:T(8,128)} %target_hbm.1), custom_call_target="tpu_custom_call" | custom-call | tf_op jit(solution)/shard_map/pallas_call | solution.py:377
  2.3 15.7 %all-to-all-start.1 = ((bf16[16,48,128]{2,1,0:T(8,128)(2,1)}), bf16[16,48,128]{2,1,0:T(8,128)(2,1)S(1)}, u32[]{:S(2)}, u32[]{:S(2)}) async-start(bf16[16,48,128]{2,1,0:T(8,128)(2,1)} %get-tuple-element.17), calls=%async_computation.1 | async-start | bytes 393216 | tf_op jit(solution)/shard_map/all_to_all | solution.py:400
  18.1 4.8 %collective-permute-start = (bf16[80,128]{1,0:T(8,128)(2,1)S(1)}, bf16[80,128]{1,0:T(8,128)(2,1)S(1)}, u32[]{:S(2)}, u32[]{:S(2)}) collective-permute-start(bf16[80,128]{1,0:T(8,128)(2,1)S(1)} %get-tuple-element.16.own_ref), channel_id=1, source_target_pairs={{0,8},{8,0},{1,9},{9,1},{2,10},{10,2},{3,11},{11,3},{4,12},{12,4},... | collective-permute-start | bytes 61448 | tf_op jit(solution)/shard_map/ppermute | solution.py:401
  22.9 1.2 %collective-permute-done.far_ref = bf16[80,128]{1,0:T(8,128)(2,1)S(1)} collective-permute-done((bf16[80,128]{1,0:T(8,128)(2,1)S(1)}, bf16[80,128]{1,0:T(8,128)(2,1)S(1)}, u32[]{:S(2)}, u32[]{:S(2)}) %collective-permute-start) | collective-permute-done | bytes 20512 | tf_op jit(solution)/shard_map/ppermute | solution.py:401
  24.1 0.8 shard_map.69
  24.9 5.7 %all-to-all-done.1 = bf16[16,48,128]{2,1,0:T(8,128)(2,1)S(1)} async-done(((bf16[16,48,128]{2,1,0:T(8,128)(2,1)}), bf16[16,48,128]{2,1,0:T(8,128)(2,1)S(1)}, u32[]{:S(2)}, u32[]{:S(2)}) %all-to-all-start.1) | async-done | bytes 196640 | tf_op jit(solution)/shard_map/all_to_all | solution.py:400
  30.6 5.0 %all-to-all-start = ((bf16[8,2,80,128]{3,2,1,0:T(8,128)(2,1)}), bf16[8,2,80,128]{3,2,1,0:T(8,128)(2,1)S(1)}, u32[]{:S(2)}, u32[]{:S(2)}) async-start(bf16[8,2,80,128]{3,2,1,0:T(8,128)(2,1)} %shard_map.69), calls=%async_computation | async-start | bytes 655360 | tf_op jit(solution)/shard_map/all_to_all | solution.py:407
  35.6 6.8 %all-gather = bf16[32,48,128]{2,1,0:T(8,128)(2,1)S(1)} all-gather(bf16[16,48,128]{2,1,0:T(8,128)(2,1)S(1)} %all-to-all-done.1), channel_id=2, replica_groups=mesh['z'=16,'c'=2,'far'=2,'near'=2,'x'=4] {'c'}, dimensions={0}, use_global_device_ids=true | all-gather | bytes 589824 | tf_op jit(solution)/shard_map/all_gather | solution.py:400
  42.4 0.5 shard_map.70
  42.9 0.0 all-to-all-done.y_ref
  42.9 5.2 %shard_map.71 = (bf16[1536,1024]{1,0:T(8,128)(2,1)}, bf16[512,1024]{1,0:T(8,128)(2,1)S(1)}, bf16[16,16,1024]{2,1,0:T(8,128)(2,1)S(1)}) custom-call(bf16[8,2,80,128]{3,2,1,0:T(8,128)(2,1)S(1)} %all-to-all-done.y_ref, bf16[2048,128]{1,0:T(8,128)(2,1)S(1)} %get-tuple-element.18.col_ref, bf16[32,2048]{1,0:T(8,128)(2,1)S(1)} %get-tuple-element.19.b_ref, ...), custom_call_target="tpu_custom_call" | custom-call | flops 671088640 | bytes 4194304 | tf_op jit(solution)/shard_map/pallas_call | solution.py:415
  48.2 15.8 %all_to_all.30.part_ref = bf16[16,16,1024]{2,1,0:T(8,128)(2,1)S(1)} all-to-all(bf16[16,16,1024]{2,1,0:T(8,128)(2,1)S(1)} %get-tuple-element.21), channel_id=1, replica_groups=mesh['z'=16,'c'=2,'far'=2,'near'=2,'x'=4] {'far','near','x'}, dimensions={0} | all-to-all | bytes 1048576 | tf_op jit(solution)/shard_map/all_to_all | solution.py:431
  64.0 0.3 shard_map.72
  64.3 19.0 %all_to_all.31 = bf16[16,16,128]{2,1,0:T(8,128)(2,1)S(1)} all-to-all(bf16[16,16,128]{2,1,0:T(8,128)(2,1)S(1)} %get-tuple-element.22), channel_id=1, replica_groups=mesh['z'=16,'c'=2,'far'=2,'near'=2,'x'=4] {'z'}, dimensions={0} | all-to-all | bytes 131072 | tf_op jit(solution)/shard_map/all_to_all | solution.py:436
  83.3 5.5 %all-gather.1 = bf16[32,16,128]{2,1,0:T(8,128)(2,1)S(1)} all-gather(bf16[16,16,128]{2,1,0:T(8,128)(2,1)S(1)} %all_to_all.31), channel_id=3, replica_groups=mesh['z'=16,'c'=2,'far'=2,'near'=2,'x'=4] {'c'}, dimensions={0}, use_global_device_ids=true | all-gather | bytes 196608 | tf_op jit(solution)/shard_map/all_gather | solution.py:436
  88.8 2.8 %shard_map.73 = (f32[16,1,128]{2,1,0:T(1,128)}, bf16[32,2048]{1,0:T(8,128)(2,1)S(1)}, f32[16,128]{1,0:T(8,128)S(1)}) custom-call(bf16[2,16,16,128]{3,2,1,0:T(8,128)(2,1)S(1)} %bitcast.6, bf16[32,2048]{1,0:T(8,128)(2,1)S(1)} %get-tuple-element.19.b_ref, f32[16,1024]{1,0:T(8,128)S(1)} %get-tuple-element.23.w_ref, f32[16,1024]{1,0:T(8,128)S(1)} %get-tuple-element.24.br_ref, ...), custom_call_target="tpu_custom_call" | custom-call | tf_op jit(solution)/shard_map/pallas_call | solution.py:437
  91.6 3.5 %all-to-all-start.4 = ((f32[16,1,128]{2,1,0:T(1,128)}), f32[16,1,128]{2,1,0:T(1,128)S(1)}, u32[]{:S(2)}, u32[]{:S(2)}) async-start(f32[16,1,128]{2,1,0:T(1,128)} %get-tuple-element.27), calls=%async_computation.4 | async-start | bytes 16384 | tf_op jit(solution)/shard_map/all_to_all | solution.py:446
  95.1 6.8 %shard_map.74.mean_ref = f32[16,16,128]{2,1,0:T(8,128)S(1)} custom-call(bf16[8,2,80,128]{3,2,1,0:T(8,128)(2,1)S(1)} %all-to-all-done.y_ref, bf16[2048,128]{1,0:T(8,128)(2,1)S(1)} %get-tuple-element.18.col_ref, bf16[32,2048]{1,0:T(8,128)(2,1)S(1)} %get-tuple-element.19.b_ref, bf16[32,2048]{1,0:T(8,128)(2,1)S(1)} %get-tuple-element.28.r_ref), custom_call_target="tpu_custom_call" | custom-call | flops 671088640 | bytes 4194304 | tf_op jit(solution)/shard_map/pallas_call | solution.py:447
  101.9 4.3 %all-to-all-done.4 = f32[16,1,128]{2,1,0:T(1,128)S(1)} async-done(((f32[16,1,128]{2,1,0:T(1,128)}), f32[16,1,128]{2,1,0:T(1,128)S(1)}, u32[]{:S(2)}, u32[]{:S(2)}) %all-to-all-start.4) | async-done | bytes 8224 | tf_op jit(solution)/shard_map/all_to_all | solution.py:446
  106.2 2.9 %all-gather.2 = f32[32,1,128]{2,1,0:T(1,128)S(1)} all-gather(f32[16,1,128]{2,1,0:T(1,128)S(1)} %all-to-all-done.4), channel_id=4, replica_groups=mesh['z'=16,'c'=2,'far'=2,'near'=2,'x'=4] {'c'}, dimensions={0}, use_global_device_ids=true | all-gather | bytes 24576 | tf_op jit(solution)/shard_map/all_gather | solution.py:446
  109.2 9.9 %all_to_all.32.part_ref = f32[16,24,128]{2,1,0:T(8,128)S(1)} all-to-all(f32[16,24,128]{2,1,0:T(8,128)S(1)} %shard_map.75), channel_id=1, replica_groups=mesh['z'=16,'c'=2,'far'=2,'near'=2,'x'=4] {'far','near','x'}, dimensions={0} | all-to-all | bytes 393216 | tf_op jit(solution)/shard_map/all_to_all | solution.py:454
  119.1 0.9 shard_map.76
  (1 shorter events, 0.0 us)
Async XLA Ops:
  2.3 28.2 %all-to-all-start.1 = ((bf16[16,48,128]{2,1,0:T(8,128)(2,1)}), bf16[16,48,128]{2,1,0:T(8,128)(2,1)S(1)}, u32[]{:S(2)}, u32[]{:S(2)}) async-start(bf16[16,48,128]{2,1,0:T(8,128)(2,1)} %get-tuple-element.17), calls=%async_computation.1 | async-start | bytes 393216 | tf_op jit(solution)/shard_map/all_to_all | solution.py:400
  18.1 6.0 %collective-permute-start = (bf16[80,128]{1,0:T(8,128)(2,1)S(1)}, bf16[80,128]{1,0:T(8,128)(2,1)S(1)}, u32[]{:S(2)}, u32[]{:S(2)}) collective-permute-start(bf16[80,128]{1,0:T(8,128)(2,1)S(1)} %get-tuple-element.16.own_ref), channel_id=1, source_target_pairs={{0,8},{8,0},{1,9},{9,1},{2,10},{10,2},{3,11},{11,3},{4,12},{12,4},... | collective-permute-start | bytes 61448 | tf_op jit(solution)/shard_map/ppermute | solution.py:401
  30.6 12.3 %all-to-all-start = ((bf16[8,2,80,128]{3,2,1,0:T(8,128)(2,1)}), bf16[8,2,80,128]{3,2,1,0:T(8,128)(2,1)S(1)}, u32[]{:S(2)}, u32[]{:S(2)}) async-start(bf16[8,2,80,128]{3,2,1,0:T(8,128)(2,1)} %shard_map.69), calls=%async_computation | async-start | bytes 655360 | tf_op jit(solution)/shard_map/all_to_all | solution.py:407
  91.6 14.7 %all-to-all-start.4 = ((f32[16,1,128]{2,1,0:T(1,128)}), f32[16,1,128]{2,1,0:T(1,128)S(1)}, u32[]{:S(2)}, u32[]{:S(2)}) async-start(f32[16,1,128]{2,1,0:T(1,128)} %get-tuple-element.27), calls=%async_computation.4 | async-start | bytes 16384 | tf_op jit(solution)/shard_map/all_to_all | solution.py:446

commit v8 on v7

--- a/solution.py
+++ b/solution.py
@@ -22,7 +22,7 @@
 PIECE = COLS // CHUNKS
 KEPT = 1
 STORED = CHUNKS - KEPT
-READ = 256
+READ = 512
 READS = STORED * PIECE // READ
 PARAMS = pltpu.CompilerParams(vmem_limit_bytes=24 * 1024 * 1024)
 

time: 121 us -> 121 us (level)
  no operation moved by 1% of the time
where the time goes in v8:
time: 121 us; the launch traced here: 120 us
  blocking collectives  59.9 us (50%)
  starting transfers between devices  29.1 us (24%)
  Pallas kernels  19.2 us (16%)
  waiting for transfers between devices  11.2 us (9%)
    all_to_all x1, blocking collectives, per_device(): w_in = lax.all_gather(lax.all_to_all(w_out, 'z', 0, 0), 'c', axis=0)  19 us
    all_to_all x1, blocking collectives, per_device(): image_in = lax.all_to_all(image_out, ('far', 'near', 'x'), 0, 0)  15.8 us
    all_to_all x1, starting transfers between devices, per_device(): z_in = lax.all_gather(lax.all_to_all(z_out, 'z', 0, 0), 'c', axis=0)  15.7 us
    all_to_all x1, blocking collectives, per_device(): mean_in = lax.all_to_all(mean_out, ('far', 'near', 'x'), 0, 0)  9.9 us
    pallas_call x1, Pallas kernels, per_device(): call(cand_mean, out_shape=shape(NQ, RHS, 128), scratch_shapes=[*build, *[...  6.83 us
    all_gather x1, blocking collectives, per_device(): z_in = lax.all_gather(lax.all_to_all(z_out, 'z', 0, 0), 'c', axis=0)  6.82 us
    all_to_all x1, waiting for transfers between devices, per_device(): z_in = lax.all_gather(lax.all_to_all(z_out, 'z', 0, 0), 'c', axis=0)  5.69 us
    all_gather x1, blocking collectives, per_device(): w_in = lax.all_gather(lax.all_to_all(w_out, 'z', 0, 0), 'c', axis=0)  5.52 us
  transfers between devices with their start and end apart: 4, of which 3 were waited for; matrix products, arithmetic and copies ran while one was open for 0% of the time, Pallas kernels for 7%

profile of v8, /device:TPU:1, one launch (start us, length us, event | category | flops | bytes accessed | tf_op | source)
XLA Modules:
  0.0 120.1 jit_solution(8276483493500193807)
XLA Ops:
  0.6 1.7 %shard_map.68 = (bf16[80,128]{1,0:T(8,128)(2,1)S(1)}, bf16[16,48,128]{2,1,0:T(8,128)(2,1)}, f32[16,128]{1,0:T(8,128)S(1)}) custom-call(f32[64,64]{1,0:T(8,128)} %train_hbm.1, f32[64,64]{1,0:T(8,128)} %cand_hbm.1, f32[1,64]{1,0:T(1,128)} %bitcast.8, f32[1,64]{1,0:T(1,128)} %bitcast.9, f32[16,64]{1,0:T(8,128)} %target_hbm.1), custom_call_target="tpu_custom_call" | custom-call | tf_op jit(solution)/shard_map/pallas_call | solution.py:377
  2.3 15.7 %all-to-all-start.1 = ((bf16[16,48,128]{2,1,0:T(8,128)(2,1)}), bf16[16,48,128]{2,1,0:T(8,128)(2,1)S(1)}, u32[]{:S(2)}, u32[]{:S(2)}) async-start(bf16[16,48,128]{2,1,0:T(8,128)(2,1)} %get-tuple-element.17), calls=%async_computation.1 | async-start | bytes 393216 | tf_op jit(solution)/shard_map/all_to_all | solution.py:400
  18.1 4.8 %collective-permute-start = (bf16[80,128]{1,0:T(8,128)(2,1)S(1)}, bf16[80,128]{1,0:T(8,128)(2,1)S(1)}, u32[]{:S(2)}, u32[]{:S(2)}) collective-permute-start(bf16[80,128]{1,0:T(8,128)(2,1)S(1)} %get-tuple-element.16.own_ref), channel_id=1, source_target_pairs={{0,8},{8,0},{1,9},{9,1},{2,10},{10,2},{3,11},{11,3},{4,12},{12,4},... | collective-permute-start | bytes 61448 | tf_op jit(solution)/shard_map/ppermute | solution.py:401
  22.9 1.2 collective-permute-done.far_ref
  24.1 0.8 shard_map.69
  24.9 5.7 %all-to-all-done.1 = bf16[16,48,128]{2,1,0:T(8,128)(2,1)S(1)} async-done(((bf16[16,48,128]{2,1,0:T(8,128)(2,1)}), bf16[16,48,128]{2,1,0:T(8,128)(2,1)S(1)}, u32[]{:S(2)}, u32[]{:S(2)}) %all-to-all-start.1) | async-done | bytes 196640 | tf_op jit(solution)/shard_map/all_to_all | solution.py:400
  30.6 5.0 %all-to-all-start = ((bf16[8,2,80,128]{3,2,1,0:T(8,128)(2,1)}), bf16[8,2,80,128]{3,2,1,0:T(8,128)(2,1)S(1)}, u32[]{:S(2)}, u32[]{:S(2)}) async-start(bf16[8,2,80,128]{3,2,1,0:T(8,128)(2,1)} %shard_map.69), calls=%async_computation | async-start | bytes 655360 | tf_op jit(solution)/shard_map/all_to_all | solution.py:407
  35.6 6.8 %all-gather = bf16[32,48,128]{2,1,0:T(8,128)(2,1)S(1)} all-gather(bf16[16,48,128]{2,1,0:T(8,128)(2,1)S(1)} %all-to-all-done.1), channel_id=2, replica_groups=mesh['z'=16,'c'=2,'far'=2,'near'=2,'x'=4] {'c'}, dimensions={0}, use_global_device_ids=true | all-gather | bytes 589824 | tf_op jit(solution)/shard_map/all_gather | solution.py:400
  42.4 0.5 shard_map.70
  42.9 0.0 all-to-all-done.y_ref
  42.9 5.2 %shard_map.71 = (bf16[1536,1024]{1,0:T(8,128)(2,1)}, bf16[512,1024]{1,0:T(8,128)(2,1)S(1)}, bf16[16,16,1024]{2,1,0:T(8,128)(2,1)S(1)}) custom-call(bf16[8,2,80,128]{3,2,1,0:T(8,128)(2,1)S(1)} %all-to-all-done.y_ref, bf16[2048,128]{1,0:T(8,128)(2,1)S(1)} %get-tuple-element.18.col_ref, bf16[32,2048]{1,0:T(8,128)(2,1)S(1)} %get-tuple-element.19.b_ref, ...), custom_call_target="tpu_custom_call" | custom-call | flops 671088640 | bytes 4194304 | tf_op jit(solution)/shard_map/pallas_call | solution.py:415
  48.2 15.8 %all_to_all.30.part_ref = bf16[16,16,1024]{2,1,0:T(8,128)(2,1)S(1)} all-to-all(bf16[16,16,1024]{2,1,0:T(8,128)(2,1)S(1)} %get-tuple-element.21), channel_id=1, replica_groups=mesh['z'=16,'c'=2,'far'=2,'near'=2,'x'=4] {'far','near','x'}, dimensions={0} | all-to-all | bytes 1048576 | tf_op jit(solution)/shard_map/all_to_all | solution.py:431
  64.0 0.3 shard_map.72
  64.3 19.0 %all_to_all.31 = bf16[16,16,128]{2,1,0:T(8,128)(2,1)S(1)} all-to-all(bf16[16,16,128]{2,1,0:T(8,128)(2,1)S(1)} %get-tuple-element.22), channel_id=1, replica_groups=mesh['z'=16,'c'=2,'far'=2,'near'=2,'x'=4] {'z'}, dimensions={0} | all-to-all | bytes 131072 | tf_op jit(solution)/shard_map/all_to_all | solution.py:436
  83.3 5.5 %all-gather.1 = bf16[32,16,128]{2,1,0:T(8,128)(2,1)S(1)} all-gather(bf16[16,16,128]{2,1,0:T(8,128)(2,1)S(1)} %all_to_all.31), channel_id=3, replica_groups=mesh['z'=16,'c'=2,'far'=2,'near'=2,'x'=4] {'c'}, dimensions={0}, use_global_device_ids=true | all-gather | bytes 196608 | tf_op jit(solution)/shard_map/all_gather | solution.py:436
  88.8 2.9 %shard_map.73 = (f32[16,1,128]{2,1,0:T(1,128)}, bf16[32,2048]{1,0:T(8,128)(2,1)S(1)}, f32[16,128]{1,0:T(8,128)S(1)}) custom-call(bf16[2,16,16,128]{3,2,1,0:T(8,128)(2,1)S(1)} %bitcast.6, bf16[32,2048]{1,0:T(8,128)(2,1)S(1)} %get-tuple-element.19.b_ref, f32[16,1024]{1,0:T(8,128)S(1)} %get-tuple-element.23.w_ref, f32[16,1024]{1,0:T(8,128)S(1)} %get-tuple-element.24.br_ref, ...), custom_call_target="tpu_custom_call" | custom-call | tf_op jit(solution)/shard_map/pallas_call | solution.py:437
  91.7 3.5 %all-to-all-start.4 = ((f32[16,1,128]{2,1,0:T(1,128)}), f32[16,1,128]{2,1,0:T(1,128)S(1)}, u32[]{:S(2)}, u32[]{:S(2)}) async-start(f32[16,1,128]{2,1,0:T(1,128)} %get-tuple-element.27), calls=%async_computation.4 | async-start | bytes 16384 | tf_op jit(solution)/shard_map/all_to_all | solution.py:446
  95.2 6.8 %shard_map.74.mean_ref = f32[16,16,128]{2,1,0:T(8,128)S(1)} custom-call(bf16[8,2,80,128]{3,2,1,0:T(8,128)(2,1)S(1)} %all-to-all-done.y_ref, bf16[2048,128]{1,0:T(8,128)(2,1)S(1)} %get-tuple-element.18.col_ref, bf16[32,2048]{1,0:T(8,128)(2,1)S(1)} %get-tuple-element.19.b_ref, bf16[32,2048]{1,0:T(8,128)(2,1)S(1)} %get-tuple-element.28.r_ref), custom_call_target="tpu_custom_call" | custom-call | flops 671088640 | bytes 4194304 | tf_op jit(solution)/shard_map/pallas_call | solution.py:447
  102.0 4.3 %all-to-all-done.4 = f32[16,1,128]{2,1,0:T(1,128)S(1)} async-done(((f32[16,1,128]{2,1,0:T(1,128)}), f32[16,1,128]{2,1,0:T(1,128)S(1)}, u32[]{:S(2)}, u32[]{:S(2)}) %all-to-all-start.4) | async-done | bytes 8224 | tf_op jit(solution)/shard_map/all_to_all | solution.py:446
  106.4 2.9 %all-gather.2 = f32[32,1,128]{2,1,0:T(1,128)S(1)} all-gather(f32[16,1,128]{2,1,0:T(1,128)S(1)} %all-to-all-done.4), channel_id=4, replica_groups=mesh['z'=16,'c'=2,'far'=2,'near'=2,'x'=4] {'c'}, dimensions={0}, use_global_device_ids=true | all-gather | bytes 24576 | tf_op jit(solution)/shard_map/all_gather | solution.py:446
  109.3 9.9 %all_to_all.32.part_ref = f32[16,24,128]{2,1,0:T(8,128)S(1)} all-to-all(f32[16,24,128]{2,1,0:T(8,128)S(1)} %shard_map.75), channel_id=1, replica_groups=mesh['z'=16,'c'=2,'far'=2,'near'=2,'x'=4] {'far','near','x'}, dimensions={0} | all-to-all | bytes 393216 | tf_op jit(solution)/shard_map/all_to_all | solution.py:454
  119.2 0.9 shard_map.76
  (1 shorter events, 0.0 us)
Async XLA Ops:
  2.3 28.2 %all-to-all-start.1 = ((bf16[16,48,128]{2,1,0:T(8,128)(2,1)}), bf16[16,48,128]{2,1,0:T(8,128)(2,1)S(1)}, u32[]{:S(2)}, u32[]{:S(2)}) async-start(bf16[16,48,128]{2,1,0:T(8,128)(2,1)} %get-tuple-element.17), calls=%async_computation.1 | async-start | bytes 393216 | tf_op jit(solution)/shard_map/all_to_all | solution.py:400
  18.1 6.0 %collective-permute-start = (bf16[80,128]{1,0:T(8,128)(2,1)S(1)}, bf16[80,128]{1,0:T(8,128)(2,1)S(1)}, u32[]{:S(2)}, u32[]{:S(2)}) collective-permute-start(bf16[80,128]{1,0:T(8,128)(2,1)S(1)} %get-tuple-element.16.own_ref), channel_id=1, source_target_pairs={{0,8},{8,0},{1,9},{9,1},{2,10},{10,2},{3,11},{11,3},{4,12},{12,4},... | collective-permute-start | bytes 61448 | tf_op jit(solution)/shard_map/ppermute | solution.py:401
  30.6 12.3 %all-to-all-start = ((bf16[8,2,80,128]{3,2,1,0:T(8,128)(2,1)}), bf16[8,2,80,128]{3,2,1,0:T(8,128)(2,1)S(1)}, u32[]{:S(2)}, u32[]{:S(2)}) async-start(bf16[8,2,80,128]{3,2,1,0:T(8,128)(2,1)} %shard_map.69), calls=%async_computation | async-start | bytes 655360 | tf_op jit(solution)/shard_map/all_to_all | solution.py:407
  91.7 14.7 %all-to-all-start.4 = ((f32[16,1,128]{2,1,0:T(1,128)}), f32[16,1,128]{2,1,0:T(1,128)S(1)}, u32[]{:S(2)}, u32[]{:S(2)}) async-start(f32[16,1,128]{2,1,0:T(1,128)} %get-tuple-element.27), calls=%async_computation.4 | async-start | bytes 16384 | tf_op jit(solution)/shard_map/all_to_all | solution.py:446

commit v9 on v8

--- a/solution.py
+++ b/solution.py
@@ -72,22 +72,24 @@
     ]
     for copy in copies:
         copy.start()
-    for copy in copies:
+    for copy in copies[:3]:
         copy.wait()
     eye = lax.broadcasted_iota(jnp.int32, (D, D), 0) == lax.broadcasted_iota(
         jnp.int32, (D, D), 1
     )
     inv = jnp.sum(jnp.where(eye, inv_ref[...], 0.0), axis=1, keepdims=True)
     train = train_ref[...] * inv
-    cand = cand_ref[...] * inv
     target = target_ref[...]
     b_high, b_low = halves(target)
     b = jnp.concatenate([b_high, b_low], axis=1)
-    both = jnp.concatenate([train.astype(BF16), cand.astype(BF16)], axis=1)
     folded = jnp.concatenate([train[:32].astype(BF16), train[32:].astype(BF16)], axis=1)
     for i in range(NZ):
         z_ref[i, 0:32, :] = folded
         z_ref[i, 32:48, :] = b
+    for copy in copies[3:]:
+        copy.wait()
+    cand = cand_ref[...] * inv
+    both = jnp.concatenate([train.astype(BF16), cand.astype(BF16)], axis=1)
     y_ref[0:64, :] = both
     y_ref[64:80, :] = b
     side_ref[...] = jnp.concatenate(

time: 121 us -> 121 us (level)
  no operation moved by 1% of the time
where the time goes in v9:
time: 121 us; the launch traced here: 120 us
  blocking collectives  59.9 us (50%)
  starting transfers between devices  29.1 us (24%)
  Pallas kernels  19.1 us (16%)
  waiting for transfers between devices  11.2 us (9%)
    all_to_all x1, blocking collectives, per_device(): w_in = lax.all_gather(lax.all_to_all(w_out, 'z', 0, 0), 'c', axis=0)  19 us
    all_to_all x1, blocking collectives, per_device(): image_in = lax.all_to_all(image_out, ('far', 'near', 'x'), 0, 0)  15.8 us
    all_to_all x1, starting transfers between devices, per_device(): z_in = lax.all_gather(lax.all_to_all(z_out, 'z', 0, 0), 'c', axis=0)  15.7 us
    all_to_all x1, blocking collectives, per_device(): mean_in = lax.all_to_all(mean_out, ('far', 'near', 'x'), 0, 0)  9.89 us
    pallas_call x1, Pallas kernels, per_device(): call(cand_mean, out_shape=shape(NQ, RHS, 128), scratch_shapes=[*build, *[...  6.83 us
    all_gather x1, blocking collectives, per_device(): z_in = lax.all_gather(lax.all_to_all(z_out, 'z', 0, 0), 'c', axis=0)  6.82 us
    all_to_all x1, waiting for transfers between devices, per_device(): z_in = lax.all_gather(lax.all_to_all(z_out, 'z', 0, 0), 'c', axis=0)  5.69 us
    all_gather x1, blocking collectives, per_device(): w_in = lax.all_gather(lax.all_to_all(w_out, 'z', 0, 0), 'c', axis=0)  5.51 us
  transfers between devices with their start and end apart: 4, of which 3 were waited for; matrix products, arithmetic and copies ran while one was open for 0% of the time, Pallas kernels for 7%

profile of v9, /device:TPU:1, one launch (start us, length us, event | category | flops | bytes accessed | tf_op | source)
XLA Modules:
  0.0 120.0 jit_solution(5028018592407090881)
XLA Ops:
  0.6 1.7 %shard_map.68 = (bf16[80,128]{1,0:T(8,128)(2,1)S(1)}, bf16[16,48,128]{2,1,0:T(8,128)(2,1)}, f32[16,128]{1,0:T(8,128)S(1)}) custom-call(f32[64,64]{1,0:T(8,128)} %train_hbm.1, f32[64,64]{1,0:T(8,128)} %cand_hbm.1, f32[1,64]{1,0:T(1,128)} %bitcast.8, f32[1,64]{1,0:T(1,128)} %bitcast.9, f32[16,64]{1,0:T(8,128)} %target_hbm.1), custom_call_target="tpu_custom_call" | custom-call | tf_op jit(solution)/shard_map/pallas_call | solution.py:379
  2.3 15.7 %all-to-all-start.1 = ((bf16[16,48,128]{2,1,0:T(8,128)(2,1)}), bf16[16,48,128]{2,1,0:T(8,128)(2,1)S(1)}, u32[]{:S(2)}, u32[]{:S(2)}) async-start(bf16[16,48,128]{2,1,0:T(8,128)(2,1)} %get-tuple-element.17), calls=%async_computation.1 | async-start | bytes 393216 | tf_op jit(solution)/shard_map/all_to_all | solution.py:402
  18.0 4.8 %collective-permute-start = (bf16[80,128]{1,0:T(8,128)(2,1)S(1)}, bf16[80,128]{1,0:T(8,128)(2,1)S(1)}, u32[]{:S(2)}, u32[]{:S(2)}) collective-permute-start(bf16[80,128]{1,0:T(8,128)(2,1)S(1)} %get-tuple-element.16.own_ref), channel_id=1, source_target_pairs={{0,8},{8,0},{1,9},{9,1},{2,10},{10,2},{3,11},{11,3},{4,12},{12,4},... | collective-permute-start | bytes 61448 | tf_op jit(solution)/shard_map/ppermute | solution.py:403
  22.9 1.2 %collective-permute-done.far_ref = bf16[80,128]{1,0:T(8,128)(2,1)S(1)} collective-permute-done((bf16[80,128]{1,0:T(8,128)(2,1)S(1)}, bf16[80,128]{1,0:T(8,128)(2,1)S(1)}, u32[]{:S(2)}, u32[]{:S(2)}) %collective-permute-start) | collective-permute-done | bytes 20512 | tf_op jit(solution)/shard_map/ppermute | solution.py:403
  24.1 0.8 shard_map.69
  24.8 5.7 %all-to-all-done.1 = bf16[16,48,128]{2,1,0:T(8,128)(2,1)S(1)} async-done(((bf16[16,48,128]{2,1,0:T(8,128)(2,1)}), bf16[16,48,128]{2,1,0:T(8,128)(2,1)S(1)}, u32[]{:S(2)}, u32[]{:S(2)}) %all-to-all-start.1) | async-done | bytes 196640 | tf_op jit(solution)/shard_map/all_to_all | solution.py:402
  30.5 5.0 %all-to-all-start = ((bf16[8,2,80,128]{3,2,1,0:T(8,128)(2,1)}), bf16[8,2,80,128]{3,2,1,0:T(8,128)(2,1)S(1)}, u32[]{:S(2)}, u32[]{:S(2)}) async-start(bf16[8,2,80,128]{3,2,1,0:T(8,128)(2,1)} %shard_map.69), calls=%async_computation | async-start | bytes 655360 | tf_op jit(solution)/shard_map/all_to_all | solution.py:409
  35.6 6.8 %all-gather = bf16[32,48,128]{2,1,0:T(8,128)(2,1)S(1)} all-gather(bf16[16,48,128]{2,1,0:T(8,128)(2,1)S(1)} %all-to-all-done.1), channel_id=2, replica_groups=mesh['z'=16,'c'=2,'far'=2,'near'=2,'x'=4] {'c'}, dimensions={0}, use_global_device_ids=true | all-gather | bytes 589824 | tf_op jit(solution)/shard_map/all_gather | solution.py:402
  42.4 0.5 shard_map.70
  42.9 0.0 all-to-all-done.y_ref
  42.9 5.2 %shard_map.71 = (bf16[1536,1024]{1,0:T(8,128)(2,1)}, bf16[512,1024]{1,0:T(8,128)(2,1)S(1)}, bf16[16,16,1024]{2,1,0:T(8,128)(2,1)S(1)}) custom-call(bf16[8,2,80,128]{3,2,1,0:T(8,128)(2,1)S(1)} %all-to-all-done.y_ref, bf16[2048,128]{1,0:T(8,128)(2,1)S(1)} %get-tuple-element.18.col_ref, bf16[32,2048]{1,0:T(8,128)(2,1)S(1)} %get-tuple-element.19.b_ref, ...), custom_call_target="tpu_custom_call" | custom-call | flops 671088640 | bytes 4194304 | tf_op jit(solution)/shard_map/pallas_call | solution.py:417
  48.1 15.8 %all_to_all.30.part_ref = bf16[16,16,1024]{2,1,0:T(8,128)(2,1)S(1)} all-to-all(bf16[16,16,1024]{2,1,0:T(8,128)(2,1)S(1)} %get-tuple-element.21), channel_id=1, replica_groups=mesh['z'=16,'c'=2,'far'=2,'near'=2,'x'=4] {'far','near','x'}, dimensions={0} | all-to-all | bytes 1048576 | tf_op jit(solution)/shard_map/all_to_all | solution.py:433
  63.9 0.3 shard_map.72
  64.2 19.0 %all_to_all.31 = bf16[16,16,128]{2,1,0:T(8,128)(2,1)S(1)} all-to-all(bf16[16,16,128]{2,1,0:T(8,128)(2,1)S(1)} %get-tuple-element.22), channel_id=1, replica_groups=mesh['z'=16,'c'=2,'far'=2,'near'=2,'x'=4] {'z'}, dimensions={0} | all-to-all | bytes 131072 | tf_op jit(solution)/shard_map/all_to_all | solution.py:438
  83.2 5.5 %all-gather.1 = bf16[32,16,128]{2,1,0:T(8,128)(2,1)S(1)} all-gather(bf16[16,16,128]{2,1,0:T(8,128)(2,1)S(1)} %all_to_all.31), channel_id=3, replica_groups=mesh['z'=16,'c'=2,'far'=2,'near'=2,'x'=4] {'c'}, dimensions={0}, use_global_device_ids=true | all-gather | bytes 196608 | tf_op jit(solution)/shard_map/all_gather | solution.py:438
  88.7 2.9 %shard_map.73 = (f32[16,1,128]{2,1,0:T(1,128)}, bf16[32,2048]{1,0:T(8,128)(2,1)S(1)}, f32[16,128]{1,0:T(8,128)S(1)}) custom-call(bf16[2,16,16,128]{3,2,1,0:T(8,128)(2,1)S(1)} %bitcast.6, bf16[32,2048]{1,0:T(8,128)(2,1)S(1)} %get-tuple-element.19.b_ref, f32[16,1024]{1,0:T(8,128)S(1)} %get-tuple-element.23.w_ref, f32[16,1024]{1,0:T(8,128)S(1)} %get-tuple-element.24.br_ref, ...), custom_call_target="tpu_custom_call" | custom-call | tf_op jit(solution)/shard_map/pallas_call | solution.py:439
  91.7 3.5 %all-to-all-start.4 = ((f32[16,1,128]{2,1,0:T(1,128)}), f32[16,1,128]{2,1,0:T(1,128)S(1)}, u32[]{:S(2)}, u32[]{:S(2)}) async-start(f32[16,1,128]{2,1,0:T(1,128)} %get-tuple-element.27), calls=%async_computation.4 | async-start | bytes 16384 | tf_op jit(solution)/shard_map/all_to_all | solution.py:448
  95.2 6.8 %shard_map.74.mean_ref = f32[16,16,128]{2,1,0:T(8,128)S(1)} custom-call(bf16[8,2,80,128]{3,2,1,0:T(8,128)(2,1)S(1)} %all-to-all-done.y_ref, bf16[2048,128]{1,0:T(8,128)(2,1)S(1)} %get-tuple-element.18.col_ref, bf16[32,2048]{1,0:T(8,128)(2,1)S(1)} %get-tuple-element.19.b_ref, bf16[32,2048]{1,0:T(8,128)(2,1)S(1)} %get-tuple-element.28.r_ref), custom_call_target="tpu_custom_call" | custom-call | flops 671088640 | bytes 4194304 | tf_op jit(solution)/shard_map/pallas_call | solution.py:449
  102.0 4.3 %all-to-all-done.4 = f32[16,1,128]{2,1,0:T(1,128)S(1)} async-done(((f32[16,1,128]{2,1,0:T(1,128)}), f32[16,1,128]{2,1,0:T(1,128)S(1)}, u32[]{:S(2)}, u32[]{:S(2)}) %all-to-all-start.4) | async-done | bytes 8224 | tf_op jit(solution)/shard_map/all_to_all | solution.py:448
  106.3 2.9 %all-gather.2 = f32[32,1,128]{2,1,0:T(1,128)S(1)} all-gather(f32[16,1,128]{2,1,0:T(1,128)S(1)} %all-to-all-done.4), channel_id=4, replica_groups=mesh['z'=16,'c'=2,'far'=2,'near'=2,'x'=4] {'c'}, dimensions={0}, use_global_device_ids=true | all-gather | bytes 24576 | tf_op jit(solution)/shard_map/all_gather | solution.py:448
  109.3 9.9 %all_to_all.32.part_ref = f32[16,24,128]{2,1,0:T(8,128)S(1)} all-to-all(f32[16,24,128]{2,1,0:T(8,128)S(1)} %shard_map.75), channel_id=1, replica_groups=mesh['z'=16,'c'=2,'far'=2,'near'=2,'x'=4] {'far','near','x'}, dimensions={0} | all-to-all | bytes 393216 | tf_op jit(solution)/shard_map/all_to_all | solution.py:456
  119.2 0.9 shard_map.76
  (1 shorter events, 0.0 us)
Async XLA Ops:
  2.3 28.2 %all-to-all-start.1 = ((bf16[16,48,128]{2,1,0:T(8,128)(2,1)}), bf16[16,48,128]{2,1,0:T(8,128)(2,1)S(1)}, u32[]{:S(2)}, u32[]{:S(2)}) async-start(bf16[16,48,128]{2,1,0:T(8,128)(2,1)} %get-tuple-element.17), calls=%async_computation.1 | async-start | bytes 393216 | tf_op jit(solution)/shard_map/all_to_all | solution.py:402
  18.0 6.0 %collective-permute-start = (bf16[80,128]{1,0:T(8,128)(2,1)S(1)}, bf16[80,128]{1,0:T(8,128)(2,1)S(1)}, u32[]{:S(2)}, u32[]{:S(2)}) collective-permute-start(bf16[80,128]{1,0:T(8,128)(2,1)S(1)} %get-tuple-element.16.own_ref), channel_id=1, source_target_pairs={{0,8},{8,0},{1,9},{9,1},{2,10},{10,2},{3,11},{11,3},{4,12},{12,4},... | collective-permute-start | bytes 61448 | tf_op jit(solution)/shard_map/ppermute | solution.py:403
  30.5 12.3 %all-to-all-start = ((bf16[8,2,80,128]{3,2,1,0:T(8,128)(2,1)}), bf16[8,2,80,128]{3,2,1,0:T(8,128)(2,1)S(1)}, u32[]{:S(2)}, u32[]{:S(2)}) async-start(bf16[8,2,80,128]{3,2,1,0:T(8,128)(2,1)} %shard_map.69), calls=%async_computation | async-start | bytes 655360 | tf_op jit(solution)/shard_map/all_to_all | solution.py:409
  91.7 14.7 %all-to-all-start.4 = ((f32[16,1,128]{2,1,0:T(1,128)}), f32[16,1,128]{2,1,0:T(1,128)S(1)}, u32[]{:S(2)}, u32[]{:S(2)}) async-start(f32[16,1,128]{2,1,0:T(1,128)} %get-tuple-element.27), calls=%async_computation.4 | async-start | bytes 16384 | tf_op jit(solution)/shard_map/all_to_all | solution.py:448
